TPU v7x, 32 devices: a whole 2x2x4 slice. The times are simulated.
32 devices in a mesh: seq: 8 (over z, x), head: 2 (over y), dp: 2 (over core).
Axes of the slice: x: 2, y: 2, z: 4, core: 2. Of those that a mesh axis runs over, the one named last changes fastest.
Arguments:
- queries: bfloat16 [2, 2048, 1024], P('dp', 'seq', 'head'), may hold values from -6 to 6
- key_rows: bfloat16 [2, 2048, 1024], P('dp', 'seq', 'head'), may hold values from -6 to 6
- value_rows: bfloat16 [2, 2048, 1024], P('dp', 'seq', 'head'), may hold values from -140 to 140
- stretch_doc: int32 [2, 8], P('dp', 'seq'), may hold values from 0 to 3, never falling along the last dimension, each value on 1 to 4 neighbouring positions
- head_gain: float32 [8, 128], P('head'), may hold values from 0.1 to 1.9
- w_out: bfloat16 [1024, 2048], P('head'), may hold values from -0.1875 to 0.1875
- cotangent: bfloat16 [2, 2048, 2048], P('dp', 'seq'), may hold values from -40 to 40
Outputs:
- layer_out: bfloat16 [2, 2048, 2048], P('dp', ('seq', 'head'))
- query_grad: bfloat16 [2, 2048, 1024], P('dp', 'seq', 'head')
- key_grad: bfloat16 [2, 2048, 1024], P('dp', 'seq', 'head')
- value_grad: bfloat16 [2, 2048, 1024], P('dp', 'seq', 'head')
- gain_grad: float32 [8, 128], P('head')
Inputs may be any that keep to these rules, and one draw needn't show every extreme that they name: `stretch_doc`: document numbers never fall along a sequence; each document spans 1 to 4 whole stretches, and one spans exactly that many.
All inputs are finite; a program needn't handle non-finite values.
Results may differ from a plain program's by a relative error of at most 0.0055.
Values may be sent and summed in bfloat16 or wider, within the bound.
No kernel may reach another device: no remote copies, remote signals or barrier semaphores. Data moves between devices by JAX's collectives and lax.ppermute only.
A program may use at most 64 MiB of HBM per device.

v0:
```python
import math

import jax
import jax.numpy as jnp
from jax import lax
from jax.sharding import PartitionSpec as P

epsilon = 1e-05
highest = lax.Precision.HIGHEST


def shifted(block, axis, distance):
    devices = range(lax.axis_size(axis))
    route = [(i - distance, i) for i in devices if i - distance in devices]
    return lax.ppermute(block, axis, route)


def link_docs(earlier, following):
    sum_early, doc_early = earlier
    sum_late, doc_late = following
    merged = jnp.where(doc_early[0] == doc_late[0], sum_late + sum_early, sum_late)
    running = jnp.where(doc_late[0] < 0.5, sum_early, merged)
    return (running, jnp.where(doc_late < 0.5, doc_early, doc_late))


def double_chain(start, mover, seq_size):
    current = mover(start, 1)
    reach = 1
    while reach < seq_size - 1:
        current = link_docs(mover(current, reach), current)
        reach = reach * 2
    return current


def on_device(queries, key_rows, value_rows, stretch_doc, head_gain, w_out, cotangent):
    token_count = queries.shape[1]
    local_width = queries.shape[2]
    head_count = head_gain.shape[0]
    head_dim = head_gain.shape[1]
    stretches = stretch_doc.shape[1]
    stretch_len = token_count // stretches
    seq_size = lax.axis_size("seq")
    blocks = (stretches, stretch_len, head_count, head_dim)
    query_blk = queries[0].reshape(blocks)
    key_blk = key_rows[0].reshape(blocks)
    value_blk = value_rows[0].reshape(blocks)
    doc_ids = stretch_doc[0]
    doc_float = doc_ids.astype(jnp.float32) + 1.0
    stretch_order = jnp.arange(stretches)
    same_doc = doc_ids[:, None] == doc_ids[None, :]
    before_mask = jnp.where(
        same_doc & (stretch_order[None, :] < stretch_order[:, None]), 1.0, 0.0
    ).astype(jnp.float32)
    after_mask = jnp.where(
        same_doc & (stretch_order[None, :] > stretch_order[:, None]), 1.0, 0.0
    ).astype(jnp.float32)
    positions = jnp.arange(stretch_len)
    causal = positions[:, None] >= positions[None, :]

    def move_forward(pair, distance):
        return shifted((pair[0], pair[1]), "seq", distance)

    def move_backward(pair, distance):
        return shifted((pair[0], pair[1]), "seq", -distance)

    kv_sum = jnp.einsum("cshd,cshe->chde", key_blk, value_blk, preferred_element_type=jnp.float32)
    last_pick = jnp.where(doc_float == doc_float[0], 1.0, 0.0).astype(jnp.float32)
    own_state = jnp.einsum("c,chde->hde", last_pick, kv_sum, precision=highest)
    incoming, incoming_doc = double_chain((own_state, doc_float), move_forward, seq_size)
    take_in = jnp.where(doc_float == incoming_doc[0], 1.0, 0.0).astype(jnp.float32)
    states = (
        jnp.einsum("cj,jhde->chde", before_mask, kv_sum, precision=highest)
        + take_in[:, None, None, None] * incoming
    )
    scores = jnp.einsum("cthd,cshd->chts", query_blk, key_blk, preferred_element_type=jnp.float32)
    attn_weights = jnp.where(causal, scores, 0.0).astype(jnp.bfloat16)
    within = jnp.einsum(
        "chts,cshe->cthe", attn_weights, value_blk, preferred_element_type=jnp.float32
    )
    query_f = query_blk.astype(jnp.float32)
    carried = jnp.einsum("cthd,chde->cthe", query_f, states, precision=highest)
    attended = within + carried
    inv_rms = lax.rsqrt(jnp.mean(attended * attended, axis=-1, keepdims=True) + epsilon)
    unit_rows = attended * inv_rms
    normed_rows = (unit_rows * head_gain).astype(jnp.bfloat16).reshape(token_count, local_width)
    exchanged = lax.all_to_all(normed_rows, "head", split_axis=0, concat_axis=1, tiled=True)
    summed = jnp.dot(
        exchanged,
        lax.all_gather(w_out, "head", axis=0, tiled=True),
        preferred_element_type=jnp.float32,
    )
    layer_out = summed.astype(jnp.bfloat16)[None]
    grad_normed = jnp.einsum(
        "tm,fm->tf", cotangent[0], w_out, preferred_element_type=jnp.float32
    ).reshape(blocks)
    gain_part = jnp.sum(grad_normed * unit_rows, axis=(0, 1))
    total_tokens = seq_size * lax.axis_size("dp") * token_count
    gain_grad = lax.psum(gain_part, ("seq", "dp")) / math.sqrt(total_tokens)
    scaled = grad_normed * head_gain
    grad_attended = inv_rms * (
        scaled - unit_rows * jnp.mean(scaled * unit_rows, axis=-1, keepdims=True)
    )
    grad_bf = grad_attended.astype(jnp.bfloat16)
    query_term = jnp.einsum(
        "cthd,cthe->chde", query_blk, grad_bf, preferred_element_type=jnp.float32
    )
    first_pick = jnp.where(doc_float == doc_float[0], 1.0, 0.0).astype(jnp.float32)
    own_grad = jnp.einsum("c,chde->hde", first_pick, query_term, precision=highest)
    incoming_grad, grad_doc = double_chain((own_grad, doc_float), move_backward, seq_size)
    take_back = jnp.where(doc_float == grad_doc[0], 1.0, 0.0).astype(jnp.float32)
    grad_states = (
        jnp.einsum("cj,jhde->chde", after_mask, query_term, precision=highest)
        + take_back[:, None, None, None] * incoming_grad
    )
    grad_scores = jnp.einsum(
        "cthe,cshe->chts", grad_bf, value_blk, preferred_element_type=jnp.float32
    )
    grad_weights = jnp.where(causal, grad_scores, 0.0).astype(jnp.bfloat16)
    grad_f = grad_bf.astype(jnp.float32)
    query_grad = jnp.einsum(
        "chts,cshd->cthd", grad_weights, key_blk, preferred_element_type=jnp.float32
    ) + jnp.einsum("cthe,chde->cthd", grad_f, states, precision=highest)
    key_grad = jnp.einsum(
        "chts,cthd->cshd", grad_weights, query_blk, preferred_element_type=jnp.float32
    ) + jnp.einsum("cshe,chde->cshd", value_blk.astype(jnp.float32), grad_states, precision=highest)
    value_grad = jnp.einsum(
        "chts,cthe->cshe", attn_weights, grad_bf, preferred_element_type=jnp.float32
    ) + jnp.einsum("cshd,chde->cshe", key_blk.astype(jnp.float32), grad_states, precision=highest)
    out_shape = (1, token_count, local_width)
    return (
        layer_out,
        query_grad.astype(jnp.bfloat16).reshape(out_shape),
        key_grad.astype(jnp.bfloat16).reshape(out_shape),
        value_grad.astype(jnp.bfloat16).reshape(out_shape),
        gain_grad,
    )


def solution(mesh):
    return jax.shard_map(
        on_device,
        mesh=mesh,
        in_specs=(
            P("dp", "seq", "head"),
            P("dp", "seq", "head"),
            P("dp", "seq", "head"),
            P("dp", "seq"),
            P("head", None),
            P("head", None),
            P("dp", "seq", None),
        ),
        out_specs=(
            P("dp", ("seq", "head"), None),
            P("dp", "seq", "head"),
            P("dp", "seq", "head"),
            P("dp", "seq", "head"),
            P("head", None),
        ),
        check_vma=False,
    )
```

profile of v0, /device:TPU:0, one launch (start us, length us, event | category | flops | bytes accessed | tf_op | source)
XLA Modules:
  0.0 170.5 jit_solution(11719621536188737796)
XLA Ops:
  10.5 4.9 %collective-permute-start.4 = (f32[4,128,128]{2,1,0:T(8,128)S(1)}, f32[4,128,128]{2,1,0:T(8,128)S(1)}, u32[]{:S(2)}, u32[]{:S(2)}) collective-permute-start(f32[4,128,128]{2,1,0:T(8,128)S(1)} %get-tuple-element.19), channel_id=1, source_target_pairs={{0,4},{4,8},{8,12},{12,16},{16,20},{20,24},{24,28},{1,5},{5,9},{9,... | collective-permute-start | bytes 786440 | tf_op jit(solution)/shard_map/ppermute | solution.py:15
  15.3 5.5 %collective-permute-done.4 = f32[4,128,128]{2,1,0:T(8,128)S(1)} collective-permute-done((f32[4,128,128]{2,1,0:T(8,128)S(1)}, f32[4,128,128]{2,1,0:T(8,128)S(1)}, u32[]{:S(2)}, u32[]{:S(2)}) %collective-permute-start.4) | collective-permute-done | bytes 262176 | tf_op jit(solution)/shard_map/ppermute | solution.py:15
  20.9 4.4 %collective-permute-start.5 = (f32[4,128,128]{2,1,0:T(8,128)S(1)}, f32[4,128,128]{2,1,0:T(8,128)S(1)}, u32[]{:S(2)}, u32[]{:S(2)}) collective-permute-start(f32[4,128,128]{2,1,0:T(8,128)S(1)} %collective-permute-done.4), channel_id=1, source_target_pairs={{0,4},{4,8},{8,12},{12,16},{16,20},{20,24},{24,28},{1,5},{5,9},{9,... | collective-permute-start | bytes 786440 | tf_op jit(solution)/shard_map/ppermute | solution.py:15
  25.2 5.6 %collective-permute-start = (f32[1]{0:T(128)}, f32[1]{0:T(128)}, u32[]{:S(2)}, u32[]{:S(2)}) collective-permute-start(f32[1]{0:T(128)} %bitcast.1), channel_id=1, source_target_pairs={{0,4},{4,8},{8,12},{12,16},{16,20},{20,24},{24,28},{1,5},{5,9},{9,... | collective-permute-start | bytes 20 | tf_op jit(solution)/shard_map/ppermute | solution.py:15
  31.0 4.5 %collective-permute-start.1 = (f32[1]{0:T(128)}, f32[1]{0:T(128)}, u32[]{:S(2)}, u32[]{:S(2)}) collective-permute-start(f32[1]{0:T(128)} %collective-permute-done), channel_id=1, source_target_pairs={{0,4},{4,8},{8,12},{12,16},{16,20},{20,24},{24,28},{1,5},{5,9},{9,... | collective-permute-start | bytes 20 | tf_op jit(solution)/shard_map/ppermute | solution.py:15
  37.6 6.4 %collective-permute-start.6 = (f32[4,128,128]{2,1,0:T(8,128)S(1)}, f32[4,128,128]{2,1,0:T(8,128)S(1)}, u32[]{:S(2)}, u32[]{:S(2)}) collective-permute-start(f32[4,128,128]{2,1,0:T(8,128)S(1)} %fusion.14), channel_id=1, source_target_pairs={{0,8},{4,12},{8,16},{12,20},{16,24},{20,28},{1,9},{5,13},{9,17},{1... | collective-permute-start | bytes 786440 | tf_op jit(solution)/shard_map/ppermute | solution.py:15
  44.0 2.3 %fusion.7 = f32[256,512]{0,1:T(8,128)S(1)} fusion(bf16[512,2048]{1,0:T(8,128)(2,1)} %param.12, bf16[1,256,2048]{2,1,0:T(8,128)(2,1)S(1)} %copy-done), kind=kOutput, calls=%fused_computation.17 | convolution fusion | flops 536870912 | bytes 3670016 | tf_op jit(solution)/shard_map/tm,fm->tf/dot_general | solution.py:93
  47.6 4.9 %collective-permute-start.2 = (f32[1]{0:T(128)}, f32[1]{0:T(128)}, u32[]{:S(2)}, u32[]{:S(2)}) collective-permute-start(f32[1]{0:T(128)} %select_n.117), channel_id=1, source_target_pairs={{0,8},{4,12},{8,16},{12,20},{16,24},{20,28},{1,9},{5,13},{9,17},{1... | collective-permute-start | bytes 20 | tf_op jit(solution)/shard_map/ppermute | solution.py:15
  53.3 5.0 %collective-permute-start.7 = (f32[4,128,128]{2,1,0:T(8,128)S(1)}, f32[4,128,128]{2,1,0:T(8,128)S(1)}, u32[]{:S(2)}, u32[]{:S(2)}) collective-permute-start(f32[4,128,128]{2,1,0:T(8,128)S(1)} %fusion.13), channel_id=1, source_target_pairs={{0,16},{4,20},{8,24},{12,28},{1,17},{5,21},{9,25},{13,29},{2,18},{... | collective-permute-start | bytes 786440 | tf_op jit(solution)/shard_map/ppermute | solution.py:15
  59.5 2.7 %collective-permute-start.3 = (f32[1]{0:T(128)}, f32[1]{0:T(128)}, u32[]{:S(2)}, u32[]{:S(2)}) collective-permute-start(f32[1]{0:T(128)} %select_n.118), channel_id=1, source_target_pairs={{0,16},{4,20},{8,24},{12,28},{1,17},{5,21},{9,25},{13,29},{2,18},{... | collective-permute-start | bytes 20 | tf_op jit(solution)/shard_map/ppermute | solution.py:15
  65.4 1.3 collective-permute-start.12
  66.7 1.3 collective-permute-start.8
  68.0 5.8 %collective-permute-done.8 = f32[1]{0:T(128)} collective-permute-done((f32[1]{0:T(128)}, f32[1]{0:T(128)}, u32[]{:S(2)}, u32[]{:S(2)}) %collective-permute-start.8) | collective-permute-done | bytes 36 | tf_op jit(solution)/shard_map/ppermute | solution.py:15
  75.7 5.2 %collective-permute-done.9 = f32[1]{0:T(128)} collective-permute-done((f32[1]{0:T(128)}, f32[1]{0:T(128)}, u32[]{:S(2)}, u32[]{:S(2)}) %collective-permute-start.9) | collective-permute-done | bytes 36 | tf_op jit(solution)/shard_map/ppermute | solution.py:15
  82.1 1.3 collective-permute-start.10
  84.6 3.2 %collective-permute-done.10 = f32[1]{0:T(128)} collective-permute-done((f32[1]{0:T(128)}, f32[1]{0:T(128)}, u32[]{:S(2)}, u32[]{:S(2)}) %collective-permute-start.10) | collective-permute-done | bytes 36 | tf_op jit(solution)/shard_map/ppermute | solution.py:15
  88.5 1.3 collective-permute-start.11
  90.5 4.4 %collective-permute-done.11 = f32[1]{0:T(128)} collective-permute-done((f32[1]{0:T(128)}, f32[1]{0:T(128)}, u32[]{:S(2)}, u32[]{:S(2)}) %collective-permute-start.11) | collective-permute-done | bytes 36 | tf_op jit(solution)/shard_map/ppermute | solution.py:15
  98.2 7.1 %collective-permute-done.13 = f32[4,128,128]{1,2,0:T(8,128)S(1)} collective-permute-done((f32[4,128,128]{1,2,0:T(8,128)S(1)}, f32[4,128,128]{1,2,0:T(8,128)S(1)}, u32[]{:S(2)}, u32[]{:S(2)}) %collective-permute-start.13) | collective-permute-done | bytes 262176 | tf_op jit(solution)/shard_map/ppermute | solution.py:15
  109.6 3.4 %all-to-all-start = ((bf16[2,128,512]{1,2,0:T(8,128)(2,1)}), bf16[2,128,512]{1,2,0:T(8,128)(2,1)S(1)}, u32[]{:S(2)}, u32[]{:S(2)}) async-start(bf16[2,128,512]{1,2,0:T(8,128)(2,1)} %copy.39), calls=%async_computation | async-start | bytes 524288 | tf_op jit(solution)/shard_map/all_to_all | solution.py:86
  113.1 31.5 %psum.7 = f32[4,128]{1,0:T(4,128)S(1)} all-reduce(f32[4,128]{1,0:T(4,128)S(1)} %get-tuple-element.15), channel_id=1, replica_groups=mesh['seq'=8,'head'=2,'dp'=2] {'seq','dp'}, use_global_device_ids=true, to_apply=%region_3.4 | all-reduce | flops 512 | bytes 4096 | tf_op jit(solution)/shard_map/psum | solution.py:98
  147.7 1.3 convolution_bitcast_fusion
  149.0 8.3 %collective-permute-done.15 = f32[4,128,128]{1,2,0:T(8,128)S(1)} collective-permute-done((f32[4,128,128]{1,2,0:T(8,128)S(1)}, f32[4,128,128]{1,2,0:T(8,128)S(1)}, u32[]{:S(2)}, u32[]{:S(2)}) %collective-permute-start.15) | collective-permute-done | bytes 262176 | tf_op jit(solution)/shard_map/ppermute | solution.py:15
  160.0 3.7 %fusion = bf16[1,128,2048]{2,1,0:T(8,128)(2,1)} fusion(bf16[128,1024]{0,1:T(8,128)(2,1)S(1)} %bitcast.79, bf16[1024,2048]{1,0:T(8,128)(2,1)} %all-gather.2.cloned.1.call-done), kind=kOutput, calls=%fused_computation.1 | convolution fusion | flops 537133056 | bytes 4980736 | tf_op jit(solution)/shard_map/dot_general | solution.py:87
  (58 shorter events, 18.5 us)
Async XLA Ops:
  7.2 36.9 %copy-start = (bf16[1,256,2048]{2,1,0:T(8,128)(2,1)S(1)}, bf16[1,256,2048]{2,1,0:T(8,128)(2,1)}, u32[]{:S(2)}) copy-start(bf16[1,256,2048]{2,1,0:T(8,128)(2,1)} %param.13) | copy-start | bytes 3145732
  7.2 23.7 %copy-start.2 = (bf16[1,256,512]{2,1,0:T(8,128)(2,1)S(1)}, bf16[1,256,512]{2,1,0:T(8,128)(2,1)}, u32[]{:S(2)}) copy-start(bf16[1,256,512]{2,1,0:T(8,128)(2,1)} %param.7) | copy-start | bytes 786436
  7.2 152.8 %all-gather.2.cloned.1.call-start = ((), (), s32[]{:S(2)}) async-start(), calls=%async_computation.1 | async-start | bytes 6291456 | tf_op jit(solution)/shard_map/all_gather | solution.py:89
  10.5 10.4 %collective-permute-start.4 = (f32[4,128,128]{2,1,0:T(8,128)S(1)}, f32[4,128,128]{2,1,0:T(8,128)S(1)}, u32[]{:S(2)}, u32[]{:S(2)}) collective-permute-start(f32[4,128,128]{2,1,0:T(8,128)S(1)} %get-tuple-element.19), channel_id=1, source_target_pairs={{0,4},{4,8},{8,12},{12,16},{16,20},{20,24},{24,28},{1,5},{5,9},{9,... | collective-permute-start | bytes 786440 | tf_op jit(solution)/shard_map/ppermute | solution.py:15
  20.9 16.7 %collective-permute-start.5 = (f32[4,128,128]{2,1,0:T(8,128)S(1)}, f32[4,128,128]{2,1,0:T(8,128)S(1)}, u32[]{:S(2)}, u32[]{:S(2)}) collective-permute-start(f32[4,128,128]{2,1,0:T(8,128)S(1)} %collective-permute-done.4), channel_id=1, source_target_pairs={{0,4},{4,8},{8,12},{12,16},{16,20},{20,24},{24,28},{1,5},{5,9},{9,... | collective-permute-start | bytes 786440 | tf_op jit(solution)/shard_map/ppermute | solution.py:15
  25.2 5.8 %collective-permute-start = (f32[1]{0:T(128)}, f32[1]{0:T(128)}, u32[]{:S(2)}, u32[]{:S(2)}) collective-permute-start(f32[1]{0:T(128)} %bitcast.1), channel_id=1, source_target_pairs={{0,4},{4,8},{8,12},{12,16},{16,20},{20,24},{24,28},{1,5},{5,9},{9,... | collective-permute-start | bytes 20 | tf_op jit(solution)/shard_map/ppermute | solution.py:15
  31.0 5.3 %collective-permute-start.1 = (f32[1]{0:T(128)}, f32[1]{0:T(128)}, u32[]{:S(2)}, u32[]{:S(2)}) collective-permute-start(f32[1]{0:T(128)} %collective-permute-done), channel_id=1, source_target_pairs={{0,4},{4,8},{8,12},{12,16},{16,20},{20,24},{24,28},{1,5},{5,9},{9,... | collective-permute-start | bytes 20 | tf_op jit(solution)/shard_map/ppermute | solution.py:15
  37.6 26.4 %copy-start.3 = (f32[4,128]{1,0:T(4,128)S(1)}, f32[4,128]{1,0:T(4,128)}, u32[]{:S(2)}) copy-start(f32[4,128]{1,0:T(4,128)} %param.11) | copy-start | bytes 6148
  37.6 15.6 %collective-permute-start.6 = (f32[4,128,128]{2,1,0:T(8,128)S(1)}, f32[4,128,128]{2,1,0:T(8,128)S(1)}, u32[]{:S(2)}, u32[]{:S(2)}) collective-permute-start(f32[4,128,128]{2,1,0:T(8,128)S(1)} %fusion.14), channel_id=1, source_target_pairs={{0,8},{4,12},{8,16},{12,20},{16,24},{20,28},{1,9},{5,13},{9,17},{1... | collective-permute-start | bytes 786440 | tf_op jit(solution)/shard_map/ppermute | solution.py:15
  47.6 4.9 %collective-permute-start.2 = (f32[1]{0:T(128)}, f32[1]{0:T(128)}, u32[]{:S(2)}, u32[]{:S(2)}) collective-permute-start(f32[1]{0:T(128)} %select_n.117), channel_id=1, source_target_pairs={{0,8},{4,12},{8,16},{12,20},{16,24},{20,28},{1,9},{5,13},{9,17},{1... | collective-permute-start | bytes 20 | tf_op jit(solution)/shard_map/ppermute | solution.py:15
  53.3 10.2 %collective-permute-start.7 = (f32[4,128,128]{2,1,0:T(8,128)S(1)}, f32[4,128,128]{2,1,0:T(8,128)S(1)}, u32[]{:S(2)}, u32[]{:S(2)}) collective-permute-start(f32[4,128,128]{2,1,0:T(8,128)S(1)} %fusion.13), channel_id=1, source_target_pairs={{0,16},{4,20},{8,24},{12,28},{1,17},{5,21},{9,25},{13,29},{2,18},{... | collective-permute-start | bytes 786440 | tf_op jit(solution)/shard_map/ppermute | solution.py:15
  59.5 2.7 %collective-permute-start.3 = (f32[1]{0:T(128)}, f32[1]{0:T(128)}, u32[]{:S(2)}, u32[]{:S(2)}) collective-permute-start(f32[1]{0:T(128)} %select_n.118), channel_id=1, source_target_pairs={{0,16},{4,20},{8,24},{12,28},{1,17},{5,21},{9,25},{13,29},{2,18},{... | collective-permute-start | bytes 20 | tf_op jit(solution)/shard_map/ppermute | solution.py:15
  65.4 30.8 %collective-permute-start.12 = (f32[4,128,128]{1,2,0:T(8,128)S(1)}, f32[4,128,128]{1,2,0:T(8,128)S(1)}, u32[]{:S(2)}, u32[]{:S(2)}) collective-permute-start(f32[4,128,128]{1,2,0:T(8,128)S(1)} %multiply_bitcast_fusion), channel_id=1, source_target_pairs={{4,0},{8,4},{12,8},{16,12},{20,16},{24,20},{28,24},{5,1},{9,5},{13... | collective-permute-start | bytes 786440 | tf_op jit(solution)/shard_map/ppermute | solution.py:15
  66.7 7.1 %collective-permute-start.8 = (f32[1]{0:T(128)}, f32[1]{0:T(128)}, u32[]{:S(2)}, u32[]{:S(2)}) collective-permute-start(f32[1]{0:T(128)} %bitcast.1), channel_id=1, source_target_pairs={{4,0},{8,4},{12,8},{16,12},{20,16},{24,20},{28,24},{5,1},{9,5},{13... | collective-permute-start | bytes 20 | tf_op jit(solution)/shard_map/ppermute | solution.py:15
  73.8 7.1 %collective-permute-start.9 = (f32[1]{0:T(128)}, f32[1]{0:T(128)}, u32[]{:S(2)}, u32[]{:S(2)}) collective-permute-start(f32[1]{0:T(128)} %collective-permute-done.8), channel_id=1, source_target_pairs={{4,0},{8,4},{12,8},{16,12},{20,16},{24,20},{28,24},{5,1},{9,5},{13... | collective-permute-start | bytes 20 | tf_op jit(solution)/shard_map/ppermute | solution.py:15
  82.1 5.7 %collective-permute-start.10 = (f32[1]{0:T(128)}, f32[1]{0:T(128)}, u32[]{:S(2)}, u32[]{:S(2)}) collective-permute-start(f32[1]{0:T(128)} %select_n.135), channel_id=1, source_target_pairs={{8,0},{12,4},{16,8},{20,12},{24,16},{28,20},{9,1},{13,5},{17,9},{2... | collective-permute-start | bytes 20 | tf_op jit(solution)/shard_map/ppermute | solution.py:15
  88.5 6.4 %collective-permute-start.11 = (f32[1]{0:T(128)}, f32[1]{0:T(128)}, u32[]{:S(2)}, u32[]{:S(2)}) collective-permute-start(f32[1]{0:T(128)} %select_n.136), channel_id=1, source_target_pairs={{16,0},{20,4},{24,8},{28,12},{17,1},{21,5},{25,9},{29,13},{18,2},{... | collective-permute-start | bytes 20 | tf_op jit(solution)/shard_map/ppermute | solution.py:15
  96.2 9.1 %collective-permute-start.13 = (f32[4,128,128]{1,2,0:T(8,128)S(1)}, f32[4,128,128]{1,2,0:T(8,128)S(1)}, u32[]{:S(2)}, u32[]{:S(2)}) collective-permute-start(f32[4,128,128]{1,2,0:T(8,128)S(1)} %collective-permute-done.12), channel_id=1, source_target_pairs={{4,0},{8,4},{12,8},{16,12},{20,16},{24,20},{28,24},{5,1},{9,5},{13... | collective-permute-start | bytes 786440 | tf_op jit(solution)/shard_map/ppermute | solution.py:15
  97.9 9.2 %copy-start.1 = (bf16[4,256,256]{2,1,0:T(8,128)(2,1)}, bf16[4,256,256]{2,1,0:T(8,128)(2,1)S(1)}, u32[]{:S(2)}) copy-start(bf16[4,256,256]{2,1,0:T(8,128)(2,1)S(1)} %fusion.2) | copy-start | bytes 1572868
  105.4 39.5 %collective-permute-start.14 = (f32[4,128,128]{1,2,0:T(8,128)S(1)}, f32[4,128,128]{1,2,0:T(8,128)}, u32[]{:S(2)}, u32[]{:S(2)}) collective-permute-start(f32[4,128,128]{1,2,0:T(8,128)S(1)} %fusion.11), channel_id=1, source_target_pairs={{8,0},{12,4},{16,8},{20,12},{24,16},{28,20},{9,1},{13,5},{17,9},{2... | collective-permute-start | bytes 786440 | tf_op jit(solution)/shard_map/ppermute | solution.py:15
  109.6 50.3 %all-to-all-start = ((bf16[2,128,512]{1,2,0:T(8,128)(2,1)}), bf16[2,128,512]{1,2,0:T(8,128)(2,1)S(1)}, u32[]{:S(2)}, u32[]{:S(2)}) async-start(bf16[2,128,512]{1,2,0:T(8,128)(2,1)} %copy.39), calls=%async_computation | async-start | bytes 524288 | tf_op jit(solution)/shard_map/all_to_all | solution.py:86
  145.8 11.5 %collective-permute-start.15 = (f32[4,128,128]{1,2,0:T(8,128)S(1)}, f32[4,128,128]{1,2,0:T(8,128)S(1)}, u32[]{:S(2)}, u32[]{:S(2)}) collective-permute-start(f32[4,128,128]{1,2,0:T(8,128)S(1)} %fusion.10), channel_id=1, source_target_pairs={{16,0},{20,4},{24,8},{28,12},{17,1},{21,5},{25,9},{29,13},{18,2},{... | collective-permute-start | bytes 786440 | tf_op jit(solution)/shard_map/ppermute | solution.py:15
Sparse Core Ops, SparseCore 0:
  31.0 57.0 all-gather.1
where the time goes:
time: 172 us; the launch traced here: 171 us
  starting transfers between devices  52.1 us (30%)
  waiting for transfers between devices  39.9 us (23%)
  blocking collectives  31.5 us (18%)
  between operations  26.5 us (15%)
  matrix products  10.9 us (6%)
  local copies, waits for them, and re-layouts  6.59 us (4%)
  other arithmetic  2.95 us (2%)
    ppermute x16, starting transfers between devices, shifted(): return lax.ppermute(block, axis, route)  48.7 us
    ppermute x16, waiting for transfers between devices, shifted(): return lax.ppermute(block, axis, route)  39.9 us
    psum x1, blocking collectives, on_device(): gain_grad = lax.psum(gain_part, ('seq', 'dp')) / math.sqrt(total_tokens)  31.5 us
    dot_general x1, matrix products, on_device(): jnp.dot(exchanged, lax.all_gather(w_out, 'head', axis=0, tiled=True), pre...  3.73 us
    all_to_all x1, starting transfers between devices, on_device(): lax.all_to_all(normed_rows, 'head', split_axis=0, concat_axis=1, tiled=True)  3.44 us
  transfers between devices with their start and end apart: 18, of which 8 were waited for; matrix products, arithmetic and copies ran while one was open for 8% of the time, Pallas kernels for 0%

commit v1 on v0

v1 whole, which is shorter than its diff:
```python
import functools
import math

import jax
import jax.numpy as jnp
from jax import lax
from jax.experimental import pallas as pl
from jax.experimental.pallas import tpu as pltpu
from jax.sharding import PartitionSpec as P

EPSILON = 1e-05
F32 = jnp.float32
BF16 = jnp.bfloat16
TAIL = 16


def nn(a, b):
    return lax.dot_general(a, b, (((1,), (0,)), ((), ())), preferred_element_type=F32)


def nt(a, b):
    return lax.dot_general(a, b, (((1,), (1,)), ((), ())), preferred_element_type=F32)


def tn(a, b):
    return lax.dot_general(a, b, (((0,), (0,)), ((), ())), preferred_element_type=F32)


def call(body, out_shapes, n_in, flops, moved, smem=()):
    spec = lambda i: pl.BlockSpec(memory_space=pltpu.SMEM if i in smem else pltpu.VMEM)
    return pl.pallas_call(
        body,
        out_shape=[jax.ShapeDtypeStruct(s, t) for s, t in out_shapes],
        in_specs=[spec(i) for i in range(n_in)],
        out_specs=[pl.BlockSpec(memory_space=pltpu.VMEM) for _ in out_shapes],
        cost_estimate=pl.CostEstimate(flops=flops, bytes_accessed=moved, transcendentals=0),
        compiler_params=pltpu.CompilerParams(vmem_limit_bytes=40 << 20),
    )


def swap_route(size, distance, odd):
    route = {i: i for i in range(size)}
    for i in range(size - distance):
        if (i // distance) % 2 == odd:
            route[i], route[i + distance] = i + distance, i
    return sorted(route.items())


def swaps(block, distance):
    size = lax.axis_size("seq")
    return [lax.ppermute(block, "seq", swap_route(size, distance, odd)) for odd in (0, 1)]


def exchange(block, axis, distance):
    size = lax.axis_size(axis)
    return lax.ppermute(block, axis, [(i, i ^ distance) for i in range(size)])


def put_doc(msg_ref, doc, rows):
    msg_ref[rows:, :] = jnp.full((TAIL, msg_ref.shape[1]), doc + 1, F32).astype(BF16)


def taken(even_ref, odd_ref, doc, distance, forward):
    rows = even_ref.shape[0] - TAIL
    me, size = lax.axis_index("seq"), lax.axis_size("seq")
    upper = lax.rem(lax.div(me, distance), 2)
    from_odd = upper == 0 if forward else upper == 1
    there = me >= distance if forward else me + distance < size
    got = jnp.where(from_odd, odd_ref[...].astype(F32), even_ref[...].astype(F32))
    mine = jnp.where(there, doc + 1, -1).astype(F32)
    return jnp.where(got[rows : rows + 1, :] == mine, got[:rows, :], 0.0)


def outer_body(heads, dim, doc_ref, key_ref, value_ref, sum_ref, msg_ref):
    for h in range(heads):
        cols, rows = slice(h * dim, (h + 1) * dim), slice(h * dim, (h + 1) * dim)
        total = tn(key_ref[:, cols], value_ref[:, cols])
        sum_ref[rows, :] = total
        msg_ref[rows, :] = total.astype(BF16)
    put_doc(msg_ref, doc_ref[0, 0], heads * dim)


def local_body(
    heads, dim, query_ref, key_ref, value_ref, cot_ref, w_ref, weight_ref, within_ref, normed_grad_ref
):
    tokens = query_ref.shape[0]
    causal = lax.broadcasted_iota(jnp.int32, (tokens, tokens), 0) >= lax.broadcasted_iota(
        jnp.int32, (tokens, tokens), 1
    )
    for h in range(heads):
        cols = slice(h * dim, (h + 1) * dim)
        scores = nt(query_ref[:, cols], key_ref[:, cols])
        weights = jnp.where(causal, scores, 0.0).astype(BF16)
        weight_ref[h * tokens : (h + 1) * tokens, :] = weights
        within_ref[:, cols] = nn(weights, value_ref[:, cols])
    normed_grad_ref[...] = nt(cot_ref[...], w_ref[...])


def merge_body(distance, forward, first, doc_ref, sum_ref, *refs):
    term_ref, refs = (None, refs) if first else (refs[0], refs[1:])
    even_ref, odd_ref, out_ref, msg_ref = refs
    rows = sum_ref.shape[0]
    doc = doc_ref[0, 0]
    term = taken(even_ref, odd_ref, doc, distance, forward)
    if not first:
        term = term + term_ref[...]
    out_ref[...] = term
    msg_ref[:rows, :] = (sum_ref[...] + term).astype(BF16)
    put_doc(msg_ref, doc, rows)


def forward_body(
    heads, dim, distance, doc_ref, query_ref, within_ref, normed_grad_ref, gain_ref, term_ref,
    even_ref, odd_ref, state_ref, keep_ref, send_ref, grad_ref, outer_ref, msg_ref, gain_grad_ref, normed_ref,
):
    doc = doc_ref[0, 0]
    half = keep_ref.shape[0]
    state_ref[...] = (
        term_ref[...] + taken(even_ref, odd_ref, doc, distance, True)
    ).astype(BF16)
    for h in range(heads):
        cols, rows = slice(h * dim, (h + 1) * dim), slice(h * dim, (h + 1) * dim)
        query = query_ref[:, cols]
        attended = within_ref[:, cols] + nn(query, state_ref[rows, :])
        inv_rms = lax.rsqrt(jnp.mean(attended * attended, axis=-1, keepdims=True) + EPSILON)
        unit = attended * inv_rms
        gain = gain_ref[h : h + 1, :]
        normed_ref[:, cols] = (unit * gain).astype(BF16)
        normed_grad = normed_grad_ref[:, cols]
        gain_grad_ref[h : h + 1, :] = jnp.sum(normed_grad * unit, axis=0, keepdims=True)
        scaled = normed_grad * gain
        grad = inv_rms * (scaled - unit * jnp.mean(scaled * unit, axis=-1, keepdims=True))
        grad = grad.astype(BF16)
        grad_ref[:, cols] = grad
        outer = tn(query, grad)
        outer_ref[rows, :] = outer
        msg_ref[rows, :] = outer.astype(BF16)
    put_doc(msg_ref, doc, heads * dim)
    head = lax.axis_index("head")
    keep_ref[...] = normed_ref[pl.ds(pl.multiple_of(head * half, half), half), :]
    send_ref[...] = normed_ref[pl.ds(pl.multiple_of((1 - head) * half, half), half), :]


def backward_body(
    heads, dim, query_ref, key_ref, value_ref, weight_ref, grad_ref, state_ref,
    query_grad_ref, key_part_ref, value_part_ref,
):
    tokens = query_ref.shape[0]
    causal = lax.broadcasted_iota(jnp.int32, (tokens, tokens), 0) >= lax.broadcasted_iota(
        jnp.int32, (tokens, tokens), 1
    )
    for h in range(heads):
        cols, rows = slice(h * dim, (h + 1) * dim), slice(h * dim, (h + 1) * dim)
        grad = grad_ref[:, cols]
        grad_scores = nt(grad, value_ref[:, cols])
        grad_weights = jnp.where(causal, grad_scores, 0.0).astype(BF16)
        query_grad_ref[:, cols] = (
            nn(grad_weights, key_ref[:, cols]) + nt(grad, state_ref[rows, :])
        ).astype(BF16)
        key_part_ref[:, cols] = tn(grad_weights, query_ref[:, cols])
        value_part_ref[:, cols] = tn(weight_ref[h * tokens : (h + 1) * tokens, :], grad)


def last_body(
    heads, dim, distance, doc_ref, key_ref, value_ref, key_part_ref, value_part_ref, term_ref,
    even_ref, odd_ref, key_grad_ref, value_grad_ref,
):
    state = (
        term_ref[...] + taken(even_ref, odd_ref, doc_ref[0, 0], distance, False)
    ).astype(BF16)
    for h in range(heads):
        cols, rows = slice(h * dim, (h + 1) * dim), slice(h * dim, (h + 1) * dim)
        key_grad_ref[:, cols] = (
            key_part_ref[:, cols] + nt(value_ref[:, cols], state[rows, :])
        ).astype(BF16)
        value_grad_ref[:, cols] = (
            value_part_ref[:, cols] + nn(key_ref[:, cols], state[rows, :])
        ).astype(BF16)


def layer_body(keep_ref, got_ref, own_ref, mine_ref, other_ref, out_ref):
    width = mine_ref.shape[0]
    core = lax.axis_index("dp")
    at = lambda i: pl.ds(pl.multiple_of(i * width, width), width)
    out_ref[...] = (
        nn(keep_ref[...], own_ref[...])
        + nn(got_ref[:, at(core)], mine_ref[...])
        + nn(got_ref[:, at(1 - core)], other_ref[...])
    ).astype(BF16)


def on_device(queries, key_rows, value_rows, stretch_doc, head_gain, w_out, cotangent):
    tokens, width = queries.shape[1:]
    heads, dim = head_gain.shape
    model = w_out.shape[1]
    size = lax.axis_size("seq")
    query, key, value, cot = queries[0], key_rows[0], value_rows[0], cotangent[0]
    matrix = 2 * tokens * dim * dim * heads
    square = 2 * tokens * tokens * dim * heads
    summed, message = (heads * dim, dim), (heads * dim + TAIL, dim)
    distances = [1]
    while 2 * distances[-1] - 1 < size // 2 - 1:
        distances.append(2 * distances[-1])

    core = lax.axis_index("dp")
    half = lax.dynamic_slice_in_dim(w_out, core * (width // 2), width // 2, 0)
    w_mine = exchange(half, "head", 1)
    w_other = exchange(w_mine, "dp", 1)

    def spread(outer, msg, forward):
        term = None
        for distance in distances[:-1]:
            first = term is None
            even, odd = swaps(msg, distance)
            term, msg = call(
                functools.partial(merge_body, distance, forward, first),
                [(summed, F32), (message, BF16)], 4 if first else 5, 0, 1 << 20, (0,),
            )(stretch_doc, outer, *(() if first else (term,)), even, odd)
        return term, *swaps(msg, distances[-1])

    outer, msg = call(
        functools.partial(outer_body, heads, dim), [(summed, F32), (message, BF16)], 3, matrix, 1 << 20, (0,)
    )(stretch_doc, key, value)
    weights, within, normed_grad = call(
        functools.partial(local_body, heads, dim),
        [((heads * tokens, tokens), BF16), ((tokens, width), F32), ((tokens, width), F32)],
        5, 2 * square + 2 * tokens * width * model, 6 << 20,
    )(query, key, value, cot, w_out)
    term, even, odd = spread(outer, msg, True)
    state, keep, send, grad, outer, msg, gain_part = pl.pallas_call(
        functools.partial(forward_body, heads, dim, distances[-1]),
        out_shape=[
            jax.ShapeDtypeStruct(s, t)
            for s, t in (
                (summed, BF16), ((tokens // 2, width), BF16), ((tokens // 2, width), BF16),
                ((tokens, width), BF16), (summed, F32), (message, BF16), ((heads, dim), F32),
            )
        ],
        in_specs=[pl.BlockSpec(memory_space=pltpu.SMEM)] + [pl.BlockSpec(memory_space=pltpu.VMEM)] * 7,
        out_specs=[pl.BlockSpec(memory_space=pltpu.VMEM)] * 7,
        scratch_shapes=[pltpu.VMEM((tokens, width), BF16)],
        cost_estimate=pl.CostEstimate(flops=2 * matrix, bytes_accessed=4 << 20, transcendentals=0),
        compiler_params=pltpu.CompilerParams(vmem_limit_bytes=40 << 20),
    )(stretch_doc, query, within, normed_grad, head_gain, term, even, odd)
    got = exchange(send, "head", 1)
    query_grad, key_part, value_part = call(
        functools.partial(backward_body, heads, dim),
        [((tokens, width), BF16), ((tokens, width), F32), ((tokens, width), F32)],
        6, 4 * square + matrix, 4 << 20,
    )(query, key, value, weights, grad, state)
    if size & (size - 1) == 0:
        gain_sum = gain_part
        for axis, distance in [("dp", 1)] + [("seq", 1 << i) for i in range(size.bit_length() - 1)]:
            gain_sum = gain_sum + exchange(gain_sum, axis, distance)
    else:
        gain_sum = lax.psum(gain_part, ("seq", "dp"))
    gain_grad = gain_sum / math.sqrt(size * lax.axis_size("dp") * tokens)
    term, even, odd = spread(outer, msg, False)
    key_grad, value_grad = call(
        functools.partial(last_body, heads, dim, distances[-1]),
        [((tokens, width), BF16), ((tokens, width), BF16)], 8, 2 * matrix, 3 << 20, (0,),
    )(stretch_doc, key, value, key_part, value_part, term, even, odd)
    (layer_out,) = call(
        layer_body, [((tokens // 2, model), BF16)], 5, 2 * tokens * width * model, 6 << 20
    )(keep, got, w_out, w_mine, w_other)
    return layer_out[None], query_grad[None], key_grad[None], value_grad[None], gain_grad


def solution(mesh):
    rows = P("dp", "seq", "head")
    return jax.shard_map(
        on_device,
        mesh=mesh,
        in_specs=(rows, rows, rows, P("dp", "seq"), P("head", None), P("head", None), P("dp", "seq", None)),
        out_specs=(P("dp", ("seq", "head"), None), rows, rows, rows, P("head", None)),
        check_vma=False,
    )
```

time: 172 us -> 78.4 us (0.46)
  blocking collectives: 31.5 us -> 0 us
  between operations: 26.5 us -> 1.46 us
  starting transfers between devices: 52.1 us -> 29.2 us
  matrix products: 10.9 us -> 0 us
  waiting for transfers between devices: 39.9 us -> 32.4 us
  Pallas kernels: 0 us -> 6.94 us
  other arithmetic: 2.95 us -> 0.59 us
    psum x1 -> x0, blocking collectives: 31.5 us -> none  [on_device(): gain_grad = lax.psum(gain_part, ('seq', 'dp')) / math.sqrt(total_tokens)]
    ppermute x16 -> x15, starting transfers between devices: 48.7 us -> 29.2 us  [the longest x7 16.4 us: exchange(): return lax.ppermute(block, axis, [(i, i ^ distance) for i in range(size)])]
    dot_general x14 -> x0, matrix products: 10.9 us -> none  [the longest x1 3.73 us: on_device(): jnp.dot(exchanged, lax.all_gather(w_out, 'head', axis=0, tiled=True), pre...]
    ppermute x16 -> x15, waiting for transfers between devices: 39.9 us -> 32.4 us  [the longest x7 26.2 us: exchange(): return lax.ppermute(block, axis, [(i, i ^ distance) for i in range(size)])]
    pallas_call x0 -> x8, Pallas kernels: none -> 6.94 us  [the longest x1 1.92 us: on_device(): call(functools.partial(backward_body, heads, dim), [((tokens, width), BF1...]
    all_to_all x1 -> x0, starting transfers between devices: 3.44 us -> none  [on_device(): lax.all_to_all(normed_rows, 'head', split_axis=0, concat_axis=1, tiled=True)]
    unnamed x11 -> x20, local copies, waits for them, and re-layouts: 2.56 us -> 5.98 us
    another operation x3 -> x0, local copies, waits for them, and re-layouts: 2.21 us -> none
  transfers between devices with their start and end apart: 18 -> 15, of which waited for: 8 -> 6; matrix products, arithmetic and copies ran while one was open for 8% -> 1% of each run, Pallas kernels for 0% -> 7%
where the time goes in v1:
time: 78.4 us; the launch traced here: 78 us
  waiting for transfers between devices  32.4 us (41%)
  starting transfers between devices  29.2 us (37%)
  local copies, waits for them, and re-layouts  7.45 us (10%)
  Pallas kernels  6.94 us (9%)
  between operations  1.46 us (2%)
    ppermute x7, waiting for transfers between devices, exchange(): return lax.ppermute(block, axis, [(i, i ^ distance) for i in range(size)])  26.2 us
    ppermute x7, starting transfers between devices, exchange(): return lax.ppermute(block, axis, [(i, i ^ distance) for i in range(size)])  16.4 us
    ppermute x8, starting transfers between devices, swaps(): lax.ppermute(block, 'seq', swap_route(size, distance, odd))  12.7 us
    ppermute x8, waiting for transfers between devices, swaps(): lax.ppermute(block, 'seq', swap_route(size, distance, odd))  6.24 us
    unnamed x20, local copies, waits for them, and re-layouts  5.98 us
    pallas_call x1, Pallas kernels, on_device(): call(functools.partial(backward_body, heads, dim), [((tokens, width), BF1...  1.92 us
  transfers between devices with their start and end apart: 15, of which 6 were waited for; matrix products, arithmetic and copies ran while one was open for 1% of the time, Pallas kernels for 7%

profile of v1, /device:TPU:0, one launch (start us, length us, event | category | flops | bytes accessed | tf_op | source)
XLA Modules:
  0.0 78.0 jit_solution(14539605517731869062)
XLA Ops:
  0.6 1.5 %constant_dynamic-slice_fusion = bf16[256,2048]{1,0:T(8,128)(2,1)S(1)} fusion(bf16[512,2048]{1,0:T(8,128)(2,1)} %own_ref.1, s32[]{:T(128)S(6)} %select_n.3), kind=kLoop, calls=%fused_computation.1 | loop fusion | bytes 2097156 | tf_op jit(solution)/shard_map/dynamic_slice | solution.py:206
  2.1 3.0 %collective-permute-start.5 = (bf16[256,2048]{1,0:T(8,128)(2,1)S(1)}, bf16[256,2048]{1,0:T(8,128)(2,1)S(1)}, u32[]{:S(2)}, u32[]{:S(2)}) collective-permute-start(bf16[256,2048]{1,0:T(8,128)(2,1)S(1)} %constant_dynamic-slice_fusion), channel_id=1, source_target_pairs={{0,2},{2,0},{1,3},{3,1},{4,6},{6,4},{5,7},{7,5},{8,10},{10,8},{9,1... | collective-permute-start | bytes 3145736 | tf_op jit(solution)/shard_map/ppermute | solution.py:56
  5.2 23.2 %collective-permute-done.5.mine_ref = bf16[256,2048]{1,0:T(8,128)(2,1)S(1)} collective-permute-done((bf16[256,2048]{1,0:T(8,128)(2,1)S(1)}, bf16[256,2048]{1,0:T(8,128)(2,1)S(1)}, u32[]{:S(2)}, u32[]{:S(2)}) %collective-permute-start.5) | collective-permute-done | bytes 1048608 | tf_op jit(solution)/shard_map/ppermute | solution.py:56
  29.0 0.9 %copy-done.1 = bf16[1,256,512]{2,1,0:T(8,128)(2,1)S(1)} copy-done((bf16[1,256,512]{2,1,0:T(8,128)(2,1)S(1)}, bf16[1,256,512]{2,1,0:T(8,128)(2,1)}, u32[]{:S(2)}) %copy-start.1) | copy-done | bytes 262168
  29.9 0.9 %copy-done.4 = bf16[1,256,512]{2,1,0:T(8,128)(2,1)S(1)} copy-done((bf16[1,256,512]{2,1,0:T(8,128)(2,1)S(1)}, bf16[1,256,512]{2,1,0:T(8,128)(2,1)}, u32[]{:S(2)}) %copy-start.4) | copy-done | bytes 262168
  31.1 1.8 %collective-permute-start = (bf16[528,128]{1,0:T(8,128)(2,1)S(1)}, bf16[528,128]{1,0:T(8,128)(2,1)S(1)}, u32[]{:S(2)}, u32[]{:S(2)}) collective-permute-start(bf16[528,128]{1,0:T(8,128)(2,1)S(1)} %get-tuple-element.29), channel_id=1, source_target_pairs={{0,4},{4,0},{8,12},{12,8},{16,20},{20,16},{24,28},{28,24},{1,5},{5... | collective-permute-start | bytes 405512 | tf_op jit(solution)/shard_map/ppermute | solution.py:51
  33.6 3.6 %collective-permute-done.refs_0_ = bf16[528,128]{1,0:T(8,128)(2,1)S(1)} collective-permute-done((bf16[528,128]{1,0:T(8,128)(2,1)S(1)}, bf16[528,128]{1,0:T(8,128)(2,1)S(1)}, u32[]{:S(2)}, u32[]{:S(2)}) %collective-permute-start) | collective-permute-done | bytes 135200 | tf_op jit(solution)/shard_map/ppermute | solution.py:51
  37.3 5.9 %collective-permute-start.2 = (bf16[528,128]{1,0:T(8,128)(2,1)S(1)}, bf16[528,128]{1,0:T(8,128)(2,1)S(1)}, u32[]{:S(2)}, u32[]{:S(2)}) collective-permute-start(bf16[528,128]{1,0:T(8,128)(2,1)S(1)} %get-tuple-element.31), channel_id=1, source_target_pairs={{0,8},{4,12},{8,0},{12,4},{16,24},{20,28},{24,16},{28,20},{1,9},{5... | collective-permute-start | bytes 405512 | tf_op jit(solution)/shard_map/ppermute | solution.py:51
  43.8 0.9 %copy-done.2 = bf16[1,256,512]{2,1,0:T(8,128)(2,1)S(1)} copy-done((bf16[1,256,512]{2,1,0:T(8,128)(2,1)S(1)}, bf16[1,256,512]{2,1,0:T(8,128)(2,1)}, u32[]{:S(2)}) %copy-start.2) | copy-done | bytes 262168
  44.8 0.9 %copy-done.5 = bf16[1,256,512]{2,1,0:T(8,128)(2,1)S(1)} copy-done((bf16[1,256,512]{2,1,0:T(8,128)(2,1)S(1)}, bf16[1,256,512]{2,1,0:T(8,128)(2,1)}, u32[]{:S(2)}) %copy-start.5) | copy-done | bytes 262168
  45.7 0.9 %copy-done.7 = bf16[1,256,512]{2,1,0:T(8,128)(2,1)S(1)} copy-done((bf16[1,256,512]{2,1,0:T(8,128)(2,1)S(1)}, bf16[1,256,512]{2,1,0:T(8,128)(2,1)}, u32[]{:S(2)}) %copy-start.7) | copy-done | bytes 262168
  46.7 1.2 %copy-done.8 = bf16[1,256,2048]{2,1,0:T(8,128)(2,1)S(1)} copy-done((bf16[1,256,2048]{2,1,0:T(8,128)(2,1)S(1)}, bf16[1,256,2048]{2,1,0:T(8,128)(2,1)}, u32[]{:S(2)}) %copy-start.8) | copy-done | bytes 1048600
  47.9 1.2 %shard_map.110 = (bf16[1024,256]{1,0:T(8,128)(2,1)S(1)}, f32[256,512]{1,0:T(8,128)S(1)}, f32[256,512]{1,0:T(8,128)S(1)}) custom-call(bf16[256,512]{1,0:T(8,128)(2,1)S(1)} %bitcast.16, bf16[256,512]{1,0:T(8,128)(2,1)S(1)} %bitcast.9, bf16[256,512]{1,0:T(8,128)(2,1)S(1)} %bitcast.13, bf16[256,2048]{1,0:T(8,128)(2,1)S(1)} %bitcast.19, bf16[512,2048]{1,0:T(8,128)(2,1)S(1)} %copy-done), custom_call_target="tpu_custom_call" | custom-call | flops 671088640 | bytes 6291456 | tf_op jit(solution)/shard_map/pallas_call | solution.py:224
  51.3 1.1 %collective-permute-done.11 = f32[4,128]{1,0:T(4,128)S(1)} collective-permute-done((f32[4,128]{1,0:T(4,128)S(1)}, f32[4,128]{1,0:T(4,128)S(1)}, u32[]{:S(2)}, u32[]{:S(2)}) %collective-permute-start.11) | collective-permute-done | bytes 2080 | tf_op jit(solution)/shard_map/ppermute | solution.py:56
  52.5 6.6 %collective-permute-start.12 = (f32[4,128]{1,0:T(4,128)S(1)}, f32[4,128]{1,0:T(4,128)S(1)}, u32[]{:S(2)}, u32[]{:S(2)}) collective-permute-start(f32[4,128]{1,0:T(4,128)S(1)} %add.16), channel_id=1, source_target_pairs={{0,4},{4,0},{8,12},{12,8},{16,20},{20,16},{24,28},{28,24},{1,5},{5... | collective-permute-start | bytes 6152 | tf_op jit(solution)/shard_map/ppermute | solution.py:56
  59.0 1.6 %collective-permute-done.12 = f32[4,128]{1,0:T(4,128)S(1)} collective-permute-done((f32[4,128]{1,0:T(4,128)S(1)}, f32[4,128]{1,0:T(4,128)S(1)}, u32[]{:S(2)}, u32[]{:S(2)}) %collective-permute-start.12) | collective-permute-done | bytes 2080 | tf_op jit(solution)/shard_map/ppermute | solution.py:56
  60.6 1.8 %collective-permute-start.13 = (f32[4,128]{1,0:T(4,128)S(1)}, f32[4,128]{1,0:T(4,128)S(1)}, u32[]{:S(2)}, u32[]{:S(2)}) collective-permute-start(f32[4,128]{1,0:T(4,128)S(1)} %add.17), channel_id=1, source_target_pairs={{0,8},{4,12},{8,0},{12,4},{16,24},{20,28},{24,16},{28,20},{1,9},{5... | collective-permute-start | bytes 6152 | tf_op jit(solution)/shard_map/ppermute | solution.py:56
  62.4 1.5 %collective-permute-start.4 = (bf16[128,512]{1,0:T(8,128)(2,1)S(1)}, bf16[128,512]{1,0:T(8,128)(2,1)S(1)}, u32[]{:S(2)}, u32[]{:S(2)}) collective-permute-start(bf16[128,512]{1,0:T(8,128)(2,1)S(1)} %get-tuple-element.33), channel_id=1, source_target_pairs={{0,2},{2,0},{1,3},{3,1},{4,6},{6,4},{5,7},{7,5},{8,10},{10,8},{9,1... | collective-permute-start | bytes 393224 | tf_op jit(solution)/shard_map/ppermute | solution.py:56
  64.2 3.5 %collective-permute-start.14 = (f32[4,128]{1,0:T(4,128)S(1)}, f32[4,128]{1,0:T(4,128)S(1)}, u32[]{:S(2)}, u32[]{:S(2)}) collective-permute-start(f32[4,128]{1,0:T(4,128)S(1)} %add.18), channel_id=1, source_target_pairs={{0,16},{4,20},{8,24},{12,28},{16,0},{20,4},{24,8},{28,12},{1,17},{... | collective-permute-start | bytes 6152 | tf_op jit(solution)/shard_map/ppermute | solution.py:56
  67.7 1.9 %shard_map.115 = (bf16[256,512]{1,0:T(8,128)(2,1)}, f32[256,512]{1,0:T(8,128)S(1)}, f32[256,512]{1,0:T(8,128)S(1)}) custom-call(bf16[256,512]{1,0:T(8,128)(2,1)S(1)} %bitcast.18, bf16[256,512]{1,0:T(8,128)(2,1)S(1)} %bitcast.10, bf16[256,512]{1,0:T(8,128)(2,1)S(1)} %bitcast.14, bf16[1024,256]{1,0:T(8,128)(2,1)S(1)} %get-tuple-element.34.weight_ref, ...), custom_call_target="tpu_custom_call" | custom-call | flops 301989888 | bytes 4194304 | tf_op jit(solution)/shard_map/pallas_call | solution.py:246
  70.3 1.9 %collective-permute-start.9 = (bf16[528,128]{1,0:T(8,128)(2,1)S(1)}, bf16[528,128]{1,0:T(8,128)(2,1)S(1)}, u32[]{:S(2)}, u32[]{:S(2)}) collective-permute-start(bf16[528,128]{1,0:T(8,128)(2,1)S(1)} %get-tuple-element.43), channel_id=1, source_target_pairs={{0,8},{4,12},{8,0},{12,4},{16,24},{20,28},{24,16},{28,20},{1,9},{5... | collective-permute-start | bytes 405512 | tf_op jit(solution)/shard_map/ppermute | solution.py:51
  72.8 2.6 %collective-permute-done.9.even_ref = bf16[528,128]{1,0:T(8,128)(2,1)S(1)} collective-permute-done((bf16[528,128]{1,0:T(8,128)(2,1)S(1)}, bf16[528,128]{1,0:T(8,128)(2,1)S(1)}, u32[]{:S(2)}, u32[]{:S(2)}) %collective-permute-start.9) | collective-permute-done | bytes 135200 | tf_op jit(solution)/shard_map/ppermute | solution.py:51
  75.4 1.1 %shard_map.117 = (bf16[256,512]{1,0:T(8,128)(2,1)}, bf16[256,512]{1,0:T(8,128)(2,1)}) custom-call(s32[1,1]{1,0:T(1,128)S(6)} %copy.12.doc_ref, bf16[256,512]{1,0:T(8,128)(2,1)S(1)} %bitcast.11, bf16[256,512]{1,0:T(8,128)(2,1)S(1)} %bitcast.15, f32[256,512]{1,0:T(8,128)S(1)} %get-tuple-element.38.key_part_ref, ...), custom_call_target="tpu_custom_call" | custom-call | flops 67108864 | bytes 3145728 | tf_op jit(solution)/shard_map/pallas_call | solution.py:259
  76.5 1.5 %shard_map.114 = bf16[128,2048]{1,0:T(8,128)(2,1)} custom-call(bf16[128,512]{1,0:T(8,128)(2,1)S(1)} %get-tuple-element.32.keep_ref, bf16[128,512]{1,0:T(8,128)(2,1)S(1)} %collective-permute-done.4.got_ref, bf16[512,2048]{1,0:T(8,128)(2,1)S(1)} %copy-done, bf16[256,2048]{1,0:T(8,128)(2,1)S(1)} %collective-permute-done.5.mine_ref, ...), custom_call_target="tpu_custom_call" | custom-call | flops 536870912 | bytes 6291456 | tf_op jit(solution)/shard_map/pallas_call | solution.py:263
  (39 shorter events, 5.5 us)
Async XLA Ops:
  0.6 43.2 %copy-start = (bf16[512,2048]{1,0:T(8,128)(2,1)S(1)}, bf16[512,2048]{1,0:T(8,128)(2,1)}, u32[]{:S(2)}) copy-start(bf16[512,2048]{1,0:T(8,128)(2,1)} %own_ref.1) | copy-start | bytes 6291460
  2.1 26.2 %collective-permute-start.5 = (bf16[256,2048]{1,0:T(8,128)(2,1)S(1)}, bf16[256,2048]{1,0:T(8,128)(2,1)S(1)}, u32[]{:S(2)}, u32[]{:S(2)}) collective-permute-start(bf16[256,2048]{1,0:T(8,128)(2,1)S(1)} %constant_dynamic-slice_fusion), channel_id=1, source_target_pairs={{0,2},{2,0},{1,3},{3,1},{4,6},{6,4},{5,7},{7,5},{8,10},{10,8},{9,1... | collective-permute-start | bytes 3145736 | tf_op jit(solution)/shard_map/ppermute | solution.py:56
  28.3 48.2 %collective-permute-start.6 = (bf16[256,2048]{1,0:T(8,128)(2,1)S(1)}, bf16[256,2048]{1,0:T(8,128)(2,1)S(1)}, u32[]{:S(2)}, u32[]{:S(2)}) collective-permute-start(bf16[256,2048]{1,0:T(8,128)(2,1)S(1)} %collective-permute-done.5.mine_ref), channel_id=1, source_target_pairs={{0,1},{1,0},{2,3},{3,2},{4,5},{5,4},{6,7},{7,6},{8,9},{9,8},{10,11... | collective-permute-start | bytes 3145736 | tf_op jit(solution)/shard_map/ppermute | solution.py:56
  29.0 1.0 %copy-start.1 = (bf16[1,256,512]{2,1,0:T(8,128)(2,1)S(1)}, bf16[1,256,512]{2,1,0:T(8,128)(2,1)}, u32[]{:S(2)}) copy-start(bf16[1,256,512]{2,1,0:T(8,128)(2,1)} %param.8) | copy-start | bytes 786436
  29.9 0.9 %copy-start.4 = (bf16[1,256,512]{2,1,0:T(8,128)(2,1)S(1)}, bf16[1,256,512]{2,1,0:T(8,128)(2,1)}, u32[]{:S(2)}) copy-start(bf16[1,256,512]{2,1,0:T(8,128)(2,1)} %param.9) | copy-start | bytes 786436
  31.1 6.1 %collective-permute-start = (bf16[528,128]{1,0:T(8,128)(2,1)S(1)}, bf16[528,128]{1,0:T(8,128)(2,1)S(1)}, u32[]{:S(2)}, u32[]{:S(2)}) collective-permute-start(bf16[528,128]{1,0:T(8,128)(2,1)S(1)} %get-tuple-element.29), channel_id=1, source_target_pairs={{0,4},{4,0},{8,12},{12,8},{16,20},{20,16},{24,28},{28,24},{1,5},{5... | collective-permute-start | bytes 405512 | tf_op jit(solution)/shard_map/ppermute | solution.py:51
  32.9 4.3 %collective-permute-start.1 = (bf16[528,128]{1,0:T(8,128)(2,1)S(1)}, bf16[528,128]{1,0:T(8,128)(2,1)S(1)}, u32[]{:S(2)}, u32[]{:S(2)}) collective-permute-start(bf16[528,128]{1,0:T(8,128)(2,1)S(1)} %get-tuple-element.29), channel_id=1, source_target_pairs={{0,0},{4,8},{8,4},{12,16},{16,12},{20,24},{24,20},{28,28},{1,1},{5... | collective-permute-start | bytes 405512 | tf_op jit(solution)/shard_map/ppermute | solution.py:51
  37.3 11.8 %copy-start.9 = (f32[4,128]{1,0:T(4,128)S(1)}, f32[4,128]{1,0:T(4,128)}, u32[]{:S(2)}) copy-start(f32[4,128]{1,0:T(4,128)} %gain_ref.1) | copy-start | bytes 6148
  37.3 11.8 %collective-permute-start.2 = (bf16[528,128]{1,0:T(8,128)(2,1)S(1)}, bf16[528,128]{1,0:T(8,128)(2,1)S(1)}, u32[]{:S(2)}, u32[]{:S(2)}) collective-permute-start(bf16[528,128]{1,0:T(8,128)(2,1)S(1)} %get-tuple-element.31), channel_id=1, source_target_pairs={{0,8},{4,12},{8,0},{12,4},{16,24},{20,28},{24,16},{28,20},{1,9},{5... | collective-permute-start | bytes 405512 | tf_op jit(solution)/shard_map/ppermute | solution.py:51
  43.1 6.0 %collective-permute-start.3 = (bf16[528,128]{1,0:T(8,128)(2,1)S(1)}, bf16[528,128]{1,0:T(8,128)(2,1)S(1)}, u32[]{:S(2)}, u32[]{:S(2)}) collective-permute-start(bf16[528,128]{1,0:T(8,128)(2,1)S(1)} %get-tuple-element.31), channel_id=1, source_target_pairs={{0,0},{4,4},{8,16},{12,20},{16,8},{20,12},{24,24},{28,28},{1,1},{5... | collective-permute-start | bytes 405512 | tf_op jit(solution)/shard_map/ppermute | solution.py:51
  43.8 1.0 %copy-start.2 = (bf16[1,256,512]{2,1,0:T(8,128)(2,1)S(1)}, bf16[1,256,512]{2,1,0:T(8,128)(2,1)}, u32[]{:S(2)}) copy-start(bf16[1,256,512]{2,1,0:T(8,128)(2,1)} %param.8) | copy-start | bytes 786436
  44.8 0.9 %copy-start.5 = (bf16[1,256,512]{2,1,0:T(8,128)(2,1)S(1)}, bf16[1,256,512]{2,1,0:T(8,128)(2,1)}, u32[]{:S(2)}) copy-start(bf16[1,256,512]{2,1,0:T(8,128)(2,1)} %param.9) | copy-start | bytes 786436
  46.7 1.2 %copy-start.8 = (bf16[1,256,2048]{2,1,0:T(8,128)(2,1)S(1)}, bf16[1,256,2048]{2,1,0:T(8,128)(2,1)}, u32[]{:S(2)}) copy-start(bf16[1,256,2048]{2,1,0:T(8,128)(2,1)} %param.13) | copy-start | bytes 3145732
  47.9 19.8 %copy-start.3 = (bf16[1,256,512]{2,1,0:T(8,128)(2,1)S(1)}, bf16[1,256,512]{2,1,0:T(8,128)(2,1)}, u32[]{:S(2)}) copy-start(bf16[1,256,512]{2,1,0:T(8,128)(2,1)} %param.8) | copy-start | bytes 786436
  47.9 19.8 %copy-start.6 = (bf16[1,256,512]{2,1,0:T(8,128)(2,1)S(1)}, bf16[1,256,512]{2,1,0:T(8,128)(2,1)}, u32[]{:S(2)}) copy-start(bf16[1,256,512]{2,1,0:T(8,128)(2,1)} %param.9) | copy-start | bytes 786436
  50.0 19.6 %collective-permute-start.7 = (bf16[528,128]{1,0:T(8,128)(2,1)S(1)}, bf16[528,128]{1,0:T(8,128)(2,1)S(1)}, u32[]{:S(2)}, u32[]{:S(2)}) collective-permute-start(bf16[528,128]{1,0:T(8,128)(2,1)S(1)} %get-tuple-element.41), channel_id=1, source_target_pairs={{0,4},{4,0},{8,12},{12,8},{16,20},{20,16},{24,28},{28,24},{1,5},{5... | collective-permute-start | bytes 405512 | tf_op jit(solution)/shard_map/ppermute | solution.py:51
  50.6 19.0 %collective-permute-start.8 = (bf16[528,128]{1,0:T(8,128)(2,1)S(1)}, bf16[528,128]{1,0:T(8,128)(2,1)S(1)}, u32[]{:S(2)}, u32[]{:S(2)}) collective-permute-start(bf16[528,128]{1,0:T(8,128)(2,1)S(1)} %get-tuple-element.41), channel_id=1, source_target_pairs={{0,0},{4,8},{8,4},{12,16},{16,12},{20,24},{24,20},{28,28},{1,1},{5... | collective-permute-start | bytes 405512 | tf_op jit(solution)/shard_map/ppermute | solution.py:51
  51.2 1.2 %collective-permute-start.11 = (f32[4,128]{1,0:T(4,128)S(1)}, f32[4,128]{1,0:T(4,128)S(1)}, u32[]{:S(2)}, u32[]{:S(2)}) collective-permute-start(f32[4,128]{1,0:T(4,128)S(1)} %get-tuple-element.46), channel_id=1, source_target_pairs={{0,1},{1,0},{2,3},{3,2},{4,5},{5,4},{6,7},{7,6},{8,9},{9,8},{10,11... | collective-permute-start | bytes 6152 | tf_op jit(solution)/shard_map/ppermute | solution.py:56
  52.5 8.1 %collective-permute-start.12 = (f32[4,128]{1,0:T(4,128)S(1)}, f32[4,128]{1,0:T(4,128)S(1)}, u32[]{:S(2)}, u32[]{:S(2)}) collective-permute-start(f32[4,128]{1,0:T(4,128)S(1)} %add.16), channel_id=1, source_target_pairs={{0,4},{4,0},{8,12},{12,8},{16,20},{20,16},{24,28},{28,24},{1,5},{5... | collective-permute-start | bytes 6152 | tf_op jit(solution)/shard_map/ppermute | solution.py:56
  60.6 3.6 %collective-permute-start.13 = (f32[4,128]{1,0:T(4,128)S(1)}, f32[4,128]{1,0:T(4,128)S(1)}, u32[]{:S(2)}, u32[]{:S(2)}) collective-permute-start(f32[4,128]{1,0:T(4,128)S(1)} %add.17), channel_id=1, source_target_pairs={{0,8},{4,12},{8,0},{12,4},{16,24},{20,28},{24,16},{28,20},{1,9},{5... | collective-permute-start | bytes 6152 | tf_op jit(solution)/shard_map/ppermute | solution.py:56
  62.4 14.1 %collective-permute-start.4 = (bf16[128,512]{1,0:T(8,128)(2,1)S(1)}, bf16[128,512]{1,0:T(8,128)(2,1)S(1)}, u32[]{:S(2)}, u32[]{:S(2)}) collective-permute-start(bf16[128,512]{1,0:T(8,128)(2,1)S(1)} %get-tuple-element.33), channel_id=1, source_target_pairs={{0,2},{2,0},{1,3},{3,1},{4,6},{6,4},{5,7},{7,5},{8,10},{10,8},{9,1... | collective-permute-start | bytes 393224 | tf_op jit(solution)/shard_map/ppermute | solution.py:56
  64.2 8.0 %collective-permute-start.14 = (f32[4,128]{1,0:T(4,128)S(1)}, f32[4,128]{1,0:T(4,128)S(1)}, u32[]{:S(2)}, u32[]{:S(2)}) collective-permute-start(f32[4,128]{1,0:T(4,128)S(1)} %add.18), channel_id=1, source_target_pairs={{0,16},{4,20},{8,24},{12,28},{16,0},{20,4},{24,8},{28,12},{1,17},{... | collective-permute-start | bytes 6152 | tf_op jit(solution)/shard_map/ppermute | solution.py:56
  69.7 3.1 %collective-permute-start.10 = (bf16[528,128]{1,0:T(8,128)(2,1)S(1)}, bf16[528,128]{1,0:T(8,128)(2,1)S(1)}, u32[]{:S(2)}, u32[]{:S(2)}) collective-permute-start(bf16[528,128]{1,0:T(8,128)(2,1)S(1)} %get-tuple-element.43), channel_id=1, source_target_pairs={{0,0},{4,4},{8,16},{12,20},{16,8},{20,12},{24,24},{28,28},{1,1},{5... | collective-permute-start | bytes 405512 | tf_op jit(solution)/shard_map/ppermute | solution.py:51
  70.3 5.1 %collective-permute-start.9 = (bf16[528,128]{1,0:T(8,128)(2,1)S(1)}, bf16[528,128]{1,0:T(8,128)(2,1)S(1)}, u32[]{:S(2)}, u32[]{:S(2)}) collective-permute-start(bf16[528,128]{1,0:T(8,128)(2,1)S(1)} %get-tuple-element.43), channel_id=1, source_target_pairs={{0,8},{4,12},{8,0},{12,4},{16,24},{20,28},{24,16},{28,20},{1,9},{5... | collective-permute-start | bytes 405512 | tf_op jit(solution)/shard_map/ppermute | solution.py:51
  (1 other events, 0.9 us)

commit v2 on v1

--- a/solution.py
+++ b/solution.py
@@ -12,6 +12,7 @@
 F32 = jnp.float32
 BF16 = jnp.bfloat16
 TAIL = 16
+GAIN = 4
 
 
 def nn(a, b):
@@ -26,13 +27,14 @@
     return lax.dot_general(a, b, (((0,), (0,)), ((), ())), preferred_element_type=F32)
 
 
-def call(body, out_shapes, n_in, flops, moved, smem=()):
-    spec = lambda i: pl.BlockSpec(memory_space=pltpu.SMEM if i in smem else pltpu.VMEM)
+def call(body, outs, places, flops, moved, scratch=()):
+    space = {"s": pltpu.SMEM, "v": pltpu.VMEM, "h": pltpu.HBM}
     return pl.pallas_call(
         body,
-        out_shape=[jax.ShapeDtypeStruct(s, t) for s, t in out_shapes],
-        in_specs=[spec(i) for i in range(n_in)],
-        out_specs=[pl.BlockSpec(memory_space=pltpu.VMEM) for _ in out_shapes],
+        out_shape=[jax.ShapeDtypeStruct(s, t) for s, t in outs],
+        in_specs=[pl.BlockSpec(memory_space=space[p]) for p in places],
+        out_specs=[pl.BlockSpec(memory_space=pltpu.VMEM) for _ in outs],
+        scratch_shapes=list(scratch),
         cost_estimate=pl.CostEstimate(flops=flops, bytes_accessed=moved, transcendentals=0),
         compiler_params=pltpu.CompilerParams(vmem_limit_bytes=40 << 20),
     )
@@ -56,8 +58,19 @@
     return lax.ppermute(block, axis, [(i, i ^ distance) for i in range(size)])
 
 
-def put_doc(msg_ref, doc, rows):
-    msg_ref[rows:, :] = jnp.full((TAIL, msg_ref.shape[1]), doc + 1, F32).astype(BF16)
+def put_tail(msg_ref, doc, gain=None):
+    rows, dim = msg_ref.shape[0] - TAIL, msg_ref.shape[1]
+    high = jnp.zeros((GAIN, dim), F32) if gain is None else gain.astype(BF16).astype(F32)
+    low = jnp.zeros((GAIN, dim), F32) if gain is None else gain - high
+    low = low.astype(BF16).astype(F32)
+    number = jnp.full((TAIL - 2 * GAIN, dim), doc + 1, jnp.int32).astype(F32)
+    msg_ref[rows:, :] = jnp.concatenate([high, low, number], axis=0).astype(BF16)
+    return high + low
+
+
+def sent_gain(msg_ref):
+    tail = msg_ref[msg_ref.shape[0] - TAIL :, :].astype(F32)
+    return tail[:GAIN, :] + tail[GAIN : 2 * GAIN, :]
 
 
 def taken(even_ref, odd_ref, doc, distance, forward):
@@ -68,21 +81,43 @@
     there = me >= distance if forward else me + distance < size
     got = jnp.where(from_odd, odd_ref[...].astype(F32), even_ref[...].astype(F32))
     mine = jnp.where(there, doc + 1, -1).astype(F32)
-    return jnp.where(got[rows : rows + 1, :] == mine, got[:rows, :], 0.0)
-
-
-def outer_body(heads, dim, doc_ref, key_ref, value_ref, sum_ref, msg_ref):
+    number = got[rows + 2 * GAIN : rows + 2 * GAIN + 1, :]
+    return jnp.where(number == mine, got[:rows, :], 0.0)
+
+
+def opening_body(
+    heads, dim, doc_ref, query_hbm, key_hbm, value_hbm, w_hbm,
+    query_ref, key_ref, value_ref, half_ref, sum_ref, msg_ref, sems,
+):
+    width = half_ref.shape[0]
+    core = lax.axis_index("dp")
+    ours = w_hbm.at[pl.ds(pl.multiple_of(core * width, width), width), :]
+    copies = [
+        pltpu.make_async_copy(src, dst, sems.at[i])
+        for i, (src, dst) in enumerate(
+            ((key_hbm, key_ref), (value_hbm, value_ref), (ours, half_ref), (query_hbm, query_ref))
+        )
+    ]
+    for copy in copies:
+        copy.start()
+    put_tail(msg_ref, doc_ref[0, 0])
+    copies[0].wait()
+    copies[1].wait()
     for h in range(heads):
         cols, rows = slice(h * dim, (h + 1) * dim), slice(h * dim, (h + 1) * dim)
         total = tn(key_ref[:, cols], value_ref[:, cols])
         sum_ref[rows, :] = total
         msg_ref[rows, :] = total.astype(BF16)
-    put_doc(msg_ref, doc_ref[0, 0], heads * dim)
+    copies[2].wait()
+    copies[3].wait()
 
 
 def local_body(
-    heads, dim, query_ref, key_ref, value_ref, cot_ref, w_ref, weight_ref, within_ref, normed_grad_ref
-):
+    heads, dim, query_ref, key_ref, value_ref, cot_hbm, w_ref,
+    weight_ref, within_ref, normed_grad_ref, cot_ref, sem,
+):
+    copy = pltpu.make_async_copy(cot_hbm, cot_ref, sem)
+    copy.start()
     tokens = query_ref.shape[0]
     causal = lax.broadcasted_iota(jnp.int32, (tokens, tokens), 0) >= lax.broadcasted_iota(
         jnp.int32, (tokens, tokens), 1
@@ -93,12 +128,13 @@
         weights = jnp.where(causal, scores, 0.0).astype(BF16)
         weight_ref[h * tokens : (h + 1) * tokens, :] = weights
         within_ref[:, cols] = nn(weights, value_ref[:, cols])
+    copy.wait()
     normed_grad_ref[...] = nt(cot_ref[...], w_ref[...])
 
 
-def merge_body(distance, forward, first, doc_ref, sum_ref, *refs):
+def merge_body(distance, forward, first, gains, doc_ref, sum_ref, *refs):
     term_ref, refs = (None, refs) if first else (refs[0], refs[1:])
-    even_ref, odd_ref, out_ref, msg_ref = refs
+    even_ref, odd_ref, own_ref, out_ref, msg_ref = refs[:5]
     rows = sum_ref.shape[0]
     doc = doc_ref[0, 0]
     term = taken(even_ref, odd_ref, doc, distance, forward)
@@ -106,7 +142,11 @@
         term = term + term_ref[...]
     out_ref[...] = term
     msg_ref[:rows, :] = (sum_ref[...] + term).astype(BF16)
-    put_doc(msg_ref, doc, rows)
+    if gains:
+        gain = sent_gain(own_ref) + sent_gain(even_ref)
+        refs[5][...] = put_tail(msg_ref, doc, gain)
+    else:
+        put_tail(msg_ref, doc)
 
 
 def forward_body(
@@ -135,7 +175,7 @@
         outer = tn(query, grad)
         outer_ref[rows, :] = outer
         msg_ref[rows, :] = outer.astype(BF16)
-    put_doc(msg_ref, doc, heads * dim)
+    put_tail(msg_ref, doc, gain_grad_ref[...])
     head = lax.axis_index("head")
     keep_ref[...] = normed_ref[pl.ds(pl.multiple_of(head * half, half), half), :]
     send_ref[...] = normed_ref[pl.ds(pl.multiple_of((1 - head) * half, half), half), :]
@@ -162,9 +202,15 @@
 
 
 def last_body(
-    heads, dim, distance, doc_ref, key_ref, value_ref, key_part_ref, value_part_ref, term_ref,
-    even_ref, odd_ref, key_grad_ref, value_grad_ref,
-):
+    heads, dim, distance, gains, doc_ref, key_ref, value_ref, key_part_ref, value_part_ref, term_ref,
+    even_ref, odd_ref, *refs,
+):
+    if gains:
+        own_ref, far_ref, farther_ref, key_grad_ref, value_grad_ref, gain_ref = refs
+        near = sent_gain(own_ref) + sent_gain(even_ref)
+        gain_ref[...] = near + (far_ref[...] + farther_ref[...])
+    else:
+        key_grad_ref, value_grad_ref = refs
     state = (
         term_ref[...] + taken(even_ref, odd_ref, doc_ref[0, 0], distance, False)
     ).astype(BF16)
@@ -194,74 +240,76 @@
     heads, dim = head_gain.shape
     model = w_out.shape[1]
     size = lax.axis_size("seq")
-    query, key, value, cot = queries[0], key_rows[0], value_rows[0], cotangent[0]
     matrix = 2 * tokens * dim * dim * heads
     square = 2 * tokens * tokens * dim * heads
-    summed, message = (heads * dim, dim), (heads * dim + TAIL, dim)
+    rows, summed, message = (tokens, width), (heads * dim, dim), (heads * dim + TAIL, dim)
+    small = (heads, dim)
     distances = [1]
     while 2 * distances[-1] - 1 < size // 2 - 1:
         distances.append(2 * distances[-1])
-
-    core = lax.axis_index("dp")
-    half = lax.dynamic_slice_in_dim(w_out, core * (width // 2), width // 2, 0)
-    w_mine = exchange(half, "head", 1)
-    w_other = exchange(w_mine, "dp", 1)
+    last = distances[-1]
+    gains = size & (size - 1) == 0 and len(distances) > 1
 
     def spread(outer, msg, forward):
-        term = None
+        term, gain = None, None
         for distance in distances[:-1]:
             first = term is None
+            carry = gains and not forward
             even, odd = swaps(msg, distance)
-            term, msg = call(
-                functools.partial(merge_body, distance, forward, first),
-                [(summed, F32), (message, BF16)], 4 if first else 5, 0, 1 << 20, (0,),
-            )(stretch_doc, outer, *(() if first else (term,)), even, odd)
-        return term, *swaps(msg, distances[-1])
-
-    outer, msg = call(
-        functools.partial(outer_body, heads, dim), [(summed, F32), (message, BF16)], 3, matrix, 1 << 20, (0,)
-    )(stretch_doc, key, value)
+            term, msg, *gain = call(
+                functools.partial(merge_body, distance, forward, first, carry),
+                [(summed, F32), (message, BF16)] + [(small, F32)] * carry,
+                "s" + "v" * (4 if first else 5), flops=0, moved=1 << 20,
+            )(stretch_doc, outer, *(() if first else (term,)), even, odd, msg)
+        return term, *swaps(msg, last), msg, gain
+
+    in_hbm = lambda block: pltpu.with_memory_space_constraint(block, pltpu.HBM)
+    query, key, value, half, outer, msg = call(
+        functools.partial(opening_body, heads, dim),
+        [(rows, BF16)] * 3 + [((width // 2, model), BF16), (summed, F32), (message, BF16)],
+        "shhhh", flops=matrix, moved=4 << 20, scratch=[pltpu.SemaphoreType.DMA((4,))],
+    )(stretch_doc, in_hbm(queries[0]), in_hbm(key_rows[0]), in_hbm(value_rows[0]), in_hbm(w_out))
+    w_mine = exchange(half, "head", 1)
     weights, within, normed_grad = call(
         functools.partial(local_body, heads, dim),
-        [((heads * tokens, tokens), BF16), ((tokens, width), F32), ((tokens, width), F32)],
-        5, 2 * square + 2 * tokens * width * model, 6 << 20,
-    )(query, key, value, cot, w_out)
-    term, even, odd = spread(outer, msg, True)
-    state, keep, send, grad, outer, msg, gain_part = pl.pallas_call(
-        functools.partial(forward_body, heads, dim, distances[-1]),
-        out_shape=[
-            jax.ShapeDtypeStruct(s, t)
-            for s, t in (
-                (summed, BF16), ((tokens // 2, width), BF16), ((tokens // 2, width), BF16),
-                ((tokens, width), BF16), (summed, F32), (message, BF16), ((heads, dim), F32),
-            )
+        [((heads * tokens, tokens), BF16), (rows, F32), (rows, F32)],
+        "vvvhv", flops=2 * square + 2 * tokens * width * model, moved=6 << 20,
+        scratch=[pltpu.VMEM((tokens, model), BF16), pltpu.SemaphoreType.DMA],
+    )(query, key, value, in_hbm(cotangent[0]), w_out)
+    term, even, odd, _, _ = spread(outer, msg, True)
+    state, keep, send, grad, outer, msg, gain_part = call(
+        functools.partial(forward_body, heads, dim, last),
+        [
+            (summed, BF16), ((tokens // 2, width), BF16), ((tokens // 2, width), BF16),
+            (rows, BF16), (summed, F32), (message, BF16), (small, F32),
         ],
-        in_specs=[pl.BlockSpec(memory_space=pltpu.SMEM)] + [pl.BlockSpec(memory_space=pltpu.VMEM)] * 7,
-        out_specs=[pl.BlockSpec(memory_space=pltpu.VMEM)] * 7,
-        scratch_shapes=[pltpu.VMEM((tokens, width), BF16)],
-        cost_estimate=pl.CostEstimate(flops=2 * matrix, bytes_accessed=4 << 20, transcendentals=0),
-        compiler_params=pltpu.CompilerParams(vmem_limit_bytes=40 << 20),
+        "svvvvvvv", flops=2 * matrix, moved=4 << 20, scratch=[pltpu.VMEM(rows, BF16)],
     )(stretch_doc, query, within, normed_grad, head_gain, term, even, odd)
     got = exchange(send, "head", 1)
     query_grad, key_part, value_part = call(
         functools.partial(backward_body, heads, dim),
-        [((tokens, width), BF16), ((tokens, width), F32), ((tokens, width), F32)],
-        6, 4 * square + matrix, 4 << 20,
+        [(rows, BF16), (rows, F32), (rows, F32)],
+        "vvvvvv", flops=4 * square + matrix, moved=4 << 20,
     )(query, key, value, weights, grad, state)
-    if size & (size - 1) == 0:
-        gain_sum = gain_part
-        for axis, distance in [("dp", 1)] + [("seq", 1 << i) for i in range(size.bit_length() - 1)]:
-            gain_sum = gain_sum + exchange(gain_sum, axis, distance)
+    term, even, odd, msg, gain = spread(outer, msg, False)
+    even, got = lax.optimization_barrier((even, got))
+    far = []
+    if gains:
+        far = [msg] + [exchange(gain[0], "seq", d) for d in (size // 2, size // 2 + last)]
+    key_grad, value_grad, *gain = call(
+        functools.partial(last_body, heads, dim, last, gains),
+        [(rows, BF16), (rows, BF16)] + [(small, F32)] * gains,
+        "s" + "v" * (7 + len(far)), flops=2 * matrix, moved=3 << 20,
+    )(stretch_doc, key, value, key_part, value_part, term, even, odd, *far)
+    if gains:
+        gain[0], w_mine = lax.optimization_barrier((gain[0], w_mine))
+        gain_sum = gain[0] + exchange(gain[0], "dp", 1)
     else:
         gain_sum = lax.psum(gain_part, ("seq", "dp"))
     gain_grad = gain_sum / math.sqrt(size * lax.axis_size("dp") * tokens)
-    term, even, odd = spread(outer, msg, False)
-    key_grad, value_grad = call(
-        functools.partial(last_body, heads, dim, distances[-1]),
-        [((tokens, width), BF16), ((tokens, width), BF16)], 8, 2 * matrix, 3 << 20, (0,),
-    )(stretch_doc, key, value, key_part, value_part, term, even, odd)
+    w_other = exchange(w_mine, "dp", 1)
     (layer_out,) = call(
-        layer_body, [((tokens // 2, model), BF16)], 5, 2 * tokens * width * model, 6 << 20
+        layer_body, [((tokens // 2, model), BF16)], "vvvvv", flops=2 * tokens * width * model, moved=6 << 20
     )(keep, got, w_out, w_mine, w_other)
     return layer_out[None], query_grad[None], key_grad[None], value_grad[None], gain_grad
 

time: 78.4 us -> 49.7 us (0.63)
  waiting for transfers between devices: 32.4 us -> 8.56 us
  local copies, waits for them, and re-layouts: 7.45 us -> 0.01 us
  Pallas kernels: 6.94 us -> 9.4 us
    ppermute x7 -> x6, waiting for transfers between devices: 26.2 us -> 2.16 us  [exchange(): return lax.ppermute(block, axis, [(i, i ^ distance) for i in range(size)])]
    ppermute x8, starting transfers between devices: 12.7 us -> 19.6 us  [swaps(): lax.ppermute(block, 'seq', swap_route(size, distance, odd))]
    ppermute x7 -> x6, starting transfers between devices: 16.4 us -> 9.73 us  [exchange(): return lax.ppermute(block, axis, [(i, i ^ distance) for i in range(size)])]
    unnamed x20 -> x4, local copies, waits for them, and re-layouts: 5.98 us -> 0.01 us
    pallas_call x7, Pallas kernels: 5.75 us -> 7.42 us  [the longest x1 1.92 us: on_device(): call(functools.partial(backward_body, heads, dim), [(rows, BF16), (rows,...]
    dynamic_slice x1 -> x0, local copies, waits for them, and re-layouts: 1.47 us -> none  [on_device(): half = lax.dynamic_slice_in_dim(w_out, core * (width // 2), width // 2, 0)]
    pallas_call x1, Pallas kernels: 1.18 us -> 1.98 us  [on_device(): call(functools.partial(local_body, heads, dim), [((heads * tokens, tokens...]
  transfers between devices with their start and end apart: 15 -> 14, of which waited for: 6 -> 4; matrix products, arithmetic and copies ran while one was open for 1% -> 1% of each run, Pallas kernels for 7% -> 13%
where the time goes in v2:
time: 49.7 us; the launch traced here: 49.4 us
  starting transfers between devices  29.3 us (59%)
  Pallas kernels  9.4 us (19%)
  waiting for transfers between devices  8.56 us (17%)
  between operations  1.53 us (3%)
  other arithmetic  0.58 us (1%)
    ppermute x8, starting transfers between devices, swaps(): lax.ppermute(block, 'seq', swap_route(size, distance, odd))  19.6 us
    ppermute x6, starting transfers between devices, exchange(): return lax.ppermute(block, axis, [(i, i ^ distance) for i in range(size)])  9.73 us
    ppermute x8, waiting for transfers between devices, swaps(): lax.ppermute(block, 'seq', swap_route(size, distance, odd))  6.4 us
    ppermute x6, waiting for transfers between devices, exchange(): return lax.ppermute(block, axis, [(i, i ^ distance) for i in range(size)])  2.16 us
    pallas_call x1, Pallas kernels, on_device(): call(functools.partial(local_body, heads, dim), [((heads * tokens, tokens...  1.98 us
    pallas_call x1, Pallas kernels, on_device(): call(functools.partial(backward_body, heads, dim), [(rows, BF16), (rows,...  1.92 us
    pallas_call x1, Pallas kernels, on_device(): call(layer_body, [((tokens // 2, model), BF16)], 'vvvvv', flops=2 * token...  1.52 us
    pallas_call x1, Pallas kernels, on_device(): call(functools.partial(opening_body, heads, dim), [(rows, BF16)] * 3 + [(...  1.46 us
  transfers between devices with their start and end apart: 14, of which 4 were waited for; matrix products, arithmetic and copies ran while one was open for 1% of the time, Pallas kernels for 13%

profile of v2, /device:TPU:0, one launch (start us, length us, event | category | flops | bytes accessed | tf_op | source)
XLA Modules:
  0.0 49.4 jit_solution(6974783438921099470)
XLA Ops:
  1.4 1.5 %shard_map.110 = (bf16[256,512]{1,0:T(8,128)(2,1)S(1)}, bf16[256,512]{1,0:T(8,128)(2,1)S(1)}, bf16[256,512]{1,0:T(8,128)(2,1)S(1)}, bf16[256,2048]{1,0:T(8,128)(...) custom-call(s32[1,1]{1,0:T(1,128)S(6)} %copy.12.doc_ref, bf16[256,512]{1,0:T(8,128)(2,1)} %bitcast.10, ...), custom_call_target="tpu_custom_call" | custom-call | flops 33554432 | bytes 4194304 | tf_op jit(solution)/shard_map/pallas_call | solution.py:267
  2.9 3.0 %collective-permute-start.11 = (bf16[256,2048]{1,0:T(8,128)(2,1)S(1)}, bf16[256,2048]{1,0:T(8,128)(2,1)S(1)}, u32[]{:S(2)}, u32[]{:S(2)}) collective-permute-start(bf16[256,2048]{1,0:T(8,128)(2,1)S(1)} %get-tuple-element.59), channel_id=1, source_target_pairs={{0,2},{2,0},{1,3},{3,1},{4,6},{6,4},{5,7},{7,5},{8,10},{10,8},{9,1... | collective-permute-start | bytes 3145736 | tf_op jit(solution)/shard_map/ppermute | solution.py:58
  5.9 1.5 %collective-permute-start = (bf16[528,128]{1,0:T(8,128)(2,1)S(1)}, bf16[528,128]{1,0:T(8,128)(2,1)S(1)}, u32[]{:S(2)}, u32[]{:S(2)}) collective-permute-start(bf16[528,128]{1,0:T(8,128)(2,1)S(1)} %get-tuple-element.41.refs_2_), channel_id=1, source_target_pairs={{0,4},{4,0},{8,12},{12,8},{16,20},{20,16},{24,28},{28,24},{1,5},{5... | collective-permute-start | bytes 405512 | tf_op jit(solution)/shard_map/ppermute | solution.py:53
  7.4 0.7 %collective-permute-start.1 = (bf16[528,128]{1,0:T(8,128)(2,1)S(1)}, bf16[528,128]{1,0:T(8,128)(2,1)S(1)}, u32[]{:S(2)}, u32[]{:S(2)}) collective-permute-start(bf16[528,128]{1,0:T(8,128)(2,1)S(1)} %get-tuple-element.41.refs_2_), channel_id=1, source_target_pairs={{0,0},{4,8},{8,4},{12,16},{16,12},{20,24},{24,20},{28,28},{1,1},{5... | collective-permute-start | bytes 405512 | tf_op jit(solution)/shard_map/ppermute | solution.py:53
  8.1 2.9 %collective-permute-done.refs_0_ = bf16[528,128]{1,0:T(8,128)(2,1)S(1)} collective-permute-done((bf16[528,128]{1,0:T(8,128)(2,1)S(1)}, bf16[528,128]{1,0:T(8,128)(2,1)S(1)}, u32[]{:S(2)}, u32[]{:S(2)}) %collective-permute-start) | collective-permute-done | bytes 135200 | tf_op jit(solution)/shard_map/ppermute | solution.py:53
  11.1 5.9 %collective-permute-start.2 = (bf16[528,128]{1,0:T(8,128)(2,1)S(1)}, bf16[528,128]{1,0:T(8,128)(2,1)S(1)}, u32[]{:S(2)}, u32[]{:S(2)}) collective-permute-start(bf16[528,128]{1,0:T(8,128)(2,1)S(1)} %get-tuple-element.43), channel_id=1, source_target_pairs={{0,8},{4,12},{8,0},{12,4},{16,24},{20,28},{24,16},{28,20},{1,9},{5... | collective-permute-start | bytes 405512 | tf_op jit(solution)/shard_map/ppermute | solution.py:53
  16.9 0.7 %collective-permute-start.3 = (bf16[528,128]{1,0:T(8,128)(2,1)S(1)}, bf16[528,128]{1,0:T(8,128)(2,1)S(1)}, u32[]{:S(2)}, u32[]{:S(2)}) collective-permute-start(bf16[528,128]{1,0:T(8,128)(2,1)S(1)} %get-tuple-element.43), channel_id=1, source_target_pairs={{0,0},{4,4},{8,16},{12,20},{16,8},{20,12},{24,24},{28,28},{1,1},{5... | collective-permute-start | bytes 405512 | tf_op jit(solution)/shard_map/ppermute | solution.py:53
  17.6 2.0 %shard_map.111 = (bf16[1024,256]{1,0:T(8,128)(2,1)S(1)}, f32[256,512]{1,0:T(8,128)S(1)}, f32[256,512]{1,0:T(8,128)S(1)}) custom-call(bf16[256,512]{1,0:T(8,128)(2,1)S(1)} %get-tuple-element.35.query_ref, bf16[256,512]{1,0:T(8,128)(2,1)S(1)} %get-tuple-element.36.key_ref, bf16[256,512]{1,0:T(8,128)(2,1)S(1)} %get-tuple-element.37.value_ref, ...), custom_call_target="tpu_custom_call" | custom-call | flops 671088640 | bytes 6291456 | tf_op jit(solution)/shard_map/pallas_call | solution.py:273
  19.6 0.3 collective-permute-done.2.even_ref
  19.9 1.3 %shard_map.113 = (bf16[512,128]{1,0:T(8,128)(2,1)S(1)}, bf16[128,512]{1,0:T(8,128)(2,1)S(1)}, bf16[128,512]{1,0:T(8,128)(2,1)S(1)}, bf16[256,512]{1,0:T(8,128)(2...) custom-call(s32[1,1]{1,0:T(1,128)S(6)} %copy.12.doc_ref, ...), custom_call_target="tpu_custom_call" | custom-call | flops 67108864 | bytes 4194304 | tf_op jit(solution)/shard_map/pallas_call | solution.py:280
  21.2 1.0 %collective-permute-start.4 = (bf16[528,128]{1,0:T(8,128)(2,1)S(1)}, bf16[528,128]{1,0:T(8,128)(2,1)S(1)}, u32[]{:S(2)}, u32[]{:S(2)}) collective-permute-start(bf16[528,128]{1,0:T(8,128)(2,1)S(1)} %get-tuple-element.46.refs_2_), channel_id=1, source_target_pairs={{0,4},{4,0},{8,12},{12,8},{16,20},{20,16},{24,28},{28,24},{1,5},{5... | collective-permute-start | bytes 405512 | tf_op jit(solution)/shard_map/ppermute | solution.py:53
  22.2 0.7 %collective-permute-start.5 = (bf16[528,128]{1,0:T(8,128)(2,1)S(1)}, bf16[528,128]{1,0:T(8,128)(2,1)S(1)}, u32[]{:S(2)}, u32[]{:S(2)}) collective-permute-start(bf16[528,128]{1,0:T(8,128)(2,1)S(1)} %get-tuple-element.46.refs_2_), channel_id=1, source_target_pairs={{0,0},{4,8},{8,4},{12,16},{16,12},{20,24},{24,20},{28,28},{1,1},{5... | collective-permute-start | bytes 405512 | tf_op jit(solution)/shard_map/ppermute | solution.py:53
  22.9 0.2 collective-permute-start.7
  23.1 3.2 %collective-permute-done.4.refs_0_ = bf16[528,128]{1,0:T(8,128)(2,1)S(1)} collective-permute-done((bf16[528,128]{1,0:T(8,128)(2,1)S(1)}, bf16[528,128]{1,0:T(8,128)(2,1)S(1)}, u32[]{:S(2)}, u32[]{:S(2)}) %collective-permute-start.4) | collective-permute-done | bytes 135200 | tf_op jit(solution)/shard_map/ppermute | solution.py:53
  26.3 8.6 %collective-permute-start.6 = (bf16[528,128]{1,0:T(8,128)(2,1)S(1)}, bf16[528,128]{1,0:T(8,128)(2,1)S(1)}, u32[]{:S(2)}, u32[]{:S(2)}) collective-permute-start(bf16[528,128]{1,0:T(8,128)(2,1)S(1)} %get-tuple-element.47.refs_0_), channel_id=1, source_target_pairs={{0,8},{4,12},{8,0},{12,4},{16,24},{20,28},{24,16},{28,20},{1,9},{5... | collective-permute-start | bytes 405512 | tf_op jit(solution)/shard_map/ppermute | solution.py:53
  34.9 0.7 %collective-permute-start.8 = (bf16[528,128]{1,0:T(8,128)(2,1)S(1)}, bf16[528,128]{1,0:T(8,128)(2,1)S(1)}, u32[]{:S(2)}, u32[]{:S(2)}) collective-permute-start(bf16[528,128]{1,0:T(8,128)(2,1)S(1)} %get-tuple-element.47.refs_0_), channel_id=1, source_target_pairs={{0,0},{4,4},{8,16},{12,20},{16,8},{20,12},{24,24},{28,28},{1,1},{5... | collective-permute-start | bytes 405512 | tf_op jit(solution)/shard_map/ppermute | solution.py:53
  35.6 2.7 %collective-permute-start.10 = (f32[4,128]{1,0:T(4,128)S(1)}, f32[4,128]{1,0:T(4,128)S(1)}, u32[]{:S(2)}, u32[]{:S(2)}) collective-permute-start(f32[4,128]{1,0:T(4,128)S(1)} %get-tuple-element.57), channel_id=1, source_target_pairs={{0,24},{4,28},{8,16},{12,20},{16,8},{20,12},{24,0},{28,4},{1,25},{... | collective-permute-start | bytes 6152 | tf_op jit(solution)/shard_map/ppermute | solution.py:58
  38.3 3.3 %collective-permute-start.9 = (f32[4,128]{1,0:T(4,128)S(1)}, f32[4,128]{1,0:T(4,128)S(1)}, u32[]{:S(2)}, u32[]{:S(2)}) collective-permute-start(f32[4,128]{1,0:T(4,128)S(1)} %get-tuple-element.57), channel_id=1, source_target_pairs={{0,16},{4,20},{8,24},{12,28},{16,0},{20,4},{24,8},{28,12},{1,17},{... | collective-permute-start | bytes 6152 | tf_op jit(solution)/shard_map/ppermute | solution.py:58
  41.6 1.9 %shard_map.115 = (bf16[256,512]{1,0:T(8,128)(2,1)}, f32[256,512]{1,0:T(8,128)S(1)}, f32[256,512]{1,0:T(8,128)S(1)}) custom-call(bf16[256,512]{1,0:T(8,128)(2,1)S(1)} %get-tuple-element.35.query_ref, bf16[256,512]{1,0:T(8,128)(2,1)S(1)} %get-tuple-element.36.key_ref, bf16[256,512]{1,0:T(8,128)(2,1)S(1)} %get-tuple-element.37.value_ref, ...), custom_call_target="tpu_custom_call" | custom-call | flops 301989888 | bytes 4194304 | tf_op jit(solution)/shard_map/pallas_call | solution.py:289
  43.6 1.1 %shard_map.116 = (bf16[256,512]{1,0:T(8,128)(2,1)}, bf16[256,512]{1,0:T(8,128)(2,1)}, f32[4,128]{1,0:T(4,128)S(1)}) custom-call(s32[1,1]{1,0:T(1,128)S(6)} %copy.12.doc_ref, bf16[256,512]{1,0:T(8,128)(2,1)S(1)} %get-tuple-element.36.key_ref, bf16[256,512]{1,0:T(8,128)(2,1)S(1)} %get-tuple-element.37.value_ref, ...), custom_call_target="tpu_custom_call" | custom-call | flops 67108864 | bytes 3145728 | tf_op jit(solution)/shard_map/pallas_call | solution.py:299
  44.7 0.5 %collective-permute-start.13 = (f32[4,128]{1,0:T(4,128)S(1)}, f32[4,128]{1,0:T(4,128)S(1)}, u32[]{:S(2)}, u32[]{:S(2)}) collective-permute-start(f32[4,128]{1,0:T(4,128)S(1)} %get-tuple-element.64), channel_id=1, source_target_pairs={{0,1},{1,0},{2,3},{3,2},{4,5},{5,4},{6,7},{7,6},{8,9},{9,8},{10,11... | collective-permute-start | bytes 6152 | tf_op jit(solution)/shard_map/ppermute | solution.py:58
  45.2 2.1 %collective-permute-done.13 = f32[4,128]{1,0:T(4,128)S(1)} collective-permute-done((f32[4,128]{1,0:T(4,128)S(1)}, f32[4,128]{1,0:T(4,128)S(1)}, u32[]{:S(2)}, u32[]{:S(2)}) %collective-permute-start.13) | collective-permute-done | bytes 2080 | tf_op jit(solution)/shard_map/ppermute | solution.py:58
  47.3 0.6 %add_multiply_fusion = f32[4,128]{1,0:T(4,128)} fusion(f32[4,128]{1,0:T(4,128)S(1)} %get-tuple-element.64, f32[4,128]{1,0:T(4,128)S(1)} %collective-permute-done.13), kind=kLoop, calls=%fused_computation | loop fusion | flops 1024 | bytes 6144 | tf_op jit(solution)/shard_map/div | solution.py:309
  47.9 1.5 %shard_map.117 = bf16[128,2048]{1,0:T(8,128)(2,1)} custom-call(bf16[128,512]{1,0:T(8,128)(2,1)S(1)} %get-tuple-element.44.keep_ref, bf16[128,512]{1,0:T(8,128)(2,1)S(1)} %collective-permute-done.7.got_ref, bf16[512,2048]{1,0:T(8,128)(2,1)S(1)} %copy-done, bf16[256,2048]{1,0:T(8,128)(2,1)S(1)} %collective-permute-done.11.mine_ref, ...), custom_call_target="tpu_custom_call" | custom-call | flops 536870912 | bytes 6291456 | tf_op jit(solution)/shard_map/pallas_call | solution.py:311
  (17 shorter events, 0.2 us)
Async XLA Ops:
  0.6 17.0 %copy-start = (bf16[512,2048]{1,0:T(8,128)(2,1)S(1)}, bf16[512,2048]{1,0:T(8,128)(2,1)}, u32[]{:S(2)}) copy-start(bf16[512,2048]{1,0:T(8,128)(2,1)} %own_ref.1) | copy-start | bytes 6291460
  2.9 41.8 %collective-permute-start.11 = (bf16[256,2048]{1,0:T(8,128)(2,1)S(1)}, bf16[256,2048]{1,0:T(8,128)(2,1)S(1)}, u32[]{:S(2)}, u32[]{:S(2)}) collective-permute-start(bf16[256,2048]{1,0:T(8,128)(2,1)S(1)} %get-tuple-element.59), channel_id=1, source_target_pairs={{0,2},{2,0},{1,3},{3,1},{4,6},{6,4},{5,7},{7,5},{8,10},{10,8},{9,1... | collective-permute-start | bytes 3145736 | tf_op jit(solution)/shard_map/ppermute | solution.py:58
  5.9 5.0 %collective-permute-start = (bf16[528,128]{1,0:T(8,128)(2,1)S(1)}, bf16[528,128]{1,0:T(8,128)(2,1)S(1)}, u32[]{:S(2)}, u32[]{:S(2)}) collective-permute-start(bf16[528,128]{1,0:T(8,128)(2,1)S(1)} %get-tuple-element.41.refs_2_), channel_id=1, source_target_pairs={{0,4},{4,0},{8,12},{12,8},{16,20},{20,16},{24,28},{28,24},{1,5},{5... | collective-permute-start | bytes 405512 | tf_op jit(solution)/shard_map/ppermute | solution.py:53
  7.4 3.6 %collective-permute-start.1 = (bf16[528,128]{1,0:T(8,128)(2,1)S(1)}, bf16[528,128]{1,0:T(8,128)(2,1)S(1)}, u32[]{:S(2)}, u32[]{:S(2)}) collective-permute-start(bf16[528,128]{1,0:T(8,128)(2,1)S(1)} %get-tuple-element.41.refs_2_), channel_id=1, source_target_pairs={{0,0},{4,8},{8,4},{12,16},{16,12},{20,24},{24,20},{28,28},{1,1},{5... | collective-permute-start | bytes 405512 | tf_op jit(solution)/shard_map/ppermute | solution.py:53
  11.1 8.9 %copy-start.1 = (f32[4,128]{1,0:T(4,128)S(1)}, f32[4,128]{1,0:T(4,128)}, u32[]{:S(2)}) copy-start(f32[4,128]{1,0:T(4,128)} %gain_ref.1) | copy-start | bytes 6148
  11.1 8.9 %collective-permute-start.2 = (bf16[528,128]{1,0:T(8,128)(2,1)S(1)}, bf16[528,128]{1,0:T(8,128)(2,1)S(1)}, u32[]{:S(2)}, u32[]{:S(2)}) collective-permute-start(bf16[528,128]{1,0:T(8,128)(2,1)S(1)} %get-tuple-element.43), channel_id=1, source_target_pairs={{0,8},{4,12},{8,0},{12,4},{16,24},{20,28},{24,16},{28,20},{1,9},{5... | collective-permute-start | bytes 405512 | tf_op jit(solution)/shard_map/ppermute | solution.py:53
  16.9 3.0 %collective-permute-start.3 = (bf16[528,128]{1,0:T(8,128)(2,1)S(1)}, bf16[528,128]{1,0:T(8,128)(2,1)S(1)}, u32[]{:S(2)}, u32[]{:S(2)}) collective-permute-start(bf16[528,128]{1,0:T(8,128)(2,1)S(1)} %get-tuple-element.43), channel_id=1, source_target_pairs={{0,0},{4,4},{8,16},{12,20},{16,8},{20,12},{24,24},{28,28},{1,1},{5... | collective-permute-start | bytes 405512 | tf_op jit(solution)/shard_map/ppermute | solution.py:53
  21.2 5.0 %collective-permute-start.4 = (bf16[528,128]{1,0:T(8,128)(2,1)S(1)}, bf16[528,128]{1,0:T(8,128)(2,1)S(1)}, u32[]{:S(2)}, u32[]{:S(2)}) collective-permute-start(bf16[528,128]{1,0:T(8,128)(2,1)S(1)} %get-tuple-element.46.refs_2_), channel_id=1, source_target_pairs={{0,4},{4,0},{8,12},{12,8},{16,20},{20,16},{24,28},{28,24},{1,5},{5... | collective-permute-start | bytes 405512 | tf_op jit(solution)/shard_map/ppermute | solution.py:53
  22.2 4.0 %collective-permute-start.5 = (bf16[528,128]{1,0:T(8,128)(2,1)S(1)}, bf16[528,128]{1,0:T(8,128)(2,1)S(1)}, u32[]{:S(2)}, u32[]{:S(2)}) collective-permute-start(bf16[528,128]{1,0:T(8,128)(2,1)S(1)} %get-tuple-element.46.refs_2_), channel_id=1, source_target_pairs={{0,0},{4,8},{8,4},{12,16},{16,12},{20,24},{24,20},{28,28},{1,1},{5... | collective-permute-start | bytes 405512 | tf_op jit(solution)/shard_map/ppermute | solution.py:53
  22.9 15.4 %collective-permute-start.7 = (bf16[128,512]{1,0:T(8,128)(2,1)S(1)}, bf16[128,512]{1,0:T(8,128)(2,1)S(1)}, u32[]{:S(2)}, u32[]{:S(2)}) collective-permute-start(bf16[128,512]{1,0:T(8,128)(2,1)S(1)} %get-tuple-element.48), channel_id=1, source_target_pairs={{0,2},{2,0},{1,3},{3,1},{4,6},{6,4},{5,7},{7,5},{8,10},{10,8},{9,1... | collective-permute-start | bytes 393224 | tf_op jit(solution)/shard_map/ppermute | solution.py:58
  26.3 17.2 %collective-permute-start.6 = (bf16[528,128]{1,0:T(8,128)(2,1)S(1)}, bf16[528,128]{1,0:T(8,128)(2,1)S(1)}, u32[]{:S(2)}, u32[]{:S(2)}) collective-permute-start(bf16[528,128]{1,0:T(8,128)(2,1)S(1)} %get-tuple-element.47.refs_0_), channel_id=1, source_target_pairs={{0,8},{4,12},{8,0},{12,4},{16,24},{20,28},{24,16},{28,20},{1,9},{5... | collective-permute-start | bytes 405512 | tf_op jit(solution)/shard_map/ppermute | solution.py:53
  34.9 8.6 %collective-permute-start.8 = (bf16[528,128]{1,0:T(8,128)(2,1)S(1)}, bf16[528,128]{1,0:T(8,128)(2,1)S(1)}, u32[]{:S(2)}, u32[]{:S(2)}) collective-permute-start(bf16[528,128]{1,0:T(8,128)(2,1)S(1)} %get-tuple-element.47.refs_0_), channel_id=1, source_target_pairs={{0,0},{4,4},{8,16},{12,20},{16,8},{20,12},{24,24},{28,28},{1,1},{5... | collective-permute-start | bytes 405512 | tf_op jit(solution)/shard_map/ppermute | solution.py:53
  35.6 7.9 %collective-permute-start.10 = (f32[4,128]{1,0:T(4,128)S(1)}, f32[4,128]{1,0:T(4,128)S(1)}, u32[]{:S(2)}, u32[]{:S(2)}) collective-permute-start(f32[4,128]{1,0:T(4,128)S(1)} %get-tuple-element.57), channel_id=1, source_target_pairs={{0,24},{4,28},{8,16},{12,20},{16,8},{20,12},{24,0},{28,4},{1,25},{... | collective-permute-start | bytes 6152 | tf_op jit(solution)/shard_map/ppermute | solution.py:58
  38.3 5.2 %collective-permute-start.9 = (f32[4,128]{1,0:T(4,128)S(1)}, f32[4,128]{1,0:T(4,128)S(1)}, u32[]{:S(2)}, u32[]{:S(2)}) collective-permute-start(f32[4,128]{1,0:T(4,128)S(1)} %get-tuple-element.57), channel_id=1, source_target_pairs={{0,16},{4,20},{8,24},{12,28},{16,0},{20,4},{24,8},{28,12},{1,17},{... | collective-permute-start | bytes 6152 | tf_op jit(solution)/shard_map/ppermute | solution.py:58
  44.7 3.2 %collective-permute-start.12 = (bf16[256,2048]{1,0:T(8,128)(2,1)S(1)}, bf16[256,2048]{1,0:T(8,128)(2,1)S(1)}, u32[]{:S(2)}, u32[]{:S(2)}) collective-permute-start(bf16[256,2048]{1,0:T(8,128)(2,1)S(1)} %collective-permute-done.11.mine_ref), channel_id=1, source_target_pairs={{0,1},{1,0},{2,3},{3,2},{4,5},{5,4},{6,7},{7,6},{8,9},{9,8},{10,11... | collective-permute-start | bytes 3145736 | tf_op jit(solution)/shard_map/ppermute | solution.py:58
  44.7 2.7 %collective-permute-start.13 = (f32[4,128]{1,0:T(4,128)S(1)}, f32[4,128]{1,0:T(4,128)S(1)}, u32[]{:S(2)}, u32[]{:S(2)}) collective-permute-start(f32[4,128]{1,0:T(4,128)S(1)} %get-tuple-element.64), channel_id=1, source_target_pairs={{0,1},{1,0},{2,3},{3,2},{4,5},{5,4},{6,7},{7,6},{8,9},{9,8},{10,11... | collective-permute-start | bytes 6152 | tf_op jit(solution)/shard_map/ppermute | solution.py:58

commit v3 on v2

v3 whole, which is shorter than its diff:
```python
import functools
import math

import jax
import jax.numpy as jnp
from jax import lax
from jax.experimental import pallas as pl
from jax.experimental.pallas import tpu as pltpu
from jax.sharding import PartitionSpec as P

EPSILON = 1e-05
F32 = jnp.float32
BF16 = jnp.bfloat16
TAIL = 16
GAIN = 4


def nn(a, b):
    return lax.dot_general(a, b, (((1,), (0,)), ((), ())), preferred_element_type=F32)


def nt(a, b):
    return lax.dot_general(a, b, (((1,), (1,)), ((), ())), preferred_element_type=F32)


def tn(a, b):
    return lax.dot_general(a, b, (((0,), (0,)), ((), ())), preferred_element_type=F32)


def call(body, outs, places, flops, moved, scratch=()):
    space = {"s": pltpu.SMEM, "v": pltpu.VMEM, "h": pltpu.HBM}
    return pl.pallas_call(
        body,
        out_shape=[jax.ShapeDtypeStruct(s, t) for s, t in outs],
        in_specs=[pl.BlockSpec(memory_space=space[p]) for p in places],
        out_specs=[pl.BlockSpec(memory_space=pltpu.VMEM) for _ in outs],
        scratch_shapes=list(scratch),
        cost_estimate=pl.CostEstimate(flops=flops, bytes_accessed=moved, transcendentals=0),
        compiler_params=pltpu.CompilerParams(vmem_limit_bytes=40 << 20),
    )


def pairing(size, pairs):
    partner = {i: (j, False) for a, b in pairs for i, j in ((a, b), (b, a))}
    route = []
    for i in range(size):
        to, same_stretch = partner.get(i, (i, True))
        route += [(2 * i + core, 2 * to + (core ^ same_stretch)) for core in (0, 1)]
    return route


def exchange(block, pairs):
    return lax.ppermute(block, ("seq", "dp"), pairing(lax.axis_size("seq"), pairs))


def blocks(size, distance, odd):
    return [(i, i + distance) for i in range(size - distance) if (i // distance) % 2 == odd]


def swaps(block, distance):
    size = lax.axis_size("seq")
    return [exchange(block, blocks(size, distance, odd)) for odd in (0, 1)]


def flipped(block, distance, cores):
    route = [
        (2 * i + core, 2 * (i ^ distance) + (core ^ cores))
        for i in range(lax.axis_size("seq"))
        for core in (0, 1)
    ]
    return lax.ppermute(block, ("seq", "dp"), route)


def put_tail(msg_ref, number, gain=None):
    rows, dim = msg_ref.shape[0] - TAIL, msg_ref.shape[1]
    high = jnp.zeros((GAIN, dim), F32) if gain is None else gain.astype(BF16).astype(F32)
    low = jnp.zeros((GAIN, dim), F32) if gain is None else gain - high
    low = low.astype(BF16).astype(F32)
    number = jnp.broadcast_to(number, (TAIL - 2 * GAIN, dim))
    msg_ref[rows:, :] = jnp.concatenate([high, low, number], axis=0).astype(BF16)
    return high + low


def sent_gain(msg_ref):
    tail = msg_ref[msg_ref.shape[0] - TAIL :, :].astype(F32)
    return tail[:GAIN, :] + tail[GAIN : 2 * GAIN, :]


def opened(msg):
    msg = msg.astype(F32)
    rows = msg.shape[0] - TAIL
    return msg[:rows, :], msg[rows + 2 * GAIN : rows + 2 * GAIN + 1, :]


def taken(even_ref, odd_ref, number, distance, forward):
    me, size = lax.axis_index("seq"), lax.axis_size("seq")
    upper = lax.rem(lax.div(me, distance), 2)
    from_odd = upper == 0 if forward else upper == 1
    there = me >= distance if forward else me + distance < size
    sums, theirs = opened(jnp.where(from_odd, odd_ref[...], even_ref[...]))
    return jnp.where(theirs == jnp.where(there, number, -1.0), sums, 0.0)


def beside(pair_ref, far_ref, number, forward):
    me, size = lax.axis_index("seq"), lax.axis_size("seq")
    in_pair = lax.rem(me, 2) == (1 if forward else 0)
    there = in_pair | (me >= 3 if forward else me + 3 < size)
    sums, theirs = opened(jnp.where(in_pair, pair_ref[...], far_ref[...]))
    return jnp.where(theirs == jnp.where(there, number, -1.0), sums, 0.0)


def total(refs, number, distance, forward):
    *near, even_ref, odd_ref = refs
    if len(near) == 1:
        first = near[0][...]
    else:
        first = beside(*near, number, forward)
    return first + taken(even_ref, odd_ref, number, distance, forward)


def opening_body(
    heads, dim, doc_ref, query_hbm, key_hbm, value_hbm, w_hbm,
    query_ref, key_ref, value_ref, w_ref, number_ref, sum_ref, msg_ref, sems,
):
    copies = [
        pltpu.make_async_copy(src, dst, sems.at[i])
        for i, (src, dst) in enumerate(
            ((key_hbm, key_ref), (value_hbm, value_ref), (query_hbm, query_ref), (w_hbm, w_ref))
        )
    ]
    for copy in copies:
        copy.start()
    number = jnp.broadcast_to(doc_ref[...].astype(F32) + 1.0, number_ref.shape)
    number_ref[...] = number
    put_tail(msg_ref, number[:1, :])
    copies[0].wait()
    copies[1].wait()
    for h in range(heads):
        cols, rows = slice(h * dim, (h + 1) * dim), slice(h * dim, (h + 1) * dim)
        sums = tn(key_ref[:, cols], value_ref[:, cols])
        sum_ref[rows, :] = sums
        msg_ref[rows, :] = sums.astype(BF16)
    copies[2].wait()
    copies[3].wait()


def local_body(
    heads, dim, query_ref, key_ref, value_ref, cot_hbm, w_ref,
    weight_ref, within_ref, normed_grad_ref, cot_ref, sem,
):
    copy = pltpu.make_async_copy(cot_hbm, cot_ref, sem)
    copy.start()
    tokens = query_ref.shape[0]
    causal = lax.broadcasted_iota(jnp.int32, (tokens, tokens), 0) >= lax.broadcasted_iota(
        jnp.int32, (tokens, tokens), 1
    )
    for h in range(heads):
        cols = slice(h * dim, (h + 1) * dim)
        scores = nt(query_ref[:, cols], key_ref[:, cols])
        weights = jnp.where(causal, scores, 0.0).astype(BF16)
        weight_ref[h * tokens : (h + 1) * tokens, :] = weights
        within_ref[:, cols] = nn(weights, value_ref[:, cols])
    copy.wait()
    normed_grad_ref[...] = nt(cot_ref[...], w_ref[...])


def merge_gain(gains, own_ref, other_ref):
    return sent_gain(own_ref) + sent_gain(other_ref) if gains else None


def pair_body(forward, gains, number_ref, sum_ref, own_ref, pair_ref, msg_ref):
    rows = sum_ref.shape[0]
    number = number_ref[:1, :]
    leads = lax.rem(lax.axis_index("seq"), 2) == (1 if forward else 0)
    sums, theirs = opened(pair_ref[...])
    mine = sum_ref[...]
    same = theirs == number
    keep_mine, keep_theirs = same | leads, same | jnp.logical_not(leads)
    msg_ref[:rows, :] = (jnp.where(keep_mine, mine, 0.0) + jnp.where(keep_theirs, sums, 0.0)).astype(BF16)
    put_tail(msg_ref, jnp.where(leads, number, theirs), merge_gain(gains, own_ref, pair_ref))


def merge_body(distance, forward, gains, number_ref, sum_ref, own_ref, *refs):
    *term_ref, even_ref, odd_ref, out_ref, msg_ref = refs
    rows = sum_ref.shape[0]
    number = number_ref[:1, :]
    term = taken(even_ref, odd_ref, number, distance, forward)
    if term_ref:
        term = term + term_ref[0][...]
    out_ref[...] = term
    msg_ref[:rows, :] = (sum_ref[...] + term).astype(BF16)
    put_tail(msg_ref, number, merge_gain(gains, own_ref, even_ref))


def gain_body(own_ref, other_ref, out_ref):
    out_ref[...] = merge_gain(True, own_ref, other_ref)


def forward_body(
    heads, dim, distance, number_ref, query_ref, within_ref, normed_grad_ref, gain_ref, w_ref, *refs
):
    *sum_refs, state_ref, keep_ref, send_ref, grad_ref, outer_ref, msg_ref, gain_grad_ref, normed_ref = refs
    half = keep_ref.shape[0]
    number = number_ref[:1, :]
    state_ref[...] = total(sum_refs, number, distance, True).astype(BF16)
    for h in range(heads):
        cols, rows = slice(h * dim, (h + 1) * dim), slice(h * dim, (h + 1) * dim)
        query = query_ref[:, cols]
        attended = within_ref[:, cols] + nn(query, state_ref[rows, :])
        inv_rms = lax.rsqrt(jnp.mean(attended * attended, axis=-1, keepdims=True) + EPSILON)
        unit = attended * inv_rms
        gain = gain_ref[h : h + 1, :]
        normed_ref[:, cols] = (unit * gain).astype(BF16)
        normed_grad = normed_grad_ref[:, cols]
        gain_grad_ref[h : h + 1, :] = jnp.sum(normed_grad * unit, axis=0, keepdims=True)
        scaled = normed_grad * gain
        grad = inv_rms * (scaled - unit * jnp.mean(scaled * unit, axis=-1, keepdims=True))
        grad = grad.astype(BF16)
        grad_ref[:, cols] = grad
        outer = tn(query, grad)
        outer_ref[rows, :] = outer
        msg_ref[rows, :] = outer.astype(BF16)
    put_tail(msg_ref, number, gain_grad_ref[...])
    head = lax.axis_index("head")
    keep_ref[...] = normed_ref[pl.ds(pl.multiple_of(head * half, half), half), :]
    send_ref[...] = nn(
        normed_ref[pl.ds(pl.multiple_of((1 - head) * half, half), half), :], w_ref[...]
    ).astype(BF16)


def backward_body(
    heads, dim, query_ref, key_ref, value_ref, weight_ref, grad_ref, state_ref,
    query_grad_ref, key_part_ref, value_part_ref,
):
    tokens = query_ref.shape[0]
    causal = lax.broadcasted_iota(jnp.int32, (tokens, tokens), 0) >= lax.broadcasted_iota(
        jnp.int32, (tokens, tokens), 1
    )
    for h in range(heads):
        cols, rows = slice(h * dim, (h + 1) * dim), slice(h * dim, (h + 1) * dim)
        grad = grad_ref[:, cols]
        grad_scores = nt(grad, value_ref[:, cols])
        grad_weights = jnp.where(causal, grad_scores, 0.0).astype(BF16)
        query_grad_ref[:, cols] = (
            nn(grad_weights, key_ref[:, cols]) + nt(grad, state_ref[rows, :])
        ).astype(BF16)
        key_part_ref[:, cols] = tn(grad_weights, query_ref[:, cols])
        value_part_ref[:, cols] = tn(weight_ref[h * tokens : (h + 1) * tokens, :], grad)


def last_body(
    heads, dim, distance, number_ref, key_ref, value_ref, key_part_ref, value_part_ref, *refs
):
    *sum_refs, key_grad_ref, value_grad_ref = refs
    state = total(sum_refs, number_ref[:1, :], distance, False).astype(BF16)
    for h in range(heads):
        cols, rows = slice(h * dim, (h + 1) * dim), slice(h * dim, (h + 1) * dim)
        key_grad_ref[:, cols] = (
            key_part_ref[:, cols] + nt(value_ref[:, cols], state[rows, :])
        ).astype(BF16)
        value_grad_ref[:, cols] = (
            value_part_ref[:, cols] + nn(key_ref[:, cols], state[rows, :])
        ).astype(BF16)


def layer_body(scale, keep_ref, w_ref, got_ref, *refs):
    *gain_refs, out_ref, gain_grad_ref = refs
    out_ref[...] = (nn(keep_ref[...], w_ref[...]) + got_ref[...].astype(F32)).astype(BF16)
    parts = [ref[...] for ref in gain_refs]
    if len(parts) == 4:
        parts = [(parts[0] + parts[1]) + (parts[2] + parts[3])]
    gain_grad_ref[...] = parts[0] * scale


def on_device(queries, key_rows, value_rows, stretch_doc, head_gain, w_out, cotangent):
    tokens, width = queries.shape[1:]
    heads, dim = head_gain.shape
    model = w_out.shape[1]
    size = lax.axis_size("seq")
    matrix = 2 * tokens * dim * dim * heads
    square = 2 * tokens * tokens * dim * heads
    layer = tokens * width * model
    rows, summed, message = (tokens, width), (heads * dim, dim), (heads * dim + TAIL, dim)
    small, half = (heads, dim), (tokens // 2, model)
    distances = [1]
    while 2 * distances[-1] - 1 < size // 2 - 1:
        distances.append(2 * distances[-1])
    last = distances[-1]
    gains = size & (size - 1) == 0 and len(distances) > 1

    def spread(outer, msg, forward):
        carry = gains and not forward
        if last == 2:
            pair = exchange(msg, blocks(size, 1, 0))
            far = exchange(msg, [(i, i + 3) for i in range(1, size - 3, 2)])
            (msg,) = call(
                functools.partial(pair_body, forward, carry), [(message, BF16)], "vvvv", flops=0, moved=1 << 20
            )(number, outer, msg, pair)
            return [pair, far, *swaps(msg, last)], msg
        terms = []
        for distance in distances[:-1]:
            even, odd = swaps(msg, distance)
            *terms, msg = call(
                functools.partial(merge_body, distance, forward, carry), [(summed, F32), (message, BF16)],
                "vvvvv" + "v" * len(terms), flops=0, moved=1 << 20,
            )(number, outer, msg, *terms, even, odd)
        return [*terms, *swaps(msg, last)], msg

    in_hbm = lambda block: pltpu.with_memory_space_constraint(block, pltpu.HBM)
    query, key, value, w, number, outer, msg = call(
        functools.partial(opening_body, heads, dim),
        [(rows, BF16)] * 3 + [((width, model), BF16), ((8, dim), F32), (summed, F32), (message, BF16)],
        "vhhhh", flops=matrix, moved=4 << 20, scratch=[pltpu.SemaphoreType.DMA((4,))],
    )(stretch_doc, *map(in_hbm, (queries[0], key_rows[0], value_rows[0], w_out)))
    weights, within, normed_grad = call(
        functools.partial(local_body, heads, dim),
        [((heads * tokens, tokens), BF16), (rows, F32), (rows, F32)],
        "vvvhv", flops=2 * square + 2 * layer, moved=6 << 20,
        scratch=[pltpu.VMEM((tokens, model), BF16), pltpu.SemaphoreType.DMA],
    )(query, key, value, in_hbm(cotangent[0]), w)
    sums, _ = spread(outer, msg, True)
    state, keep, send, grad, outer, msg, gain_part = call(
        functools.partial(forward_body, heads, dim, last),
        [
            (summed, BF16), ((tokens // 2, width), BF16), (half, BF16),
            (rows, BF16), (summed, F32), (message, BF16), (small, F32),
        ],
        "vvvvvv" + "v" * len(sums), flops=2 * matrix + layer, moved=4 << 20, scratch=[pltpu.VMEM(rows, BF16)],
    )(number, query, within, normed_grad, head_gain, w, *sums)
    got = lax.ppermute(send, "head", [(0, 1), (1, 0)])
    query_grad, key_part, value_part = call(
        functools.partial(backward_body, heads, dim),
        [(rows, BF16), (rows, F32), (rows, F32)],
        "vvvvvv", flops=4 * square + matrix, moved=4 << 20,
    )(query, key, value, weights, grad, state)
    sums, msg = spread(outer, msg, False)
    if gains:
        (gain,) = call(gain_body, [(small, F32)], "vv", flops=0, moved=1 << 16)(msg, sums[-2])
        across = [flipped(gain, *to) for to in ((0, 1), (size // 2, 0), (size // 2, 1))]
        gain_parts = [gain, *across]
    else:
        gain_parts = [lax.psum(gain_part, ("seq", "dp"))]
    key_grad, value_grad = call(
        functools.partial(last_body, heads, dim, last), [(rows, BF16), (rows, BF16)],
        "vvvvv" + "v" * len(sums), flops=2 * matrix, moved=3 << 20,
    )(number, key, value, key_part, value_part, *sums)
    scale = 1.0 / math.sqrt(size * lax.axis_size("dp") * tokens)
    layer_out, gain_grad = call(
        functools.partial(layer_body, scale), [(half, BF16), (small, F32)],
        "vvv" + "v" * len(gain_parts), flops=layer, moved=6 << 20,
    )(keep, w, got, *gain_parts)
    return layer_out[None], query_grad[None], key_grad[None], value_grad[None], gain_grad


def solution(mesh):
    rows = P("dp", "seq", "head")
    return jax.shard_map(
        on_device,
        mesh=mesh,
        in_specs=(rows, rows, rows, P("dp", "seq"), P("head", None), P("head", None), P("dp", "seq", None)),
        out_specs=(P("dp", ("seq", "head"), None), rows, rows, rows, P("head", None)),
        check_vma=False,
    )
```

time: 49.7 us -> 40 us (0.80)
  starting transfers between devices: 29.3 us -> 13.9 us
  waiting for transfers between devices: 8.56 us -> 14.8 us
  other arithmetic: 0.58 us -> 0 us
    ppermute x14 -> x12, starting transfers between devices: 29.3 us -> 13.9 us  [the longest x8 9.65 us: exchange(): lax.ppermute(block, ('seq', 'dp'), pairing(lax.axis_size('seq'), pairs))]
    ppermute x14 -> x12, waiting for transfers between devices: 8.56 us -> 14.8 us  [the longest x8 12.4 us: exchange(): lax.ppermute(block, ('seq', 'dp'), pairing(lax.axis_size('seq'), pairs))]
    div x1 -> x0, other arithmetic: 0.58 us -> none  [on_device(): gain_grad = gain_sum / math.sqrt(size * lax.axis_size('dp') * tokens)]
    pallas_call x4 -> x5, Pallas kernels: 2.76 us -> 2.48 us  [the longest x1 1.25 us: on_device(): call(functools.partial(layer_body, scale), [(half, BF16), (small, F32)],...]
  transfers between devices with their start and end apart: 14 -> 12, of which waited for: 4 -> 6; matrix products, arithmetic and copies ran while one was open for 1% -> 0% of each run, Pallas kernels for 13% -> 13%
where the time goes in v3:
time: 40 us; the launch traced here: 39.8 us
  waiting for transfers between devices  14.8 us (37%)
  starting transfers between devices  13.9 us (35%)
  Pallas kernels  9.61 us (24%)
  between operations  1.35 us (3%)
    ppermute x8, waiting for transfers between devices, exchange(): lax.ppermute(block, ('seq', 'dp'), pairing(lax.axis_size('seq'), pairs))  12.4 us
    ppermute x8, starting transfers between devices, exchange(): lax.ppermute(block, ('seq', 'dp'), pairing(lax.axis_size('seq'), pairs))  9.65 us
    ppermute x3, starting transfers between devices, flipped(): return lax.ppermute(block, ('seq', 'dp'), route)  2.76 us
    ppermute x3, waiting for transfers between devices, flipped(): return lax.ppermute(block, ('seq', 'dp'), route)  2.47 us
    pallas_call x1, Pallas kernels, on_device(): call(functools.partial(local_body, heads, dim), [((heads * tokens, tokens...  1.98 us
    pallas_call x1, Pallas kernels, on_device(): call(functools.partial(backward_body, heads, dim), [(rows, BF16), (rows,...  1.92 us
    pallas_call x1, Pallas kernels, on_device(): call(functools.partial(opening_body, heads, dim), [(rows, BF16)] * 3 + [(...  1.89 us
    ppermute x1, starting transfers between devices, on_device(): got = lax.ppermute(send, 'head', [(0, 1), (1, 0)])  1.55 us
  transfers between devices with their start and end apart: 12, of which 6 were waited for; matrix products, arithmetic and copies ran while one was open for 0% of the time, Pallas kernels for 13%

profile of v3, /device:TPU:0, one launch (start us, length us, event | category | flops | bytes accessed | tf_op | source)
XLA Modules:
  0.0 39.8 jit_solution(4776188373603091217)
XLA Ops:
  1.3 1.9 %shard_map.110 = (bf16[256,512]{1,0:T(8,128)(2,1)S(1)}, bf16[256,512]{1,0:T(8,128)(2,1)S(1)}, bf16[256,512]{1,0:T(8,128)(2,1)S(1)}, bf16[512,2048]{1,0:T(8,128)(...) custom-call(s32[1,1]{1,0:T(1,128)S(6)} %copy.12.doc_ref, ...), custom_call_target="tpu_custom_call" | custom-call | flops 33554432 | bytes 4194304 | tf_op jit(solution)/shard_map/pallas_call | solution.py:310
  3.2 3.0 %collective-permute-start = (bf16[528,128]{1,0:T(8,128)(2,1)S(1)}, bf16[528,128]{1,0:T(8,128)(2,1)S(1)}, u32[]{:S(2)}, u32[]{:S(2)}) collective-permute-start(bf16[528,128]{1,0:T(8,128)(2,1)S(1)} %get-tuple-element.35.own_ref), channel_id=1, source_target_pairs={{0,4},{1,5},{4,0},{5,1},{8,12},{9,13},{12,8},{13,9},{16,20},{17,21... | collective-permute-start | bytes 405512 | tf_op jit(solution)/shard_map/ppermute | solution.py:53
  6.2 4.0 %collective-permute-done.pair_ref.refs_0_ = bf16[528,128]{1,0:T(8,128)(2,1)S(1)} collective-permute-done((bf16[528,128]{1,0:T(8,128)(2,1)S(1)}, bf16[528,128]{1,0:T(8,128)(2,1)S(1)}, u32[]{:S(2)}, u32[]{:S(2)}) %collective-permute-start) | collective-permute-done | bytes 135200 | tf_op jit(solution)/shard_map/ppermute | solution.py:53
  10.2 0.1 shard_map.112
  10.2 0.0 copy-start
  10.2 0.1 collective-permute-start.3
  10.3 3.4 %collective-permute-start.2 = (bf16[528,128]{1,0:T(8,128)(2,1)S(1)}, bf16[528,128]{1,0:T(8,128)(2,1)S(1)}, u32[]{:S(2)}, u32[]{:S(2)}) collective-permute-start(bf16[528,128]{1,0:T(8,128)(2,1)S(1)} %shard_map.112), channel_id=1, source_target_pairs={{0,8},{1,9},{4,12},{5,13},{8,0},{9,1},{12,4},{13,5},{16,24},{17,25... | collective-permute-start | bytes 405512 | tf_op jit(solution)/shard_map/ppermute | solution.py:53
  13.7 2.0 %shard_map.111 = (bf16[1024,256]{1,0:T(8,128)(2,1)S(1)}, f32[256,512]{1,0:T(8,128)S(1)}, f32[256,512]{1,0:T(8,128)S(1)}) custom-call(bf16[256,512]{1,0:T(8,128)(2,1)S(1)} %get-tuple-element.29.query_ref, bf16[256,512]{1,0:T(8,128)(2,1)S(1)} %get-tuple-element.30.key_ref, bf16[256,512]{1,0:T(8,128)(2,1)S(1)} %get-tuple-element.31.value_ref, ...), custom_call_target="tpu_custom_call" | custom-call | flops 671088640 | bytes 6291456 | tf_op jit(solution)/shard_map/pallas_call | solution.py:315
  15.7 2.1 %collective-permute-done.2.refs_2_ = bf16[528,128]{1,0:T(8,128)(2,1)S(1)} collective-permute-done((bf16[528,128]{1,0:T(8,128)(2,1)S(1)}, bf16[528,128]{1,0:T(8,128)(2,1)S(1)}, u32[]{:S(2)}, u32[]{:S(2)}) %collective-permute-start.2) | collective-permute-done | bytes 135200 | tf_op jit(solution)/shard_map/ppermute | solution.py:53
  17.9 1.4 %shard_map.113 = (bf16[512,128]{1,0:T(8,128)(2,1)S(1)}, bf16[128,512]{1,0:T(8,128)(2,1)S(1)}, bf16[128,2048]{1,0:T(8,128)(2,1)S(1)}, bf16[256,512]{1,0:T(8,128)(...) custom-call(f32[8,128]{1,0:T(8,128)S(1)} %get-tuple-element.28.number_ref, ...), custom_call_target="tpu_custom_call" | custom-call | flops 335544320 | bytes 4194304 | tf_op jit(solution)/shard_map/pallas_call | solution.py:322
  19.2 1.5 %collective-permute-start.4 = (bf16[128,2048]{1,0:T(8,128)(2,1)S(1)}, bf16[128,2048]{1,0:T(8,128)(2,1)S(1)}, u32[]{:S(2)}, u32[]{:S(2)}) collective-permute-start(bf16[128,2048]{1,0:T(8,128)(2,1)S(1)} %get-tuple-element.38), channel_id=1, source_target_pairs={{0,2},{2,0},{1,3},{3,1},{4,6},{6,4},{5,7},{7,5},{8,10},{10,8},{9,1... | collective-permute-start | bytes 1572872 | tf_op jit(solution)/shard_map/ppermute | solution.py:330
  20.8 1.3 %collective-permute-start.5 = (bf16[528,128]{1,0:T(8,128)(2,1)S(1)}, bf16[528,128]{1,0:T(8,128)(2,1)S(1)}, u32[]{:S(2)}, u32[]{:S(2)}) collective-permute-start(bf16[528,128]{1,0:T(8,128)(2,1)S(1)} %get-tuple-element.40.own_ref), channel_id=1, source_target_pairs={{0,4},{1,5},{4,0},{5,1},{8,12},{9,13},{12,8},{13,9},{16,20},{17,21... | collective-permute-start | bytes 405512 | tf_op jit(solution)/shard_map/ppermute | solution.py:53
  22.1 3.7 %collective-permute-done.5.pair_ref.refs_0_ = bf16[528,128]{1,0:T(8,128)(2,1)S(1)} collective-permute-done((bf16[528,128]{1,0:T(8,128)(2,1)S(1)}, bf16[528,128]{1,0:T(8,128)(2,1)S(1)}, u32[]{:S(2)}, u32[]{:S(2)}) %collective-permute-start.5) | collective-permute-done | bytes 135200 | tf_op jit(solution)/shard_map/ppermute | solution.py:53
  25.8 0.1 shard_map.114.own_ref
  25.8 1.4 %collective-permute-start.6 = (bf16[528,128]{1,0:T(8,128)(2,1)S(1)}, bf16[528,128]{1,0:T(8,128)(2,1)S(1)}, u32[]{:S(2)}, u32[]{:S(2)}) collective-permute-start(bf16[528,128]{1,0:T(8,128)(2,1)S(1)} %shard_map.114.own_ref), channel_id=1, source_target_pairs={{0,8},{1,9},{4,12},{5,13},{8,0},{9,1},{12,4},{13,5},{16,24},{17,25... | collective-permute-start | bytes 405512 | tf_op jit(solution)/shard_map/ppermute | solution.py:53
  27.2 0.5 %collective-permute-start.11 = (bf16[528,128]{1,0:T(8,128)(2,1)S(1)}, bf16[528,128]{1,0:T(8,128)(2,1)S(1)}, u32[]{:S(2)}, u32[]{:S(2)}) collective-permute-start(bf16[528,128]{1,0:T(8,128)(2,1)S(1)} %shard_map.114.own_ref), channel_id=1, source_target_pairs={{0,1},{1,0},{4,5},{5,4},{8,16},{9,17},{12,20},{13,21},{16,8},{17,9... | collective-permute-start | bytes 405512 | tf_op jit(solution)/shard_map/ppermute | solution.py:53
  27.7 1.9 %shard_map.117 = (bf16[256,512]{1,0:T(8,128)(2,1)}, f32[256,512]{1,0:T(8,128)S(1)}, f32[256,512]{1,0:T(8,128)S(1)}) custom-call(bf16[256,512]{1,0:T(8,128)(2,1)S(1)} %get-tuple-element.29.query_ref, bf16[256,512]{1,0:T(8,128)(2,1)S(1)} %get-tuple-element.30.key_ref, bf16[256,512]{1,0:T(8,128)(2,1)S(1)} %get-tuple-element.31.value_ref, ...), custom_call_target="tpu_custom_call" | custom-call | flops 301989888 | bytes 4194304 | tf_op jit(solution)/shard_map/pallas_call | solution.py:331
  29.6 2.5 %collective-permute-done.6.other_ref.refs_2_ = bf16[528,128]{1,0:T(8,128)(2,1)S(1)} collective-permute-done((bf16[528,128]{1,0:T(8,128)(2,1)S(1)}, bf16[528,128]{1,0:T(8,128)(2,1)S(1)}, u32[]{:S(2)}, u32[]{:S(2)}) %collective-permute-start.6) | collective-permute-done | bytes 135200 | tf_op jit(solution)/shard_map/ppermute | solution.py:53
  32.2 2.0 %collective-permute-start.8 = (f32[4,128]{1,0:T(4,128)S(1)}, f32[4,128]{1,0:T(4,128)S(1)}, u32[]{:S(2)}, u32[]{:S(2)}) collective-permute-start(f32[4,128]{1,0:T(4,128)S(1)} %shard_map.115.refs_0_), channel_id=1, source_target_pairs={{0,16},{1,17},{4,20},{5,21},{8,24},{9,25},{12,28},{13,29},{16,0},{... | collective-permute-start | bytes 6152 | tf_op jit(solution)/shard_map/ppermute | solution.py:71
  34.2 0.7 %collective-permute-start.7 = (f32[4,128]{1,0:T(4,128)S(1)}, f32[4,128]{1,0:T(4,128)S(1)}, u32[]{:S(2)}, u32[]{:S(2)}) collective-permute-start(f32[4,128]{1,0:T(4,128)S(1)} %shard_map.115.refs_0_), channel_id=1, source_target_pairs={{0,1},{1,0},{4,5},{5,4},{8,9},{9,8},{12,13},{13,12},{16,17},{17,16... | collective-permute-start | bytes 6152 | tf_op jit(solution)/shard_map/ppermute | solution.py:71
  34.9 1.1 %shard_map.118 = (bf16[256,512]{1,0:T(8,128)(2,1)}, bf16[256,512]{1,0:T(8,128)(2,1)}) custom-call(f32[8,128]{1,0:T(8,128)S(1)} %get-tuple-element.28.number_ref, bf16[256,512]{1,0:T(8,128)(2,1)S(1)} %get-tuple-element.30.key_ref, bf16[256,512]{1,0:T(8,128)(2,1)S(1)} %get-tuple-element.31.value_ref, f32[256,512]{1,0:T(8,128)S(1)} %get-tuple-element.46.key_part_ref, ...), custom_call_target="tpu_custom_call" | custom-call | flops 67108864 | bytes 3145728 | tf_op jit(solution)/shard_map/pallas_call | solution.py:343
  36.0 0.3 collective-permute-done.9.refs_3_
  36.3 2.2 %collective-permute-done.8.refs_2_ = f32[4,128]{1,0:T(4,128)S(1)} collective-permute-done((f32[4,128]{1,0:T(4,128)S(1)}, f32[4,128]{1,0:T(4,128)S(1)}, u32[]{:S(2)}, u32[]{:S(2)}) %collective-permute-start.8) | collective-permute-done | bytes 2080 | tf_op jit(solution)/shard_map/ppermute | solution.py:71
  38.5 1.3 %shard_map.116 = (bf16[128,2048]{1,0:T(8,128)(2,1)}, f32[4,128]{1,0:T(4,128)}) custom-call(bf16[128,512]{1,0:T(8,128)(2,1)S(1)} %get-tuple-element.37.keep_ref, bf16[512,2048]{1,0:T(8,128)(2,1)S(1)} %get-tuple-element.32.w_ref, bf16[128,2048]{1,0:T(8,128)(2,1)S(1)} %collective-permute-done.4.got_ref, f32[4,128]{1,0:T(4,128)S(1)} %shard_map.115.refs_0_, ...), custom_call_target="tpu_custom_call" | custom-call | flops 268435456 | bytes 6291456 | tf_op jit(solution)/shard_map/pallas_call | solution.py:348
  (11 shorter events, 0.0 us)
Async XLA Ops:
  3.2 7.0 %collective-permute-start = (bf16[528,128]{1,0:T(8,128)(2,1)S(1)}, bf16[528,128]{1,0:T(8,128)(2,1)S(1)}, u32[]{:S(2)}, u32[]{:S(2)}) collective-permute-start(bf16[528,128]{1,0:T(8,128)(2,1)S(1)} %get-tuple-element.35.own_ref), channel_id=1, source_target_pairs={{0,4},{1,5},{4,0},{5,1},{8,12},{9,13},{12,8},{13,9},{16,20},{17,21... | collective-permute-start | bytes 405512 | tf_op jit(solution)/shard_map/ppermute | solution.py:53
  6.2 9.5 %collective-permute-start.1 = (bf16[528,128]{1,0:T(8,128)(2,1)S(1)}, bf16[528,128]{1,0:T(8,128)(2,1)S(1)}, u32[]{:S(2)}, u32[]{:S(2)}) collective-permute-start(bf16[528,128]{1,0:T(8,128)(2,1)S(1)} %get-tuple-element.35.own_ref), channel_id=1, source_target_pairs={{0,1},{1,0},{4,16},{5,17},{8,9},{9,8},{12,24},{13,25},{16,4},{17,5... | collective-permute-start | bytes 405512 | tf_op jit(solution)/shard_map/ppermute | solution.py:53
  10.2 7.7 %copy-start = (f32[4,128]{1,0:T(4,128)S(1)}, f32[4,128]{1,0:T(4,128)}, u32[]{:S(2)}) copy-start(f32[4,128]{1,0:T(4,128)} %gain_ref.1) | copy-start | bytes 6148
  10.2 5.5 %collective-permute-start.3 = (bf16[528,128]{1,0:T(8,128)(2,1)S(1)}, bf16[528,128]{1,0:T(8,128)(2,1)S(1)}, u32[]{:S(2)}, u32[]{:S(2)}) collective-permute-start(bf16[528,128]{1,0:T(8,128)(2,1)S(1)} %shard_map.112), channel_id=1, source_target_pairs={{0,1},{1,0},{4,5},{5,4},{8,16},{9,17},{12,20},{13,21},{16,8},{17,9... | collective-permute-start | bytes 405512 | tf_op jit(solution)/shard_map/ppermute | solution.py:53
  10.3 7.6 %collective-permute-start.2 = (bf16[528,128]{1,0:T(8,128)(2,1)S(1)}, bf16[528,128]{1,0:T(8,128)(2,1)S(1)}, u32[]{:S(2)}, u32[]{:S(2)}) collective-permute-start(bf16[528,128]{1,0:T(8,128)(2,1)S(1)} %shard_map.112), channel_id=1, source_target_pairs={{0,8},{1,9},{4,12},{5,13},{8,0},{9,1},{12,4},{13,5},{16,24},{17,25... | collective-permute-start | bytes 405512 | tf_op jit(solution)/shard_map/ppermute | solution.py:53
  19.2 19.3 %collective-permute-start.4 = (bf16[128,2048]{1,0:T(8,128)(2,1)S(1)}, bf16[128,2048]{1,0:T(8,128)(2,1)S(1)}, u32[]{:S(2)}, u32[]{:S(2)}) collective-permute-start(bf16[128,2048]{1,0:T(8,128)(2,1)S(1)} %get-tuple-element.38), channel_id=1, source_target_pairs={{0,2},{2,0},{1,3},{3,1},{4,6},{6,4},{5,7},{7,5},{8,10},{10,8},{9,1... | collective-permute-start | bytes 1572872 | tf_op jit(solution)/shard_map/ppermute | solution.py:330
  20.8 5.0 %collective-permute-start.5 = (bf16[528,128]{1,0:T(8,128)(2,1)S(1)}, bf16[528,128]{1,0:T(8,128)(2,1)S(1)}, u32[]{:S(2)}, u32[]{:S(2)}) collective-permute-start(bf16[528,128]{1,0:T(8,128)(2,1)S(1)} %get-tuple-element.40.own_ref), channel_id=1, source_target_pairs={{0,4},{1,5},{4,0},{5,1},{8,12},{9,13},{12,8},{13,9},{16,20},{17,21... | collective-permute-start | bytes 405512 | tf_op jit(solution)/shard_map/ppermute | solution.py:53
  25.8 6.3 %collective-permute-start.6 = (bf16[528,128]{1,0:T(8,128)(2,1)S(1)}, bf16[528,128]{1,0:T(8,128)(2,1)S(1)}, u32[]{:S(2)}, u32[]{:S(2)}) collective-permute-start(bf16[528,128]{1,0:T(8,128)(2,1)S(1)} %shard_map.114.own_ref), channel_id=1, source_target_pairs={{0,8},{1,9},{4,12},{5,13},{8,0},{9,1},{12,4},{13,5},{16,24},{17,25... | collective-permute-start | bytes 405512 | tf_op jit(solution)/shard_map/ppermute | solution.py:53
  27.2 7.0 %collective-permute-start.10 = (bf16[528,128]{1,0:T(8,128)(2,1)S(1)}, bf16[528,128]{1,0:T(8,128)(2,1)S(1)}, u32[]{:S(2)}, u32[]{:S(2)}) collective-permute-start(bf16[528,128]{1,0:T(8,128)(2,1)S(1)} %get-tuple-element.40.own_ref), channel_id=1, source_target_pairs={{0,1},{1,0},{4,16},{5,17},{8,9},{9,8},{12,24},{13,25},{16,4},{17,5... | collective-permute-start | bytes 405512 | tf_op jit(solution)/shard_map/ppermute | solution.py:53
  27.2 7.7 %collective-permute-start.11 = (bf16[528,128]{1,0:T(8,128)(2,1)S(1)}, bf16[528,128]{1,0:T(8,128)(2,1)S(1)}, u32[]{:S(2)}, u32[]{:S(2)}) collective-permute-start(bf16[528,128]{1,0:T(8,128)(2,1)S(1)} %shard_map.114.own_ref), channel_id=1, source_target_pairs={{0,1},{1,0},{4,5},{5,4},{8,16},{9,17},{12,20},{13,21},{16,8},{17,9... | collective-permute-start | bytes 405512 | tf_op jit(solution)/shard_map/ppermute | solution.py:53
  32.2 4.1 %collective-permute-start.9 = (f32[4,128]{1,0:T(4,128)S(1)}, f32[4,128]{1,0:T(4,128)S(1)}, u32[]{:S(2)}, u32[]{:S(2)}) collective-permute-start(f32[4,128]{1,0:T(4,128)S(1)} %shard_map.115.refs_0_), channel_id=1, source_target_pairs={{0,17},{1,16},{4,21},{5,20},{8,25},{9,24},{12,29},{13,28},{16,1},{... | collective-permute-start | bytes 6152 | tf_op jit(solution)/shard_map/ppermute | solution.py:71
  32.2 6.3 %collective-permute-start.8 = (f32[4,128]{1,0:T(4,128)S(1)}, f32[4,128]{1,0:T(4,128)S(1)}, u32[]{:S(2)}, u32[]{:S(2)}) collective-permute-start(f32[4,128]{1,0:T(4,128)S(1)} %shard_map.115.refs_0_), channel_id=1, source_target_pairs={{0,16},{1,17},{4,20},{5,21},{8,24},{9,25},{12,28},{13,29},{16,0},{... | collective-permute-start | bytes 6152 | tf_op jit(solution)/shard_map/ppermute | solution.py:71
  34.2 4.3 %collective-permute-start.7 = (f32[4,128]{1,0:T(4,128)S(1)}, f32[4,128]{1,0:T(4,128)S(1)}, u32[]{:S(2)}, u32[]{:S(2)}) collective-permute-start(f32[4,128]{1,0:T(4,128)S(1)} %shard_map.115.refs_0_), channel_id=1, source_target_pairs={{0,1},{1,0},{4,5},{5,4},{8,9},{9,8},{12,13},{13,12},{16,17},{17,16... | collective-permute-start | bytes 6152 | tf_op jit(solution)/shard_map/ppermute | solution.py:71

commit v4 on v3

--- a/solution.py
+++ b/solution.py
@@ -28,7 +28,7 @@
 
 
 def call(body, outs, places, flops, moved, scratch=()):
-    space = {"s": pltpu.SMEM, "v": pltpu.VMEM, "h": pltpu.HBM}
+    space = {"a": pl.ANY, "v": pltpu.VMEM, "h": pltpu.HBM}
     return pl.pallas_call(
         body,
         out_shape=[jax.ShapeDtypeStruct(s, t) for s, t in outs],
@@ -119,18 +119,17 @@
 
 
 def opening_body(
-    heads, dim, doc_ref, query_hbm, key_hbm, value_hbm, w_hbm,
-    query_ref, key_ref, value_ref, w_ref, number_ref, sum_ref, msg_ref, sems,
+    heads, dim, doc_any, key_hbm, value_hbm,
+    key_ref, value_ref, number_ref, sum_ref, msg_ref, doc_ref, sems,
 ):
     copies = [
         pltpu.make_async_copy(src, dst, sems.at[i])
-        for i, (src, dst) in enumerate(
-            ((key_hbm, key_ref), (value_hbm, value_ref), (query_hbm, query_ref), (w_hbm, w_ref))
-        )
+        for i, (src, dst) in enumerate(((key_hbm, key_ref), (value_hbm, value_ref), (doc_any, doc_ref)))
     ]
     for copy in copies:
         copy.start()
-    number = jnp.broadcast_to(doc_ref[...].astype(F32) + 1.0, number_ref.shape)
+    copies[2].wait()
+    number = jnp.full(number_ref.shape, doc_ref[0, 0] + 1, jnp.int32).astype(F32)
     number_ref[...] = number
     put_tail(msg_ref, number[:1, :])
     copies[0].wait()
@@ -140,27 +139,31 @@
         sums = tn(key_ref[:, cols], value_ref[:, cols])
         sum_ref[rows, :] = sums
         msg_ref[rows, :] = sums.astype(BF16)
-    copies[2].wait()
-    copies[3].wait()
 
 
 def local_body(
-    heads, dim, query_ref, key_ref, value_ref, cot_hbm, w_ref,
-    weight_ref, within_ref, normed_grad_ref, cot_ref, sem,
-):
-    copy = pltpu.make_async_copy(cot_hbm, cot_ref, sem)
-    copy.start()
+    heads, dim, query_hbm, key_ref, value_ref, cot_hbm, w_hbm,
+    query_ref, w_ref, weight_ref, within_ref, normed_grad_ref, cot_ref, sems,
+):
+    copies = [
+        pltpu.make_async_copy(src, dst, sems.at[i])
+        for i, (src, dst) in enumerate(((query_hbm, query_ref), (cot_hbm, cot_ref), (w_hbm, w_ref)))
+    ]
+    for copy in copies:
+        copy.start()
     tokens = query_ref.shape[0]
     causal = lax.broadcasted_iota(jnp.int32, (tokens, tokens), 0) >= lax.broadcasted_iota(
         jnp.int32, (tokens, tokens), 1
     )
+    copies[0].wait()
     for h in range(heads):
         cols = slice(h * dim, (h + 1) * dim)
         scores = nt(query_ref[:, cols], key_ref[:, cols])
         weights = jnp.where(causal, scores, 0.0).astype(BF16)
         weight_ref[h * tokens : (h + 1) * tokens, :] = weights
         within_ref[:, cols] = nn(weights, value_ref[:, cols])
-    copy.wait()
+    copies[1].wait()
+    copies[2].wait()
     normed_grad_ref[...] = nt(cot_ref[...], w_ref[...])
 
 
@@ -296,7 +299,9 @@
             (msg,) = call(
                 functools.partial(pair_body, forward, carry), [(message, BF16)], "vvvv", flops=0, moved=1 << 20
             )(number, outer, msg, pair)
-            return [pair, far, *swaps(msg, last)], msg
+            even, odd = swaps(msg, last)
+            even, far = lax.optimization_barrier((even, far))
+            return [pair, far, even, odd], msg
         terms = []
         for distance in distances[:-1]:
             even, odd = swaps(msg, distance)
@@ -307,17 +312,17 @@
         return [*terms, *swaps(msg, last)], msg
 
     in_hbm = lambda block: pltpu.with_memory_space_constraint(block, pltpu.HBM)
-    query, key, value, w, number, outer, msg = call(
+    key, value, number, outer, msg = call(
         functools.partial(opening_body, heads, dim),
-        [(rows, BF16)] * 3 + [((width, model), BF16), ((8, dim), F32), (summed, F32), (message, BF16)],
-        "vhhhh", flops=matrix, moved=4 << 20, scratch=[pltpu.SemaphoreType.DMA((4,))],
-    )(stretch_doc, *map(in_hbm, (queries[0], key_rows[0], value_rows[0], w_out)))
-    weights, within, normed_grad = call(
+        [(rows, BF16)] * 2 + [((8, dim), F32), (summed, F32), (message, BF16)],
+        "ahh", flops=matrix, moved=1 << 20, scratch=[pltpu.SMEM((1, 1), jnp.int32), pltpu.SemaphoreType.DMA((3,))],
+    )(stretch_doc, in_hbm(key_rows[0]), in_hbm(value_rows[0]))
+    query, w, weights, within, normed_grad = call(
         functools.partial(local_body, heads, dim),
-        [((heads * tokens, tokens), BF16), (rows, F32), (rows, F32)],
-        "vvvhv", flops=2 * square + 2 * layer, moved=6 << 20,
-        scratch=[pltpu.VMEM((tokens, model), BF16), pltpu.SemaphoreType.DMA],
-    )(query, key, value, in_hbm(cotangent[0]), w)
+        [(rows, BF16), ((width, model), BF16), ((heads * tokens, tokens), BF16), (rows, F32), (rows, F32)],
+        "hvvhh", flops=2 * square + 2 * layer, moved=6 << 20,
+        scratch=[pltpu.VMEM((tokens, model), BF16), pltpu.SemaphoreType.DMA((3,))],
+    )(in_hbm(queries[0]), key, value, in_hbm(cotangent[0]), in_hbm(w_out))
     sums, _ = spread(outer, msg, True)
     state, keep, send, grad, outer, msg, gain_part = call(
         functools.partial(forward_body, heads, dim, last),
@@ -331,7 +336,7 @@
     query_grad, key_part, value_part = call(
         functools.partial(backward_body, heads, dim),
         [(rows, BF16), (rows, F32), (rows, F32)],
-        "vvvvvv", flops=4 * square + matrix, moved=4 << 20,
+        "vvvvvv", flops=0, moved=1 << 16,
     )(query, key, value, weights, grad, state)
     sums, msg = spread(outer, msg, False)
     if gains:

time: 40 us -> 38.2 us (0.955)
  waiting for transfers between devices: 14.8 us -> 10.7 us
  starting transfers between devices: 13.9 us -> 16.1 us
    ppermute x8, waiting for transfers between devices: 12.4 us -> 10 us  [exchange(): lax.ppermute(block, ('seq', 'dp'), pairing(lax.axis_size('seq'), pairs))]
    ppermute x8, starting transfers between devices: 9.65 us -> 11.8 us  [exchange(): lax.ppermute(block, ('seq', 'dp'), pairing(lax.axis_size('seq'), pairs))]
    ppermute x3, waiting for transfers between devices: 2.47 us -> 0.69 us  [flipped(): return lax.ppermute(block, ('seq', 'dp'), route)]
  transfers between devices with their start and end apart: 12 -> 12, of which waited for: 6 -> 5; matrix products, arithmetic and copies ran while one was open for 0% -> 0% of each run, Pallas kernels for 13% -> 16%
where the time goes in v4:
time: 38.2 us; the launch traced here: 38 us
  starting transfers between devices  16.1 us (42%)
  waiting for transfers between devices  10.7 us (28%)
  Pallas kernels  9.86 us (26%)
  between operations  1.34 us (4%)
    ppermute x8, starting transfers between devices, exchange(): lax.ppermute(block, ('seq', 'dp'), pairing(lax.axis_size('seq'), pairs))  11.8 us
    ppermute x8, waiting for transfers between devices, exchange(): lax.ppermute(block, ('seq', 'dp'), pairing(lax.axis_size('seq'), pairs))  10 us
    pallas_call x1, Pallas kernels, on_device(): call(functools.partial(local_body, heads, dim), [(rows, BF16), ((width, m...  2.78 us
    ppermute x3, starting transfers between devices, flipped(): return lax.ppermute(block, ('seq', 'dp'), route)  2.75 us
    pallas_call x1, Pallas kernels, on_device(): call(functools.partial(backward_body, heads, dim), [(rows, BF16), (rows,...  1.92 us
    ppermute x1, starting transfers between devices, on_device(): got = lax.ppermute(send, 'head', [(0, 1), (1, 0)])  1.54 us
    pallas_call x1, Pallas kernels, on_device(): call(functools.partial(forward_body, heads, dim, last), [(summed, BF16),...  1.36 us
    pallas_call x1, Pallas kernels, on_device(): call(functools.partial(opening_body, heads, dim), [(rows, BF16)] * 2 + [(...  1.33 us
  transfers between devices with their start and end apart: 12, of which 5 were waited for; matrix products, arithmetic and copies ran while one was open for 0% of the time, Pallas kernels for 16%

profile of v4, /device:TPU:0, one launch (start us, length us, event | category | flops | bytes accessed | tf_op | source)
XLA Modules:
  0.0 38.0 jit_solution(7452613335809709319)
XLA Ops:
  1.3 1.3 %shard_map.110 = (bf16[256,512]{1,0:T(8,128)(2,1)S(1)}, bf16[256,512]{1,0:T(8,128)(2,1)S(1)}, f32[8,128]{1,0:T(8,128)S(1)}, f32[512,128]{1,0:T(8,128)S(1)}, bf16[528,128]{1,0:T(8,128)(2,1)S(1)}) custom-call(s32[1,1]{1,0:T(1,128)S(6)} %copy.12.doc_any, bf16[256,512]{1,0:T(8,128)(2,1)} %bitcast.9, bf16[256,512]{1,0:T(8,128)(2,1)} %bitcast.10), custom_call_target="tpu_custom_call" | custom-call | flops 33554432 | bytes 1048576 | tf_op jit(solution)/shard_map/pallas_call | solution.py:315
  2.6 3.0 %collective-permute-start = (bf16[528,128]{1,0:T(8,128)(2,1)S(1)}, bf16[528,128]{1,0:T(8,128)(2,1)S(1)}, u32[]{:S(2)}, u32[]{:S(2)}) collective-permute-start(bf16[528,128]{1,0:T(8,128)(2,1)S(1)} %get-tuple-element.39.own_ref), channel_id=1, source_target_pairs={{0,4},{1,5},{4,0},{5,1},{8,12},{9,13},{12,8},{13,9},{16,20},{17,21... | collective-permute-start | bytes 405512 | tf_op jit(solution)/shard_map/ppermute | solution.py:53
  5.6 4.0 %collective-permute-done.pair_ref.refs_0_ = bf16[528,128]{1,0:T(8,128)(2,1)S(1)} collective-permute-done((bf16[528,128]{1,0:T(8,128)(2,1)S(1)}, bf16[528,128]{1,0:T(8,128)(2,1)S(1)}, u32[]{:S(2)}, u32[]{:S(2)}) %collective-permute-start) | collective-permute-done | bytes 135200 | tf_op jit(solution)/shard_map/ppermute | solution.py:53
  9.6 0.1 shard_map.112
  9.7 0.0 copy-start
  9.7 3.4 %collective-permute-start.1 = (bf16[528,128]{1,0:T(8,128)(2,1)S(1)}, bf16[528,128]{1,0:T(8,128)(2,1)S(1)}, u32[]{:S(2)}, u32[]{:S(2)}) collective-permute-start(bf16[528,128]{1,0:T(8,128)(2,1)S(1)} %shard_map.112), channel_id=1, source_target_pairs={{0,8},{1,9},{4,12},{5,13},{8,0},{9,1},{12,4},{13,5},{16,24},{17,25... | collective-permute-start | bytes 405512 | tf_op jit(solution)/shard_map/ppermute | solution.py:53
  13.1 2.8 %shard_map.111 = (bf16[256,512]{1,0:T(8,128)(2,1)S(1)}, bf16[512,2048]{1,0:T(8,128)(2,1)S(1)}, bf16[1024,256]{1,0:T(8,128)(2,1)S(1)}, f32[256,512]{1,0:T(8,128)S(1)}, f32[256,512]{1,0:T(8,128)S(1)}) custom-call(bf16[256,512]{1,0:T(8,128)(2,1)} %bitcast.11, bf16[256,512]{1,0:T(8,128)(2,1)S(1)} %get-tuple-element.33.key_ref, ...), custom_call_target="tpu_custom_call" | custom-call | flops 671088640 | bytes 6291456 | tf_op jit(solution)/shard_map/pallas_call | solution.py:320
  15.9 0.0 collective-permute-done.2.refs_1_
  15.9 0.7 %collective-permute-done.1.refs_2_ = bf16[528,128]{1,0:T(8,128)(2,1)S(1)} collective-permute-done((bf16[528,128]{1,0:T(8,128)(2,1)S(1)}, bf16[528,128]{1,0:T(8,128)(2,1)S(1)}, u32[]{:S(2)}, u32[]{:S(2)}) %collective-permute-start.1) | collective-permute-done | bytes 135200 | tf_op jit(solution)/shard_map/ppermute | solution.py:53
  16.5 0.0 collective-permute-done.3.refs_3_
  16.5 1.4 %shard_map.113 = (bf16[512,128]{1,0:T(8,128)(2,1)S(1)}, bf16[128,512]{1,0:T(8,128)(2,1)S(1)}, bf16[128,2048]{1,0:T(8,128)(2,1)S(1)}, bf16[256,512]{1,0:T(8,128)(...) custom-call(f32[8,128]{1,0:T(8,128)S(1)} %get-tuple-element.32.number_ref, ...), custom_call_target="tpu_custom_call" | custom-call | flops 335544320 | bytes 4194304 | tf_op jit(solution)/shard_map/pallas_call | solution.py:327
  17.9 1.5 %collective-permute-start.4 = (bf16[128,2048]{1,0:T(8,128)(2,1)S(1)}, bf16[128,2048]{1,0:T(8,128)(2,1)S(1)}, u32[]{:S(2)}, u32[]{:S(2)}) collective-permute-start(bf16[128,2048]{1,0:T(8,128)(2,1)S(1)} %get-tuple-element.44), channel_id=1, source_target_pairs={{0,2},{2,0},{1,3},{3,1},{4,6},{6,4},{5,7},{7,5},{8,10},{10,8},{9,1... | collective-permute-start | bytes 1572872 | tf_op jit(solution)/shard_map/ppermute | solution.py:335
  19.4 2.0 %collective-permute-start.5 = (bf16[528,128]{1,0:T(8,128)(2,1)S(1)}, bf16[528,128]{1,0:T(8,128)(2,1)S(1)}, u32[]{:S(2)}, u32[]{:S(2)}) collective-permute-start(bf16[528,128]{1,0:T(8,128)(2,1)S(1)} %get-tuple-element.46.own_ref), channel_id=1, source_target_pairs={{0,4},{1,5},{4,0},{5,1},{8,12},{9,13},{12,8},{13,9},{16,20},{17,21... | collective-permute-start | bytes 405512 | tf_op jit(solution)/shard_map/ppermute | solution.py:53
  21.4 3.8 %collective-permute-done.5.pair_ref.refs_0_ = bf16[528,128]{1,0:T(8,128)(2,1)S(1)} collective-permute-done((bf16[528,128]{1,0:T(8,128)(2,1)S(1)}, bf16[528,128]{1,0:T(8,128)(2,1)S(1)}, u32[]{:S(2)}, u32[]{:S(2)}) %collective-permute-start.5) | collective-permute-done | bytes 135200 | tf_op jit(solution)/shard_map/ppermute | solution.py:53
  25.2 0.1 shard_map.114.own_ref
  25.3 3.4 %collective-permute-start.6 = (bf16[528,128]{1,0:T(8,128)(2,1)S(1)}, bf16[528,128]{1,0:T(8,128)(2,1)S(1)}, u32[]{:S(2)}, u32[]{:S(2)}) collective-permute-start(bf16[528,128]{1,0:T(8,128)(2,1)S(1)} %shard_map.114.own_ref), channel_id=1, source_target_pairs={{0,8},{1,9},{4,12},{5,13},{8,0},{9,1},{12,4},{13,5},{16,24},{17,25... | collective-permute-start | bytes 405512 | tf_op jit(solution)/shard_map/ppermute | solution.py:53
  28.7 1.9 %shard_map.117 = (bf16[256,512]{1,0:T(8,128)(2,1)}, f32[256,512]{1,0:T(8,128)S(1)}, f32[256,512]{1,0:T(8,128)S(1)}) custom-call(bf16[256,512]{1,0:T(8,128)(2,1)S(1)} %get-tuple-element.35.query_ref, bf16[256,512]{1,0:T(8,128)(2,1)S(1)} %get-tuple-element.33.key_ref, bf16[256,512]{1,0:T(8,128)(2,1)S(1)} %get-tuple-element.34.value_ref, ...), custom_call_target="tpu_custom_call" | custom-call | bytes 65536 | tf_op jit(solution)/shard_map/pallas_call | solution.py:336
  30.6 1.6 %collective-permute-done.6.other_ref.refs_2_ = bf16[528,128]{1,0:T(8,128)(2,1)S(1)} collective-permute-done((bf16[528,128]{1,0:T(8,128)(2,1)S(1)}, bf16[528,128]{1,0:T(8,128)(2,1)S(1)}, u32[]{:S(2)}, u32[]{:S(2)}) %collective-permute-start.6) | collective-permute-done | bytes 135200 | tf_op jit(solution)/shard_map/ppermute | solution.py:53
  32.2 1.5 %collective-permute-start.9 = (f32[4,128]{1,0:T(4,128)S(1)}, f32[4,128]{1,0:T(4,128)S(1)}, u32[]{:S(2)}, u32[]{:S(2)}) collective-permute-start(f32[4,128]{1,0:T(4,128)S(1)} %shard_map.115.refs_0_), channel_id=1, source_target_pairs={{0,16},{1,17},{4,20},{5,21},{8,24},{9,25},{12,28},{13,29},{16,0},{... | collective-permute-start | bytes 6152 | tf_op jit(solution)/shard_map/ppermute | solution.py:71
  33.8 1.2 %collective-permute-start.8 = (f32[4,128]{1,0:T(4,128)S(1)}, f32[4,128]{1,0:T(4,128)S(1)}, u32[]{:S(2)}, u32[]{:S(2)}) collective-permute-start(f32[4,128]{1,0:T(4,128)S(1)} %shard_map.115.refs_0_), channel_id=1, source_target_pairs={{0,1},{1,0},{4,5},{5,4},{8,9},{9,8},{12,13},{13,12},{16,17},{17,16... | collective-permute-start | bytes 6152 | tf_op jit(solution)/shard_map/ppermute | solution.py:71
  35.0 1.1 %shard_map.118 = (bf16[256,512]{1,0:T(8,128)(2,1)}, bf16[256,512]{1,0:T(8,128)(2,1)}) custom-call(f32[8,128]{1,0:T(8,128)S(1)} %get-tuple-element.32.number_ref, bf16[256,512]{1,0:T(8,128)(2,1)S(1)} %get-tuple-element.33.key_ref, bf16[256,512]{1,0:T(8,128)(2,1)S(1)} %get-tuple-element.34.value_ref, f32[256,512]{1,0:T(8,128)S(1)} %get-tuple-element.53.key_part_ref, ...), custom_call_target="tpu_custom_call" | custom-call | flops 67108864 | bytes 3145728 | tf_op jit(solution)/shard_map/pallas_call | solution.py:348
  36.1 0.0 collective-permute-done.10.refs_3_
  36.1 0.6 %collective-permute-done.9.refs_2_ = f32[4,128]{1,0:T(4,128)S(1)} collective-permute-done((f32[4,128]{1,0:T(4,128)S(1)}, f32[4,128]{1,0:T(4,128)S(1)}, u32[]{:S(2)}, u32[]{:S(2)}) %collective-permute-start.9) | collective-permute-done | bytes 2080 | tf_op jit(solution)/shard_map/ppermute | solution.py:71
  36.8 1.3 %shard_map.116 = (bf16[128,2048]{1,0:T(8,128)(2,1)}, f32[4,128]{1,0:T(4,128)}) custom-call(bf16[128,512]{1,0:T(8,128)(2,1)S(1)} %get-tuple-element.43.keep_ref, bf16[512,2048]{1,0:T(8,128)(2,1)S(1)} %get-tuple-element.38.w_ref, bf16[128,2048]{1,0:T(8,128)(2,1)S(1)} %collective-permute-done.4.got_ref, f32[4,128]{1,0:T(4,128)S(1)} %shard_map.115.refs_0_, ...), custom_call_target="tpu_custom_call" | custom-call | flops 268435456 | bytes 6291456 | tf_op jit(solution)/shard_map/pallas_call | solution.py:353
  (11 shorter events, 0.0 us)
Async XLA Ops:
  2.6 7.0 %collective-permute-start = (bf16[528,128]{1,0:T(8,128)(2,1)S(1)}, bf16[528,128]{1,0:T(8,128)(2,1)S(1)}, u32[]{:S(2)}, u32[]{:S(2)}) collective-permute-start(bf16[528,128]{1,0:T(8,128)(2,1)S(1)} %get-tuple-element.39.own_ref), channel_id=1, source_target_pairs={{0,4},{1,5},{4,0},{5,1},{8,12},{9,13},{12,8},{13,9},{16,20},{17,21... | collective-permute-start | bytes 405512 | tf_op jit(solution)/shard_map/ppermute | solution.py:53
  5.6 10.2 %collective-permute-start.2 = (bf16[528,128]{1,0:T(8,128)(2,1)S(1)}, bf16[528,128]{1,0:T(8,128)(2,1)S(1)}, u32[]{:S(2)}, u32[]{:S(2)}) collective-permute-start(bf16[528,128]{1,0:T(8,128)(2,1)S(1)} %get-tuple-element.39.own_ref), channel_id=1, source_target_pairs={{0,1},{1,0},{4,16},{5,17},{8,9},{9,8},{12,24},{13,25},{16,4},{17,5... | collective-permute-start | bytes 405512 | tf_op jit(solution)/shard_map/ppermute | solution.py:53
  9.7 6.9 %copy-start = (f32[4,128]{1,0:T(4,128)S(1)}, f32[4,128]{1,0:T(4,128)}, u32[]{:S(2)}) copy-start(f32[4,128]{1,0:T(4,128)} %gain_ref.1) | copy-start | bytes 6148
  9.7 6.8 %collective-permute-start.1 = (bf16[528,128]{1,0:T(8,128)(2,1)S(1)}, bf16[528,128]{1,0:T(8,128)(2,1)S(1)}, u32[]{:S(2)}, u32[]{:S(2)}) collective-permute-start(bf16[528,128]{1,0:T(8,128)(2,1)S(1)} %shard_map.112), channel_id=1, source_target_pairs={{0,8},{1,9},{4,12},{5,13},{8,0},{9,1},{12,4},{13,5},{16,24},{17,25... | collective-permute-start | bytes 405512 | tf_op jit(solution)/shard_map/ppermute | solution.py:53
  13.1 3.5 %collective-permute-start.3 = (bf16[528,128]{1,0:T(8,128)(2,1)S(1)}, bf16[528,128]{1,0:T(8,128)(2,1)S(1)}, u32[]{:S(2)}, u32[]{:S(2)}) collective-permute-start(bf16[528,128]{1,0:T(8,128)(2,1)S(1)} %shard_map.112), channel_id=1, source_target_pairs={{0,1},{1,0},{4,5},{5,4},{8,16},{9,17},{12,20},{13,21},{16,8},{17,9... | collective-permute-start | bytes 405512 | tf_op jit(solution)/shard_map/ppermute | solution.py:53
  17.9 18.9 %collective-permute-start.4 = (bf16[128,2048]{1,0:T(8,128)(2,1)S(1)}, bf16[128,2048]{1,0:T(8,128)(2,1)S(1)}, u32[]{:S(2)}, u32[]{:S(2)}) collective-permute-start(bf16[128,2048]{1,0:T(8,128)(2,1)S(1)} %get-tuple-element.44), channel_id=1, source_target_pairs={{0,2},{2,0},{1,3},{3,1},{4,6},{6,4},{5,7},{7,5},{8,10},{10,8},{9,1... | collective-permute-start | bytes 1572872 | tf_op jit(solution)/shard_map/ppermute | solution.py:335
  19.4 5.8 %collective-permute-start.5 = (bf16[528,128]{1,0:T(8,128)(2,1)S(1)}, bf16[528,128]{1,0:T(8,128)(2,1)S(1)}, u32[]{:S(2)}, u32[]{:S(2)}) collective-permute-start(bf16[528,128]{1,0:T(8,128)(2,1)S(1)} %get-tuple-element.46.own_ref), channel_id=1, source_target_pairs={{0,4},{1,5},{4,0},{5,1},{8,12},{9,13},{12,8},{13,9},{16,20},{17,21... | collective-permute-start | bytes 405512 | tf_op jit(solution)/shard_map/ppermute | solution.py:53
  21.4 9.2 %collective-permute-start.7 = (bf16[528,128]{1,0:T(8,128)(2,1)S(1)}, bf16[528,128]{1,0:T(8,128)(2,1)S(1)}, u32[]{:S(2)}, u32[]{:S(2)}) collective-permute-start(bf16[528,128]{1,0:T(8,128)(2,1)S(1)} %get-tuple-element.46.own_ref), channel_id=1, source_target_pairs={{0,1},{1,0},{4,16},{5,17},{8,9},{9,8},{12,24},{13,25},{16,4},{17,5... | collective-permute-start | bytes 405512 | tf_op jit(solution)/shard_map/ppermute | solution.py:53
  25.3 6.9 %collective-permute-start.6 = (bf16[528,128]{1,0:T(8,128)(2,1)S(1)}, bf16[528,128]{1,0:T(8,128)(2,1)S(1)}, u32[]{:S(2)}, u32[]{:S(2)}) collective-permute-start(bf16[528,128]{1,0:T(8,128)(2,1)S(1)} %shard_map.114.own_ref), channel_id=1, source_target_pairs={{0,8},{1,9},{4,12},{5,13},{8,0},{9,1},{12,4},{13,5},{16,24},{17,25... | collective-permute-start | bytes 405512 | tf_op jit(solution)/shard_map/ppermute | solution.py:53
  28.7 6.3 %collective-permute-start.11 = (bf16[528,128]{1,0:T(8,128)(2,1)S(1)}, bf16[528,128]{1,0:T(8,128)(2,1)S(1)}, u32[]{:S(2)}, u32[]{:S(2)}) collective-permute-start(bf16[528,128]{1,0:T(8,128)(2,1)S(1)} %shard_map.114.own_ref), channel_id=1, source_target_pairs={{0,1},{1,0},{4,5},{5,4},{8,16},{9,17},{12,20},{13,21},{16,8},{17,9... | collective-permute-start | bytes 405512 | tf_op jit(solution)/shard_map/ppermute | solution.py:53
  32.2 3.9 %collective-permute-start.10 = (f32[4,128]{1,0:T(4,128)S(1)}, f32[4,128]{1,0:T(4,128)S(1)}, u32[]{:S(2)}, u32[]{:S(2)}) collective-permute-start(f32[4,128]{1,0:T(4,128)S(1)} %shard_map.115.refs_0_), channel_id=1, source_target_pairs={{0,17},{1,16},{4,21},{5,20},{8,25},{9,24},{12,29},{13,28},{16,1},{... | collective-permute-start | bytes 6152 | tf_op jit(solution)/shard_map/ppermute | solution.py:71
  32.2 4.5 %collective-permute-start.9 = (f32[4,128]{1,0:T(4,128)S(1)}, f32[4,128]{1,0:T(4,128)S(1)}, u32[]{:S(2)}, u32[]{:S(2)}) collective-permute-start(f32[4,128]{1,0:T(4,128)S(1)} %shard_map.115.refs_0_), channel_id=1, source_target_pairs={{0,16},{1,17},{4,20},{5,21},{8,24},{9,25},{12,28},{13,29},{16,0},{... | collective-permute-start | bytes 6152 | tf_op jit(solution)/shard_map/ppermute | solution.py:71
  33.8 3.0 %collective-permute-start.8 = (f32[4,128]{1,0:T(4,128)S(1)}, f32[4,128]{1,0:T(4,128)S(1)}, u32[]{:S(2)}, u32[]{:S(2)}) collective-permute-start(f32[4,128]{1,0:T(4,128)S(1)} %shard_map.115.refs_0_), channel_id=1, source_target_pairs={{0,1},{1,0},{4,5},{5,4},{8,9},{9,8},{12,13},{13,12},{16,17},{17,16... | collective-permute-start | bytes 6152 | tf_op jit(solution)/shard_map/ppermute | solution.py:71

commit v5 on v4

--- a/solution.py
+++ b/solution.py
@@ -35,6 +35,7 @@
         in_specs=[pl.BlockSpec(memory_space=space[p]) for p in places],
         out_specs=[pl.BlockSpec(memory_space=pltpu.VMEM) for _ in outs],
         scratch_shapes=list(scratch),
+        name=getattr(body, "func", body).__name__,
         cost_estimate=pl.CostEstimate(flops=flops, bytes_accessed=moved, transcendentals=0),
         compiler_params=pltpu.CompilerParams(vmem_limit_bytes=40 << 20),
     )
@@ -167,11 +168,20 @@
     normed_grad_ref[...] = nt(cot_ref[...], w_ref[...])
 
 
+def fetch_body(number_ref, w_hbm, part_ref, sem):
+    rows, cols = part_ref.shape
+    core = lax.axis_index("dp")
+    ours = w_hbm.at[pl.ds(pl.multiple_of(core * rows, rows), rows), pl.ds(0, cols)]
+    copy = pltpu.make_async_copy(ours, part_ref, sem)
+    copy.start()
+    copy.wait()
+
+
 def merge_gain(gains, own_ref, other_ref):
     return sent_gain(own_ref) + sent_gain(other_ref) if gains else None
 
 
-def pair_body(forward, gains, number_ref, sum_ref, own_ref, pair_ref, msg_ref):
+def pair_body(forward, gains, number_ref, sum_ref, own_ref, pair_ref, msg_ref, *gain_ref):
     rows = sum_ref.shape[0]
     number = number_ref[:1, :]
     leads = lax.rem(lax.axis_index("seq"), 2) == (1 if forward else 0)
@@ -180,10 +190,13 @@
     same = theirs == number
     keep_mine, keep_theirs = same | leads, same | jnp.logical_not(leads)
     msg_ref[:rows, :] = (jnp.where(keep_mine, mine, 0.0) + jnp.where(keep_theirs, sums, 0.0)).astype(BF16)
-    put_tail(msg_ref, jnp.where(leads, number, theirs), merge_gain(gains, own_ref, pair_ref))
+    gain = put_tail(msg_ref, jnp.where(leads, number, theirs), merge_gain(gains, own_ref, pair_ref))
+    if gains:
+        gain_ref[0][...] = gain
 
 
 def merge_body(distance, forward, gains, number_ref, sum_ref, own_ref, *refs):
+    gain_ref, refs = (refs[-1:], refs[:-1]) if gains else ((), refs)
     *term_ref, even_ref, odd_ref, out_ref, msg_ref = refs
     rows = sum_ref.shape[0]
     number = number_ref[:1, :]
@@ -192,18 +205,20 @@
         term = term + term_ref[0][...]
     out_ref[...] = term
     msg_ref[:rows, :] = (sum_ref[...] + term).astype(BF16)
-    put_tail(msg_ref, number, merge_gain(gains, own_ref, even_ref))
-
-
-def gain_body(own_ref, other_ref, out_ref):
-    out_ref[...] = merge_gain(True, own_ref, other_ref)
+    gain = put_tail(msg_ref, number, merge_gain(gains, own_ref, even_ref))
+    if gains:
+        gain_ref[0][...] = gain
+
+
+def gain_body(own_ref, other_ref, far_ref, farther_ref, out_ref):
+    out_ref[...] = merge_gain(True, own_ref, other_ref) + (far_ref[...] + farther_ref[...])
 
 
 def forward_body(
     heads, dim, distance, number_ref, query_ref, within_ref, normed_grad_ref, gain_ref, w_ref, *refs
 ):
-    *sum_refs, state_ref, keep_ref, send_ref, grad_ref, outer_ref, msg_ref, gain_grad_ref, normed_ref = refs
-    half = keep_ref.shape[0]
+    *sum_refs, state_ref, keep_ref, give_ref, grad_ref, outer_ref, msg_ref, gain_grad_ref, normed_ref = refs
+    half, width = keep_ref.shape
     number = number_ref[:1, :]
     state_ref[...] = total(sum_refs, number, distance, True).astype(BF16)
     for h in range(heads):
@@ -226,9 +241,9 @@
     put_tail(msg_ref, number, gain_grad_ref[...])
     head = lax.axis_index("head")
     keep_ref[...] = normed_ref[pl.ds(pl.multiple_of(head * half, half), half), :]
-    send_ref[...] = nn(
-        normed_ref[pl.ds(pl.multiple_of((1 - head) * half, half), half), :], w_ref[...]
-    ).astype(BF16)
+    give = normed_ref[pl.ds(pl.multiple_of((1 - head) * half, half), half), :]
+    give_ref[:, :width] = give
+    give_ref[:, width:] = nn(give, w_ref[:, w_ref.shape[1] + width - give_ref.shape[1] :]).astype(BF16)
 
 
 def backward_body(
@@ -266,13 +281,22 @@
         ).astype(BF16)
 
 
-def layer_body(scale, keep_ref, w_ref, got_ref, *refs):
+def layer_body(scale, keep_ref, w_ref, took_ref, mine_ref, other_ref, *refs):
     *gain_refs, out_ref, gain_grad_ref = refs
-    out_ref[...] = (nn(keep_ref[...], w_ref[...]) + got_ref[...].astype(F32)).astype(BF16)
-    parts = [ref[...] for ref in gain_refs]
-    if len(parts) == 4:
-        parts = [(parts[0] + parts[1]) + (parts[2] + parts[3])]
-    gain_grad_ref[...] = parts[0] * scale
+    width, cols = mine_ref.shape
+    core = lax.axis_index("dp")
+    at = lambda i: pl.ds(pl.multiple_of(i * width, width), width)
+    keep = keep_ref[...]
+    out_ref[:, :cols] = (
+        nn(keep, w_ref[:, :cols])
+        + nn(took_ref[:, at(core)], mine_ref[...])
+        + nn(took_ref[:, at(1 - core)], other_ref[...])
+    ).astype(BF16)
+    out_ref[:, cols:] = (nn(keep, w_ref[:, cols:]) + took_ref[:, 2 * width :].astype(F32)).astype(BF16)
+    gain = gain_refs[0][...]
+    if len(gain_refs) > 1:
+        gain = gain + gain_refs[1][...]
+    gain_grad_ref[...] = gain * scale
 
 
 def on_device(queries, key_rows, value_rows, stretch_doc, head_gain, w_out, cotangent):
@@ -284,7 +308,7 @@
     square = 2 * tokens * tokens * dim * heads
     layer = tokens * width * model
     rows, summed, message = (tokens, width), (heads * dim, dim), (heads * dim + TAIL, dim)
-    small, half = (heads, dim), (tokens // 2, model)
+    small, half, cols = (heads, dim), tokens // 2, model // 2
     distances = [1]
     while 2 * distances[-1] - 1 < size // 2 - 1:
         distances.append(2 * distances[-1])
@@ -293,23 +317,25 @@
 
     def spread(outer, msg, forward):
         carry = gains and not forward
+        extra = [(small, F32)] * carry
         if last == 2:
             pair = exchange(msg, blocks(size, 1, 0))
             far = exchange(msg, [(i, i + 3) for i in range(1, size - 3, 2)])
-            (msg,) = call(
-                functools.partial(pair_body, forward, carry), [(message, BF16)], "vvvv", flops=0, moved=1 << 20
+            msg, *gain = call(
+                functools.partial(pair_body, forward, carry), [(message, BF16), *extra], "vvvv", flops=0, moved=1 << 20
             )(number, outer, msg, pair)
             even, odd = swaps(msg, last)
-            even, far = lax.optimization_barrier((even, far))
-            return [pair, far, even, odd], msg
+            even, odd, far = lax.optimization_barrier((even, odd, far))
+            return [pair, far, even, odd], msg, gain
         terms = []
         for distance in distances[:-1]:
             even, odd = swaps(msg, distance)
-            *terms, msg = call(
-                functools.partial(merge_body, distance, forward, carry), [(summed, F32), (message, BF16)],
+            term, msg, *gain = call(
+                functools.partial(merge_body, distance, forward, carry), [(summed, F32), (message, BF16), *extra],
                 "vvvvv" + "v" * len(terms), flops=0, moved=1 << 20,
             )(number, outer, msg, *terms, even, odd)
-        return [*terms, *swaps(msg, last)], msg
+            terms = [term]
+        return [*terms, *swaps(msg, last)], msg, gain
 
     in_hbm = lambda block: pltpu.with_memory_space_constraint(block, pltpu.HBM)
     key, value, number, outer, msg = call(
@@ -317,43 +343,51 @@
         [(rows, BF16)] * 2 + [((8, dim), F32), (summed, F32), (message, BF16)],
         "ahh", flops=matrix, moved=1 << 20, scratch=[pltpu.SMEM((1, 1), jnp.int32), pltpu.SemaphoreType.DMA((3,))],
     )(stretch_doc, in_hbm(key_rows[0]), in_hbm(value_rows[0]))
+    (part,) = call(fetch_body, [((width // 2, cols), BF16)], "vh", flops=0, moved=1 << 20, scratch=[pltpu.SemaphoreType.DMA])(
+        number, in_hbm(w_out)
+    )
+    across = [(0, 1), (1, 0)]
+    mine = lax.ppermute(part, "head", across)
     query, w, weights, within, normed_grad = call(
         functools.partial(local_body, heads, dim),
         [(rows, BF16), ((width, model), BF16), ((heads * tokens, tokens), BF16), (rows, F32), (rows, F32)],
         "hvvhh", flops=2 * square + 2 * layer, moved=6 << 20,
         scratch=[pltpu.VMEM((tokens, model), BF16), pltpu.SemaphoreType.DMA((3,))],
     )(in_hbm(queries[0]), key, value, in_hbm(cotangent[0]), in_hbm(w_out))
-    sums, _ = spread(outer, msg, True)
-    state, keep, send, grad, outer, msg, gain_part = call(
+    sums, _, _ = spread(outer, msg, True)
+    state, keep, give, grad, outer, msg, gain_part = call(
         functools.partial(forward_body, heads, dim, last),
         [
-            (summed, BF16), ((tokens // 2, width), BF16), (half, BF16),
+            (summed, BF16), ((half, width), BF16), ((half, width + model - cols), BF16),
             (rows, BF16), (summed, F32), (message, BF16), (small, F32),
         ],
         "vvvvvv" + "v" * len(sums), flops=2 * matrix + layer, moved=4 << 20, scratch=[pltpu.VMEM(rows, BF16)],
     )(number, query, within, normed_grad, head_gain, w, *sums)
-    got = lax.ppermute(send, "head", [(0, 1), (1, 0)])
+    took = lax.ppermute(give, "head", across)
     query_grad, key_part, value_part = call(
         functools.partial(backward_body, heads, dim),
         [(rows, BF16), (rows, F32), (rows, F32)],
         "vvvvvv", flops=0, moved=1 << 16,
     )(query, key, value, weights, grad, state)
-    sums, msg = spread(outer, msg, False)
+    sums, msg, gain = spread(outer, msg, False)
     if gains:
-        (gain,) = call(gain_body, [(small, F32)], "vv", flops=0, moved=1 << 16)(msg, sums[-2])
-        across = [flipped(gain, *to) for to in ((0, 1), (size // 2, 0), (size // 2, 1))]
-        gain_parts = [gain, *across]
+        *sums, key_part, took = lax.optimization_barrier((*sums, key_part, took))
+        far = [flipped(gain[0], to, 0) for to in (size // 2, size // 2 + last)]
+        (gain,) = call(gain_body, [(small, F32)], "vvvv", flops=0, moved=1 << 16)(msg, sums[-2], *far)
+        gain, mine = lax.optimization_barrier((gain, mine))
+        gain_parts = [gain, flipped(gain, 0, 1)]
     else:
         gain_parts = [lax.psum(gain_part, ("seq", "dp"))]
+    other = flipped(mine, 0, 1)
     key_grad, value_grad = call(
         functools.partial(last_body, heads, dim, last), [(rows, BF16), (rows, BF16)],
         "vvvvv" + "v" * len(sums), flops=2 * matrix, moved=3 << 20,
     )(number, key, value, key_part, value_part, *sums)
     scale = 1.0 / math.sqrt(size * lax.axis_size("dp") * tokens)
     layer_out, gain_grad = call(
-        functools.partial(layer_body, scale), [(half, BF16), (small, F32)],
-        "vvv" + "v" * len(gain_parts), flops=layer, moved=6 << 20,
-    )(keep, w, got, *gain_parts)
+        functools.partial(layer_body, scale), [((half, model), BF16), (small, F32)],
+        "vvvvv" + "v" * len(gain_parts), flops=2 * layer, moved=6 << 20,
+    )(keep, w, took, mine, other, *gain_parts)
     return layer_out[None], query_grad[None], key_grad[None], value_grad[None], gain_grad
 
 

time: 38.2 us -> 42.9 us (1.12)
  starting transfers between devices: 16.1 us -> 19.3 us
  Pallas kernels: 9.86 us -> 11.1 us
    ppermute x3 -> x4, starting transfers between devices: 2.75 us -> 6.8 us  [flipped(): return lax.ppermute(block, ('seq', 'dp'), route)]
    ppermute x3 -> x4, waiting for transfers between devices: 0.69 us -> 2.66 us  [flipped(): return lax.ppermute(block, ('seq', 'dp'), route)]
    ppermute x8, waiting for transfers between devices: 10 us -> 8.09 us  [exchange(): lax.ppermute(block, ('seq', 'dp'), pairing(lax.axis_size('seq'), pairs))]
    ppermute x8, starting transfers between devices: 11.8 us -> 10.4 us  [exchange(): lax.ppermute(block, ('seq', 'dp'), pairing(lax.axis_size('seq'), pairs))]
    pallas_call x4 -> x5, Pallas kernels: 1.37 us -> 2.56 us  [the longest x1 1.39 us: on_device(): call(functools.partial(layer_body, scale), [((half, model), BF16), (small...]
    ppermute x1 -> x2, starting transfers between devices: 1.54 us -> 2.09 us  [the longest x1 1.58 us: on_device(): mine = lax.ppermute(part, 'head', across)]
  transfers between devices with their start and end apart: 12 -> 14, of which waited for: 5 -> 5; matrix products, arithmetic and copies ran while one was open for 0% -> 0% of each run, Pallas kernels for 16% -> 20%
where the time goes in v5:
time: 42.9 us; the launch traced here: 42.7 us
  starting transfers between devices  19.3 us (45%)
  Pallas kernels  11.1 us (26%)
  waiting for transfers between devices  11 us (26%)
  between operations  1.37 us (3%)
    ppermute x8, starting transfers between devices, exchange(): lax.ppermute(block, ('seq', 'dp'), pairing(lax.axis_size('seq'), pairs))  10.4 us
    ppermute x8, waiting for transfers between devices, exchange(): lax.ppermute(block, ('seq', 'dp'), pairing(lax.axis_size('seq'), pairs))  8.09 us
    ppermute x4, starting transfers between devices, flipped(): return lax.ppermute(block, ('seq', 'dp'), route)  6.8 us
    pallas_call x1, Pallas kernels, on_device(): call(functools.partial(local_body, heads, dim), [(rows, BF16), ((width, m...  2.78 us
    ppermute x4, waiting for transfers between devices, flipped(): return lax.ppermute(block, ('seq', 'dp'), route)  2.66 us
    pallas_call x1, Pallas kernels, on_device(): call(functools.partial(backward_body, heads, dim), [(rows, BF16), (rows,...  1.92 us
    ppermute x1, starting transfers between devices, on_device(): mine = lax.ppermute(part, 'head', across)  1.58 us
    pallas_call x1, Pallas kernels, on_device(): call(functools.partial(layer_body, scale), [((half, model), BF16), (small...  1.39 us
  transfers between devices with their start and end apart: 14, of which 5 were waited for; matrix products, arithmetic and copies ran while one was open for 0% of the time, Pallas kernels for 20%

profile of v5, /device:TPU:0, one launch (start us, length us, event | category | flops | bytes accessed | tf_op | source)
XLA Modules:
  0.0 42.7 jit_solution(4435705722911415301)
XLA Ops:
  1.3 1.3 %opening_body.1 = (bf16[256,512]{1,0:T(8,128)(2,1)S(1)}, bf16[256,512]{1,0:T(8,128)(2,1)S(1)}, f32[8,128]{1,0:T(8,128)S(1)}, f32[512,128]{1,0:T(8,128)S(1)}, bf16[528,128]{1,0:T(8,128)(2,1)S(1)}) custom-call(s32[1,1]{1,0:T(1,128)S(6)} %copy.12.doc_any, bf16[256,512]{1,0:T(8,128)(2,1)} %bitcast.9, bf16[256,512]{1,0:T(8,128)(2,1)} %bitcast.10), custom_call_target="tpu_custom_call" | custom-call | flops 33554432 | bytes 1048576 | tf_op jit(solution)/shard_map/opening_body/pallas_call | solution.py:341
  2.6 3.0 %collective-permute-start = (bf16[528,128]{1,0:T(8,128)(2,1)S(1)}, bf16[528,128]{1,0:T(8,128)(2,1)S(1)}, u32[]{:S(2)}, u32[]{:S(2)}) collective-permute-start(bf16[528,128]{1,0:T(8,128)(2,1)S(1)} %get-tuple-element.51.own_ref), channel_id=1, source_target_pairs={{0,4},{1,5},{4,0},{5,1},{8,12},{9,13},{12,8},{13,9},{16,20},{17,21... | collective-permute-start | bytes 405512 | tf_op jit(solution)/shard_map/ppermute | solution.py:54
  5.6 4.0 %collective-permute-done.pair_ref.refs_0_ = bf16[528,128]{1,0:T(8,128)(2,1)S(1)} collective-permute-done((bf16[528,128]{1,0:T(8,128)(2,1)S(1)}, bf16[528,128]{1,0:T(8,128)(2,1)S(1)}, u32[]{:S(2)}, u32[]{:S(2)}) %collective-permute-start) | collective-permute-done | bytes 135200 | tf_op jit(solution)/shard_map/ppermute | solution.py:54
  9.6 0.1 pair_body.2
  9.7 3.4 %collective-permute-start.1 = (bf16[528,128]{1,0:T(8,128)(2,1)S(1)}, bf16[528,128]{1,0:T(8,128)(2,1)S(1)}, u32[]{:S(2)}, u32[]{:S(2)}) collective-permute-start(bf16[528,128]{1,0:T(8,128)(2,1)S(1)} %pair_body.2), channel_id=1, source_target_pairs={{0,8},{1,9},{4,12},{5,13},{8,0},{9,1},{12,4},{13,5},{16,24},{17,25... | collective-permute-start | bytes 405512 | tf_op jit(solution)/shard_map/ppermute | solution.py:54
  13.1 1.0 %fetch_body.1 = bf16[256,1024]{1,0:T(8,128)(2,1)S(1)} custom-call(f32[8,128]{1,0:T(8,128)S(1)} %get-tuple-element.44.number_ref, bf16[512,2048]{1,0:T(8,128)(2,1)} %w_hbm.3), custom_call_target="tpu_custom_call" | custom-call | bytes 1048576 | tf_op jit(solution)/shard_map/fetch_body/pallas_call | solution.py:346
  14.1 0.0 copy-start
  14.1 1.6 %collective-permute-start.11 = (bf16[256,1024]{1,0:T(8,128)(2,1)S(1)}, bf16[256,1024]{1,0:T(8,128)(2,1)S(1)}, u32[]{:S(2)}, u32[]{:S(2)}) collective-permute-start(bf16[256,1024]{1,0:T(8,128)(2,1)S(1)} %fetch_body.1), channel_id=1, source_target_pairs={{0,2},{2,0},{1,3},{3,1},{4,6},{6,4},{5,7},{7,5},{8,10},{10,8},{9,1... | collective-permute-start | bytes 1572872 | tf_op jit(solution)/shard_map/ppermute | solution.py:350
  15.7 2.8 %local_body.1 = (bf16[256,512]{1,0:T(8,128)(2,1)S(1)}, bf16[512,2048]{1,0:T(8,128)(2,1)S(1)}, bf16[1024,256]{1,0:T(8,128)(2,1)S(1)}, f32[256,512]{1,0:T(8,128)S(1)}, f32[256,512]{1,0:T(8,128)S(1)}) custom-call(bf16[256,512]{1,0:T(8,128)(2,1)} %bitcast.11, bf16[256,512]{1,0:T(8,128)(2,1)S(1)} %get-tuple-element.45.key_ref, ...), custom_call_target="tpu_custom_call" | custom-call | flops 671088640 | bytes 6291456 | tf_op jit(solution)/shard_map/local_body/pallas_call | solution.py:351
  18.5 1.4 %forward_body.1 = (bf16[512,128]{1,0:T(8,128)(2,1)S(1)}, bf16[128,512]{1,0:T(8,128)(2,1)S(1)}, bf16[128,1536]{1,0:T(8,128)(2,1)S(1)}, bf16[256,512]{1,0:T(8,128)...) custom-call(f32[8,128]{1,0:T(8,128)S(1)} %get-tuple-element.44.number_ref, ...), custom_call_target="tpu_custom_call" | custom-call | flops 335544320 | bytes 4194304 | tf_op jit(solution)/shard_map/forward_body/pallas_call | solution.py:358
  19.9 0.5 %collective-permute-start.8 = (bf16[128,1536]{1,0:T(8,128)(2,1)S(1)}, bf16[128,1536]{1,0:T(8,128)(2,1)S(1)}, u32[]{:S(2)}, u32[]{:S(2)}) collective-permute-start(bf16[128,1536]{1,0:T(8,128)(2,1)S(1)} %get-tuple-element.67), channel_id=1, source_target_pairs={{0,2},{2,0},{1,3},{3,1},{4,6},{6,4},{5,7},{7,5},{8,10},{10,8},{9,1... | collective-permute-start | bytes 1179656 | tf_op jit(solution)/shard_map/ppermute | solution.py:366
  20.4 2.5 %collective-permute-start.4 = (bf16[528,128]{1,0:T(8,128)(2,1)S(1)}, bf16[528,128]{1,0:T(8,128)(2,1)S(1)}, u32[]{:S(2)}, u32[]{:S(2)}) collective-permute-start(bf16[528,128]{1,0:T(8,128)(2,1)S(1)} %get-tuple-element.57.own_ref), channel_id=1, source_target_pairs={{0,4},{1,5},{4,0},{5,1},{8,12},{9,13},{12,8},{13,9},{16,20},{17,21... | collective-permute-start | bytes 405512 | tf_op jit(solution)/shard_map/ppermute | solution.py:54
  22.9 4.1 %collective-permute-done.4.pair_ref.refs_0_ = bf16[528,128]{1,0:T(8,128)(2,1)S(1)} collective-permute-done((bf16[528,128]{1,0:T(8,128)(2,1)S(1)}, bf16[528,128]{1,0:T(8,128)(2,1)S(1)}, u32[]{:S(2)}, u32[]{:S(2)}) %collective-permute-start.4) | collective-permute-done | bytes 135200 | tf_op jit(solution)/shard_map/ppermute | solution.py:54
  27.0 0.1 pair_body.3
  27.1 1.5 %collective-permute-start.5 = (bf16[528,128]{1,0:T(8,128)(2,1)S(1)}, bf16[528,128]{1,0:T(8,128)(2,1)S(1)}, u32[]{:S(2)}, u32[]{:S(2)}) collective-permute-start(bf16[528,128]{1,0:T(8,128)(2,1)S(1)} %get-tuple-element.59.own_ref), channel_id=1, source_target_pairs={{0,8},{1,9},{4,12},{5,13},{8,0},{9,1},{12,4},{13,5},{16,24},{17,25... | collective-permute-start | bytes 405512 | tf_op jit(solution)/shard_map/ppermute | solution.py:54
  28.6 6.2 %collective-permute-start.10 = (f32[4,128]{1,0:T(4,128)S(1)}, f32[4,128]{1,0:T(4,128)S(1)}, u32[]{:S(2)}, u32[]{:S(2)}) collective-permute-start(f32[4,128]{1,0:T(4,128)S(1)} %get-tuple-element.70), channel_id=1, source_target_pairs={{0,24},{1,25},{4,28},{5,29},{8,16},{9,17},{12,20},{13,21},{16,8},{... | collective-permute-start | bytes 6152 | tf_op jit(solution)/shard_map/ppermute | solution.py:72
  34.8 1.9 %backward_body.1 = (bf16[256,512]{1,0:T(8,128)(2,1)}, f32[256,512]{1,0:T(8,128)S(1)}, f32[256,512]{1,0:T(8,128)S(1)}) custom-call(bf16[256,512]{1,0:T(8,128)(2,1)S(1)} %get-tuple-element.47.query_ref, bf16[256,512]{1,0:T(8,128)(2,1)S(1)} %get-tuple-element.45.key_ref, bf16[256,512]{1,0:T(8,128)(2,1)S(1)} %get-tuple-element.46.value_ref, ...), custom_call_target="tpu_custom_call" | custom-call | bytes 65536 | tf_op jit(solution)/shard_map/backward_body/pallas_call | solution.py:367
  36.8 0.2 collective-permute-done.8.took_ref
  37.0 2.4 %collective-permute-done.9.far_ref = f32[4,128]{1,0:T(4,128)S(1)} collective-permute-done((f32[4,128]{1,0:T(4,128)S(1)}, f32[4,128]{1,0:T(4,128)S(1)}, u32[]{:S(2)}, u32[]{:S(2)}) %collective-permute-start.9) | collective-permute-done | bytes 2080 | tf_op jit(solution)/shard_map/ppermute | solution.py:72
  39.3 0.1 collective-permute-start.12
  39.4 0.5 %collective-permute-start.13 = (f32[4,128]{1,0:T(4,128)S(1)}, f32[4,128]{1,0:T(4,128)S(1)}, u32[]{:S(2)}, u32[]{:S(2)}) collective-permute-start(f32[4,128]{1,0:T(4,128)S(1)} %gain_body.1.refs_0_), channel_id=1, source_target_pairs={{0,1},{1,0},{4,5},{5,4},{8,9},{9,8},{12,13},{13,12},{16,17},{17,16... | collective-permute-start | bytes 6152 | tf_op jit(solution)/shard_map/ppermute | solution.py:72
  39.9 1.1 %last_body.1 = (bf16[256,512]{1,0:T(8,128)(2,1)}, bf16[256,512]{1,0:T(8,128)(2,1)}) custom-call(f32[8,128]{1,0:T(8,128)S(1)} %get-tuple-element.44.number_ref, bf16[256,512]{1,0:T(8,128)(2,1)S(1)} %get-tuple-element.45.key_ref, bf16[256,512]{1,0:T(8,128)(2,1)S(1)} %get-tuple-element.46.value_ref, f32[256,512]{1,0:T(8,128)S(1)} %get-tuple-element.75.key_part_ref, ...), custom_call_target="tpu_custom_call" | custom-call | flops 67108864 | bytes 3145728 | tf_op jit(solution)/shard_map/last_body/pallas_call | solution.py:382
  41.0 0.3 collective-permute-done.13.refs_1_
  41.3 1.4 %layer_body.1 = (bf16[128,2048]{1,0:T(8,128)(2,1)}, f32[4,128]{1,0:T(4,128)}) custom-call(bf16[128,512]{1,0:T(8,128)(2,1)S(1)} %get-tuple-element.56.keep_ref, bf16[512,2048]{1,0:T(8,128)(2,1)S(1)} %get-tuple-element.50.w_ref, bf16[128,1536]{1,0:T(8,128)(2,1)S(1)} %collective-permute-done.8.took_ref, bf16[256,1024]{1,0:T(8,128)(2,1)S(1)} %collective-permute-done.11.mine_ref, ...), custom_call_target="tpu_custom_call" | custom-call | flops 536870912 | bytes 6291456 | tf_op jit(solution)/shard_map/layer_body/pallas_call | solution.py:387
  (16 shorter events, 0.0 us)
Async XLA Ops:
  2.6 7.0 %collective-permute-start = (bf16[528,128]{1,0:T(8,128)(2,1)S(1)}, bf16[528,128]{1,0:T(8,128)(2,1)S(1)}, u32[]{:S(2)}, u32[]{:S(2)}) collective-permute-start(bf16[528,128]{1,0:T(8,128)(2,1)S(1)} %get-tuple-element.51.own_ref), channel_id=1, source_target_pairs={{0,4},{1,5},{4,0},{5,1},{8,12},{9,13},{12,8},{13,9},{16,20},{17,21... | collective-permute-start | bytes 405512 | tf_op jit(solution)/shard_map/ppermute | solution.py:54
  5.6 12.9 %collective-permute-start.3 = (bf16[528,128]{1,0:T(8,128)(2,1)S(1)}, bf16[528,128]{1,0:T(8,128)(2,1)S(1)}, u32[]{:S(2)}, u32[]{:S(2)}) collective-permute-start(bf16[528,128]{1,0:T(8,128)(2,1)S(1)} %get-tuple-element.51.own_ref), channel_id=1, source_target_pairs={{0,1},{1,0},{4,16},{5,17},{8,9},{9,8},{12,24},{13,25},{16,4},{17,5... | collective-permute-start | bytes 405512 | tf_op jit(solution)/shard_map/ppermute | solution.py:54
  9.7 8.9 %collective-permute-start.1 = (bf16[528,128]{1,0:T(8,128)(2,1)S(1)}, bf16[528,128]{1,0:T(8,128)(2,1)S(1)}, u32[]{:S(2)}, u32[]{:S(2)}) collective-permute-start(bf16[528,128]{1,0:T(8,128)(2,1)S(1)} %pair_body.2), channel_id=1, source_target_pairs={{0,8},{1,9},{4,12},{5,13},{8,0},{9,1},{12,4},{13,5},{16,24},{17,25... | collective-permute-start | bytes 405512 | tf_op jit(solution)/shard_map/ppermute | solution.py:54
  13.1 5.5 %collective-permute-start.2 = (bf16[528,128]{1,0:T(8,128)(2,1)S(1)}, bf16[528,128]{1,0:T(8,128)(2,1)S(1)}, u32[]{:S(2)}, u32[]{:S(2)}) collective-permute-start(bf16[528,128]{1,0:T(8,128)(2,1)S(1)} %pair_body.2), channel_id=1, source_target_pairs={{0,1},{1,0},{4,5},{5,4},{8,16},{9,17},{12,20},{13,21},{16,8},{17,9... | collective-permute-start | bytes 405512 | tf_op jit(solution)/shard_map/ppermute | solution.py:54
  14.1 4.4 %copy-start = (f32[4,128]{1,0:T(4,128)S(1)}, f32[4,128]{1,0:T(4,128)}, u32[]{:S(2)}) copy-start(f32[4,128]{1,0:T(4,128)} %gain_ref.1) | copy-start | bytes 6148
  14.1 25.2 %collective-permute-start.11 = (bf16[256,1024]{1,0:T(8,128)(2,1)S(1)}, bf16[256,1024]{1,0:T(8,128)(2,1)S(1)}, u32[]{:S(2)}, u32[]{:S(2)}) collective-permute-start(bf16[256,1024]{1,0:T(8,128)(2,1)S(1)} %fetch_body.1), channel_id=1, source_target_pairs={{0,2},{2,0},{1,3},{3,1},{4,6},{6,4},{5,7},{7,5},{8,10},{10,8},{9,1... | collective-permute-start | bytes 1572872 | tf_op jit(solution)/shard_map/ppermute | solution.py:350
  19.9 17.0 %collective-permute-start.8 = (bf16[128,1536]{1,0:T(8,128)(2,1)S(1)}, bf16[128,1536]{1,0:T(8,128)(2,1)S(1)}, u32[]{:S(2)}, u32[]{:S(2)}) collective-permute-start(bf16[128,1536]{1,0:T(8,128)(2,1)S(1)} %get-tuple-element.67), channel_id=1, source_target_pairs={{0,2},{2,0},{1,3},{3,1},{4,6},{6,4},{5,7},{7,5},{8,10},{10,8},{9,1... | collective-permute-start | bytes 1179656 | tf_op jit(solution)/shard_map/ppermute | solution.py:366
  20.4 6.6 %collective-permute-start.4 = (bf16[528,128]{1,0:T(8,128)(2,1)S(1)}, bf16[528,128]{1,0:T(8,128)(2,1)S(1)}, u32[]{:S(2)}, u32[]{:S(2)}) collective-permute-start(bf16[528,128]{1,0:T(8,128)(2,1)S(1)} %get-tuple-element.57.own_ref), channel_id=1, source_target_pairs={{0,4},{1,5},{4,0},{5,1},{8,12},{9,13},{12,8},{13,9},{16,20},{17,21... | collective-permute-start | bytes 405512 | tf_op jit(solution)/shard_map/ppermute | solution.py:54
  22.9 5.7 %collective-permute-start.7 = (bf16[528,128]{1,0:T(8,128)(2,1)S(1)}, bf16[528,128]{1,0:T(8,128)(2,1)S(1)}, u32[]{:S(2)}, u32[]{:S(2)}) collective-permute-start(bf16[528,128]{1,0:T(8,128)(2,1)S(1)} %get-tuple-element.57.own_ref), channel_id=1, source_target_pairs={{0,1},{1,0},{4,16},{5,17},{8,9},{9,8},{12,24},{13,25},{16,4},{17,5... | collective-permute-start | bytes 405512 | tf_op jit(solution)/shard_map/ppermute | solution.py:54
  27.1 7.8 %collective-permute-start.5 = (bf16[528,128]{1,0:T(8,128)(2,1)S(1)}, bf16[528,128]{1,0:T(8,128)(2,1)S(1)}, u32[]{:S(2)}, u32[]{:S(2)}) collective-permute-start(bf16[528,128]{1,0:T(8,128)(2,1)S(1)} %get-tuple-element.59.own_ref), channel_id=1, source_target_pairs={{0,8},{1,9},{4,12},{5,13},{8,0},{9,1},{12,4},{13,5},{16,24},{17,25... | collective-permute-start | bytes 405512 | tf_op jit(solution)/shard_map/ppermute | solution.py:54
  28.6 8.2 %collective-permute-start.6 = (bf16[528,128]{1,0:T(8,128)(2,1)S(1)}, bf16[528,128]{1,0:T(8,128)(2,1)S(1)}, u32[]{:S(2)}, u32[]{:S(2)}) collective-permute-start(bf16[528,128]{1,0:T(8,128)(2,1)S(1)} %get-tuple-element.59.own_ref), channel_id=1, source_target_pairs={{0,1},{1,0},{4,5},{5,4},{8,16},{9,17},{12,20},{13,21},{16,8},{17,9... | collective-permute-start | bytes 405512 | tf_op jit(solution)/shard_map/ppermute | solution.py:54
  28.6 8.4 %collective-permute-start.10 = (f32[4,128]{1,0:T(4,128)S(1)}, f32[4,128]{1,0:T(4,128)S(1)}, u32[]{:S(2)}, u32[]{:S(2)}) collective-permute-start(f32[4,128]{1,0:T(4,128)S(1)} %get-tuple-element.70), channel_id=1, source_target_pairs={{0,24},{1,25},{4,28},{5,29},{8,16},{9,17},{12,20},{13,21},{16,8},{... | collective-permute-start | bytes 6152 | tf_op jit(solution)/shard_map/ppermute | solution.py:72
  34.8 4.5 %collective-permute-start.9 = (f32[4,128]{1,0:T(4,128)S(1)}, f32[4,128]{1,0:T(4,128)S(1)}, u32[]{:S(2)}, u32[]{:S(2)}) collective-permute-start(f32[4,128]{1,0:T(4,128)S(1)} %get-tuple-element.70), channel_id=1, source_target_pairs={{0,16},{1,17},{4,20},{5,21},{8,24},{9,25},{12,28},{13,29},{16,0},{... | collective-permute-start | bytes 6152 | tf_op jit(solution)/shard_map/ppermute | solution.py:72
  39.3 2.0 %collective-permute-start.12 = (bf16[256,1024]{1,0:T(8,128)(2,1)S(1)}, bf16[256,1024]{1,0:T(8,128)(2,1)S(1)}, u32[]{:S(2)}, u32[]{:S(2)}) collective-permute-start(bf16[256,1024]{1,0:T(8,128)(2,1)S(1)} %collective-permute-done.11.mine_ref), channel_id=1, source_target_pairs={{0,1},{1,0},{4,5},{5,4},{8,9},{9,8},{12,13},{13,12},{16,17},{17,16... | collective-permute-start | bytes 1572872 | tf_op jit(solution)/shard_map/ppermute | solution.py:72
  39.4 1.9 %collective-permute-start.13 = (f32[4,128]{1,0:T(4,128)S(1)}, f32[4,128]{1,0:T(4,128)S(1)}, u32[]{:S(2)}, u32[]{:S(2)}) collective-permute-start(f32[4,128]{1,0:T(4,128)S(1)} %gain_body.1.refs_0_), channel_id=1, source_target_pairs={{0,1},{1,0},{4,5},{5,4},{8,9},{9,8},{12,13},{13,12},{16,17},{17,16... | collective-permute-start | bytes 6152 | tf_op jit(solution)/shard_map/ppermute | solution.py:72

commit v6 on v4

--- a/solution.py
+++ b/solution.py
@@ -13,6 +13,7 @@
 BF16 = jnp.bfloat16
 TAIL = 16
 GAIN = 4
+PARTS = 2
 
 
 def nn(a, b):
@@ -35,6 +36,7 @@
         in_specs=[pl.BlockSpec(memory_space=space[p]) for p in places],
         out_specs=[pl.BlockSpec(memory_space=pltpu.VMEM) for _ in outs],
         scratch_shapes=list(scratch),
+        name=getattr(body, "func", body).__name__,
         cost_estimate=pl.CostEstimate(flops=flops, bytes_accessed=moved, transcendentals=0),
         compiler_params=pltpu.CompilerParams(vmem_limit_bytes=40 << 20),
     )
@@ -202,7 +204,9 @@
 def forward_body(
     heads, dim, distance, number_ref, query_ref, within_ref, normed_grad_ref, gain_ref, w_ref, *refs
 ):
-    *sum_refs, state_ref, keep_ref, send_ref, grad_ref, outer_ref, msg_ref, gain_grad_ref, normed_ref = refs
+    *sum_refs, state_ref, keep_ref = refs[: -5 - PARTS]
+    send_refs = refs[-5 - PARTS : -5]
+    grad_ref, outer_ref, msg_ref, gain_grad_ref, normed_ref = refs[-5:]
     half = keep_ref.shape[0]
     number = number_ref[:1, :]
     state_ref[...] = total(sum_refs, number, distance, True).astype(BF16)
@@ -226,15 +230,17 @@
     put_tail(msg_ref, number, gain_grad_ref[...])
     head = lax.axis_index("head")
     keep_ref[...] = normed_ref[pl.ds(pl.multiple_of(head * half, half), half), :]
-    send_ref[...] = nn(
-        normed_ref[pl.ds(pl.multiple_of((1 - head) * half, half), half), :], w_ref[...]
-    ).astype(BF16)
+    give = normed_ref[pl.ds(pl.multiple_of((1 - head) * half, half), half), :]
+    width = send_refs[0].shape[1]
+    for i, send_ref in enumerate(send_refs):
+        send_ref[...] = nn(give, w_ref[:, i * width : (i + 1) * width]).astype(BF16)
 
 
 def backward_body(
-    heads, dim, query_ref, key_ref, value_ref, weight_ref, grad_ref, state_ref,
-    query_grad_ref, key_part_ref, value_part_ref,
-):
+    heads, dim, query_ref, key_ref, value_ref, weight_ref, grad_ref, state_ref, keep_ref, w_ref,
+    query_grad_ref, key_part_ref, value_part_ref, own_ref,
+):
+    own_ref[...] = nn(keep_ref[...], w_ref[...])
     tokens = query_ref.shape[0]
     causal = lax.broadcasted_iota(jnp.int32, (tokens, tokens), 0) >= lax.broadcasted_iota(
         jnp.int32, (tokens, tokens), 1
@@ -266,13 +272,16 @@
         ).astype(BF16)
 
 
-def layer_body(scale, keep_ref, w_ref, got_ref, *refs):
-    *gain_refs, out_ref, gain_grad_ref = refs
-    out_ref[...] = (nn(keep_ref[...], w_ref[...]) + got_ref[...].astype(F32)).astype(BF16)
-    parts = [ref[...] for ref in gain_refs]
-    if len(parts) == 4:
-        parts = [(parts[0] + parts[1]) + (parts[2] + parts[3])]
-    gain_grad_ref[...] = parts[0] * scale
+def layer_body(own_ref, *refs):
+    *got_refs, out_ref = refs
+    width = got_refs[0].shape[1]
+    for i, got_ref in enumerate(got_refs):
+        at = slice(i * width, (i + 1) * width)
+        out_ref[:, at] = (own_ref[:, at] + got_ref[...].astype(F32)).astype(BF16)
+
+
+def add_body(scale, one_ref, other_ref, out_ref):
+    out_ref[...] = (one_ref[...] + other_ref[...]) * scale
 
 
 def on_device(queries, key_rows, value_rows, stretch_doc, head_gain, w_out, cotangent):
@@ -291,10 +300,13 @@
     last = distances[-1]
     gains = size & (size - 1) == 0 and len(distances) > 1
 
+    beside = []
+
     def spread(outer, msg, forward):
         carry = gains and not forward
         if last == 2:
             pair = exchange(msg, blocks(size, 1, 0))
+            pair, beside[0] = lax.optimization_barrier((pair, beside[0]))
             far = exchange(msg, [(i, i + 3) for i in range(1, size - 3, 2)])
             (msg,) = call(
                 functools.partial(pair_body, forward, carry), [(message, BF16)], "vvvv", flops=0, moved=1 << 20
@@ -323,37 +335,44 @@
         "hvvhh", flops=2 * square + 2 * layer, moved=6 << 20,
         scratch=[pltpu.VMEM((tokens, model), BF16), pltpu.SemaphoreType.DMA((3,))],
     )(in_hbm(queries[0]), key, value, in_hbm(cotangent[0]), in_hbm(w_out))
+    beside.append(within)
     sums, _ = spread(outer, msg, True)
-    state, keep, send, grad, outer, msg, gain_part = call(
+    (within,) = beside
+    state, keep, *send, grad, outer, msg, gain_part = call(
         functools.partial(forward_body, heads, dim, last),
         [
-            (summed, BF16), ((tokens // 2, width), BF16), (half, BF16),
+            (summed, BF16), ((tokens // 2, width), BF16), *[((tokens // 2, model // PARTS), BF16)] * PARTS,
             (rows, BF16), (summed, F32), (message, BF16), (small, F32),
         ],
         "vvvvvv" + "v" * len(sums), flops=2 * matrix + layer, moved=4 << 20, scratch=[pltpu.VMEM(rows, BF16)],
     )(number, query, within, normed_grad, head_gain, w, *sums)
-    got = lax.ppermute(send, "head", [(0, 1), (1, 0)])
-    query_grad, key_part, value_part = call(
+    got = [lax.ppermute(part, "head", [(0, 1), (1, 0)]) for part in send]
+    query_grad, key_part, value_part, own = call(
         functools.partial(backward_body, heads, dim),
-        [(rows, BF16), (rows, F32), (rows, F32)],
-        "vvvvvv", flops=0, moved=1 << 16,
-    )(query, key, value, weights, grad, state)
+        [(rows, BF16), (rows, F32), (rows, F32), (half, F32)],
+        "vvvvvvvv", flops=0, moved=1 << 16,
+    )(query, key, value, weights, grad, state, keep, w)
+    beside[0] = key_part
     sums, msg = spread(outer, msg, False)
+    (key_part,) = beside
+    scale = 1.0 / math.sqrt(size * lax.axis_size("dp") * tokens)
+    add = lambda scale, *gain: call(
+        functools.partial(add_body, scale), [(small, F32)], "vv", flops=0, moved=1 << 16
+    )(*gain)[0]
     if gains:
         (gain,) = call(gain_body, [(small, F32)], "vv", flops=0, moved=1 << 16)(msg, sums[-2])
-        across = [flipped(gain, *to) for to in ((0, 1), (size // 2, 0), (size // 2, 1))]
-        gain_parts = [gain, *across]
-    else:
-        gain_parts = [lax.psum(gain_part, ("seq", "dp"))]
+        far = flipped(gain, size // 2, 0)
     key_grad, value_grad = call(
         functools.partial(last_body, heads, dim, last), [(rows, BF16), (rows, BF16)],
         "vvvvv" + "v" * len(sums), flops=2 * matrix, moved=3 << 20,
     )(number, key, value, key_part, value_part, *sums)
-    scale = 1.0 / math.sqrt(size * lax.axis_size("dp") * tokens)
-    layer_out, gain_grad = call(
-        functools.partial(layer_body, scale), [(half, BF16), (small, F32)],
-        "vvv" + "v" * len(gain_parts), flops=layer, moved=6 << 20,
-    )(keep, w, got, *gain_parts)
+    if gains:
+        far, key_grad = lax.optimization_barrier((far, key_grad))
+        gain = add(1.0, gain, far)
+        gain_grad = add(scale, gain, flipped(gain, 0, 1))
+    else:
+        gain_grad = lax.psum(gain_part, ("seq", "dp")) * scale
+    (layer_out,) = call(layer_body, [(half, BF16)], "v" + "v" * PARTS, flops=0, moved=2 << 20)(own, *got)
     return layer_out[None], query_grad[None], key_grad[None], value_grad[None], gain_grad
 
 

time: 38.2 us -> 38.5 us (level)
  starting transfers between devices: 16.1 us -> 13 us
  waiting for transfers between devices: 10.7 us -> 13.7 us
  Pallas kernels: 9.86 us -> 10.4 us
    ppermute x3 -> x2, waiting for transfers between devices: 0.69 us -> 3.45 us  [flipped(): return lax.ppermute(block, ('seq', 'dp'), route)]
    ppermute x3 -> x2, starting transfers between devices: 2.75 us -> 0.17 us  [flipped(): return lax.ppermute(block, ('seq', 'dp'), route)]
    ppermute x8, starting transfers between devices: 11.8 us -> 10.8 us  [exchange(): lax.ppermute(block, ('seq', 'dp'), pairing(lax.axis_size('seq'), pairs))]
    ppermute x1 -> x2, starting transfers between devices: 1.54 us -> 2.03 us  [on_device(): got = [lax.ppermute(part, 'head', [(0, 1), (1, 0)]) for part in send]]
    pallas_call x1 -> x3, Pallas kernels: 1.25 us -> 1.49 us  [the longest x1 0.91 us: on_device(): call(layer_body, [(half, BF16)], 'v' + 'v' * PARTS, flops=0, moved=2 << 20)]
  transfers between devices with their start and end apart: 12 -> 12, of which waited for: 5 -> 5; matrix products, arithmetic and copies ran while one was open for 0% -> 0% of each run, Pallas kernels for 16% -> 19%
where the time goes in v6:
time: 38.5 us; the launch traced here: 38.4 us
  waiting for transfers between devices  13.7 us (36%)
  starting transfers between devices  13 us (34%)
  Pallas kernels  10.4 us (27%)
  between operations  1.33 us (3%)
    ppermute x8, starting transfers between devices, exchange(): lax.ppermute(block, ('seq', 'dp'), pairing(lax.axis_size('seq'), pairs))  10.8 us
    ppermute x8, waiting for transfers between devices, exchange(): lax.ppermute(block, ('seq', 'dp'), pairing(lax.axis_size('seq'), pairs))  10.2 us
    ppermute x2, waiting for transfers between devices, flipped(): return lax.ppermute(block, ('seq', 'dp'), route)  3.45 us
    pallas_call x1, Pallas kernels, on_device(): call(functools.partial(local_body, heads, dim), [(rows, BF16), ((width, m...  2.79 us
    pallas_call x1, Pallas kernels, on_device(): call(functools.partial(backward_body, heads, dim), [(rows, BF16), (rows,...  2.22 us
    ppermute x2, starting transfers between devices, on_device(): got = [lax.ppermute(part, 'head', [(0, 1), (1, 0)]) for part in send]  2.03 us
    pallas_call x1, Pallas kernels, on_device(): call(functools.partial(opening_body, heads, dim), [(rows, BF16)] * 2 + [(...  1.33 us
    pallas_call x1, Pallas kernels, on_device(): call(functools.partial(forward_body, heads, dim, last), [(summed, BF16),...  1.32 us
  transfers between devices with their start and end apart: 12, of which 5 were waited for; matrix products, arithmetic and copies ran while one was open for 0% of the time, Pallas kernels for 19%

profile of v6, /device:TPU:0, one launch (start us, length us, event | category | flops | bytes accessed | tf_op | source)
XLA Modules:
  0.0 38.4 jit_solution(18284107967280643793)
XLA Ops:
  1.3 1.3 %opening_body.1 = (bf16[256,512]{1,0:T(8,128)(2,1)S(1)}, bf16[256,512]{1,0:T(8,128)(2,1)S(1)}, f32[8,128]{1,0:T(8,128)S(1)}, f32[512,128]{1,0:T(8,128)S(1)}, bf16[528,128]{1,0:T(8,128)(2,1)S(1)}) custom-call(s32[1,1]{1,0:T(1,128)S(6)} %copy.12.doc_any, bf16[256,512]{1,0:T(8,128)(2,1)} %bitcast.10, bf16[256,512]{1,0:T(8,128)(2,1)} %bitcast.11), custom_call_target="tpu_custom_call" | custom-call | flops 33554432 | bytes 1048576 | tf_op jit(solution)/shard_map/opening_body/pallas_call | solution.py:327
  2.6 3.0 %collective-permute-start = (bf16[528,128]{1,0:T(8,128)(2,1)S(1)}, bf16[528,128]{1,0:T(8,128)(2,1)S(1)}, u32[]{:S(2)}, u32[]{:S(2)}) collective-permute-start(bf16[528,128]{1,0:T(8,128)(2,1)S(1)} %get-tuple-element.43.own_ref), channel_id=1, source_target_pairs={{0,4},{1,5},{4,0},{5,1},{8,12},{9,13},{12,8},{13,9},{16,20},{17,21... | collective-permute-start | bytes 405512 | tf_op jit(solution)/shard_map/ppermute | solution.py:55
  5.6 2.8 %local_body.1 = (bf16[256,512]{1,0:T(8,128)(2,1)S(1)}, bf16[512,2048]{1,0:T(8,128)(2,1)S(1)}, bf16[1024,256]{1,0:T(8,128)(2,1)S(1)}, f32[256,512]{1,0:T(8,128)S(1)}, f32[256,512]{1,0:T(8,128)S(1)}) custom-call(bf16[256,512]{1,0:T(8,128)(2,1)} %bitcast.12, bf16[256,512]{1,0:T(8,128)(2,1)S(1)} %get-tuple-element.38.key_ref, ...), custom_call_target="tpu_custom_call" | custom-call | flops 671088640 | bytes 6291456 | tf_op jit(solution)/shard_map/local_body/pallas_call | solution.py:332
  8.4 1.2 %collective-permute-done.pair_ref.refs_0_ = bf16[528,128]{1,0:T(8,128)(2,1)S(1)} collective-permute-done((bf16[528,128]{1,0:T(8,128)(2,1)S(1)}, bf16[528,128]{1,0:T(8,128)(2,1)S(1)}, u32[]{:S(2)}, u32[]{:S(2)}) %collective-permute-start) | collective-permute-done | bytes 135200 | tf_op jit(solution)/shard_map/ppermute | solution.py:55
  9.6 0.1 pair_body.2
  9.7 3.4 %collective-permute-start.1 = (bf16[528,128]{1,0:T(8,128)(2,1)S(1)}, bf16[528,128]{1,0:T(8,128)(2,1)S(1)}, u32[]{:S(2)}, u32[]{:S(2)}) collective-permute-start(bf16[528,128]{1,0:T(8,128)(2,1)S(1)} %pair_body.2), channel_id=1, source_target_pairs={{0,8},{1,9},{4,12},{5,13},{8,0},{9,1},{12,4},{13,5},{16,24},{17,25... | collective-permute-start | bytes 405512 | tf_op jit(solution)/shard_map/ppermute | solution.py:55
  13.1 0.0 collective-permute-start.3
  13.1 0.0 collective-permute-done.2.refs_1_
  13.1 3.5 %collective-permute-done.1.refs_2_ = bf16[528,128]{1,0:T(8,128)(2,1)S(1)} collective-permute-done((bf16[528,128]{1,0:T(8,128)(2,1)S(1)}, bf16[528,128]{1,0:T(8,128)(2,1)S(1)}, u32[]{:S(2)}, u32[]{:S(2)}) %collective-permute-start.1) | collective-permute-done | bytes 135200 | tf_op jit(solution)/shard_map/ppermute | solution.py:55
  16.5 1.3 %forward_body.1 = (bf16[512,128]{1,0:T(8,128)(2,1)S(1)}, bf16[128,512]{1,0:T(8,128)(2,1)S(1)}, bf16[128,1024]{1,0:T(8,128)(2,1)S(1)}, bf16[128,1024]{1,0:T(8,128...) custom-call(f32[8,128]{1,0:T(8,128)S(1)} %get-tuple-element.42.numbe, ...), custom_call_target="tpu_custom_call" | custom-call | flops 335544320 | bytes 4194304 | tf_op jit(solution)/shard_map/forward_body/pallas_call | solution.py:341
  17.8 2.0 %collective-permute-start.6 = (bf16[528,128]{1,0:T(8,128)(2,1)S(1)}, bf16[528,128]{1,0:T(8,128)(2,1)S(1)}, u32[]{:S(2)}, u32[]{:S(2)}) collective-permute-start(bf16[528,128]{1,0:T(8,128)(2,1)S(1)} %get-tuple-element.60.own_ref), channel_id=1, source_target_pairs={{0,4},{1,5},{4,0},{5,1},{8,12},{9,13},{12,8},{13,9},{16,20},{17,21... | collective-permute-start | bytes 405512 | tf_op jit(solution)/shard_map/ppermute | solution.py:55
  19.9 1.5 %collective-permute-start.4 = (bf16[128,1024]{1,0:T(8,128)(2,1)S(1)}, bf16[128,1024]{1,0:T(8,128)(2,1)S(1)}, u32[]{:S(2)}, u32[]{:S(2)}) collective-permute-start(bf16[128,1024]{1,0:T(8,128)(2,1)S(1)} %get-tuple-element.56), channel_id=1, source_target_pairs={{0,2},{2,0},{1,3},{3,1},{4,6},{6,4},{5,7},{7,5},{8,10},{10,8},{9,1... | collective-permute-start | bytes 786440 | tf_op jit(solution)/shard_map/ppermute | solution.py:349
  21.4 0.5 %collective-permute-start.5 = (bf16[128,1024]{1,0:T(8,128)(2,1)S(1)}, bf16[128,1024]{1,0:T(8,128)(2,1)S(1)}, u32[]{:S(2)}, u32[]{:S(2)}) collective-permute-start(bf16[128,1024]{1,0:T(8,128)(2,1)S(1)} %get-tuple-element.57), channel_id=1, source_target_pairs={{0,2},{2,0},{1,3},{3,1},{4,6},{6,4},{5,7},{7,5},{8,10},{10,8},{9,1... | collective-permute-start | bytes 786440 | tf_op jit(solution)/shard_map/ppermute | solution.py:349
  21.9 2.2 %backward_body.1 = (bf16[256,512]{1,0:T(8,128)(2,1)}, f32[256,512]{1,0:T(8,128)S(1)}, f32[256,512]{1,0:T(8,128)S(1)}, f32[128,2048]{1,0:T(8,128)S(1)}) custom-call(bf16[256,512]{1,0:T(8,128)(2,1)S(1)} %get-tuple-element.40.query_ref, bf16[256,512]{1,0:T(8,128)(2,1)S(1)} %get-tuple-element.38.key_ref, bf16[256,512]{1,0:T(8,128)(2,1)S(1)} %get-tuple-element.39.value_ref, ...), custom_call_target="tpu_custom_call" | custom-call | bytes 65536 | tf_op jit(solution)/shard_map/backward_body/pallas_call | solution.py:350
  24.1 0.1 pair_body.3.own_ref
  24.2 2.2 %collective-permute-start.7 = (bf16[528,128]{1,0:T(8,128)(2,1)S(1)}, bf16[528,128]{1,0:T(8,128)(2,1)S(1)}, u32[]{:S(2)}, u32[]{:S(2)}) collective-permute-start(bf16[528,128]{1,0:T(8,128)(2,1)S(1)} %pair_body.3.own_ref), channel_id=1, source_target_pairs={{0,8},{1,9},{4,12},{5,13},{8,0},{9,1},{12,4},{13,5},{16,24},{17,25... | collective-permute-start | bytes 405512 | tf_op jit(solution)/shard_map/ppermute | solution.py:55
  26.3 0.2 collective-permute-start.10
  26.6 5.6 %collective-permute-done.7.other_ref.refs_2_ = bf16[528,128]{1,0:T(8,128)(2,1)S(1)} collective-permute-done((bf16[528,128]{1,0:T(8,128)(2,1)S(1)}, bf16[528,128]{1,0:T(8,128)(2,1)S(1)}, u32[]{:S(2)}, u32[]{:S(2)}) %collective-permute-start.7) | collective-permute-done | bytes 135200 | tf_op jit(solution)/shard_map/ppermute | solution.py:55
  32.1 0.2 collective-permute-start.9
  32.3 1.1 %last_body.1 = (bf16[256,512]{1,0:T(8,128)(2,1)}, bf16[256,512]{1,0:T(8,128)(2,1)}) custom-call(f32[8,128]{1,0:T(8,128)S(1)} %get-tuple-element.42.number_ref, bf16[256,512]{1,0:T(8,128)(2,1)S(1)} %get-tuple-element.38.key_ref, bf16[256,512]{1,0:T(8,128)(2,1)S(1)} %get-tuple-element.39.value_ref, f32[256,512]{1,0:T(8,128)S(1)} %get-tuple-element.64.key_part_ref, ...), custom_call_target="tpu_custom_call" | custom-call | flops 67108864 | bytes 3145728 | tf_op jit(solution)/shard_map/last_body/pallas_call | solution.py:365
  33.4 3.2 %collective-permute-done.9.other_ref = f32[4,128]{1,0:T(4,128)S(1)} collective-permute-done((f32[4,128]{1,0:T(4,128)S(1)}, f32[4,128]{1,0:T(4,128)S(1)}, u32[]{:S(2)}, u32[]{:S(2)}) %collective-permute-start.9) | collective-permute-done | bytes 2080 | tf_op jit(solution)/shard_map/ppermute | solution.py:73
  36.7 0.9 %layer_body.1 = bf16[128,2048]{1,0:T(8,128)(2,1)} custom-call(f32[128,2048]{1,0:T(8,128)S(1)} %get-tuple-element.55.own_ref, bf16[128,1024]{1,0:T(8,128)(2,1)S(1)} %collective-permute-done.4.refs_0_, bf16[128,1024]{1,0:T(8,128)(2,1)S(1)} %collective-permute-done.5.refs_1_), custom_call_target="tpu_custom_call" | custom-call | bytes 2097152 | tf_op jit(solution)/shard_map/layer_body/pallas_call | solution.py:375
  37.6 0.2 collective-permute-done.11.other_ref
  37.8 0.6 %add_body.3 = f32[4,128]{1,0:T(4,128)} custom-call(f32[4,128]{1,0:T(4,128)S(1)} %add_body.2.one_ref, f32[4,128]{1,0:T(4,128)S(1)} %collective-permute-done.11.other_ref), custom_call_target="tpu_custom_call" | custom-call | bytes 65536 | tf_op jit(solution)/shard_map/add_body/pallas_call | solution.py:359
  (13 shorter events, 0.0 us)
Async XLA Ops:
  2.6 7.0 %collective-permute-start = (bf16[528,128]{1,0:T(8,128)(2,1)S(1)}, bf16[528,128]{1,0:T(8,128)(2,1)S(1)}, u32[]{:S(2)}, u32[]{:S(2)}) collective-permute-start(bf16[528,128]{1,0:T(8,128)(2,1)S(1)} %get-tuple-element.43.own_ref), channel_id=1, source_target_pairs={{0,4},{1,5},{4,0},{5,1},{8,12},{9,13},{12,8},{13,9},{16,20},{17,21... | collective-permute-start | bytes 405512 | tf_op jit(solution)/shard_map/ppermute | solution.py:55
  5.6 7.4 %collective-permute-start.2 = (bf16[528,128]{1,0:T(8,128)(2,1)S(1)}, bf16[528,128]{1,0:T(8,128)(2,1)S(1)}, u32[]{:S(2)}, u32[]{:S(2)}) collective-permute-start(bf16[528,128]{1,0:T(8,128)(2,1)S(1)} %get-tuple-element.43.own_ref), channel_id=1, source_target_pairs={{0,1},{1,0},{4,16},{5,17},{8,9},{9,8},{12,24},{13,25},{16,4},{17,5... | collective-permute-start | bytes 405512 | tf_op jit(solution)/shard_map/ppermute | solution.py:55
  5.6 10.9 %copy-start = (f32[4,128]{1,0:T(4,128)S(1)}, f32[4,128]{1,0:T(4,128)}, u32[]{:S(2)}) copy-start(f32[4,128]{1,0:T(4,128)} %gain_ref.1) | copy-start | bytes 6148
  9.7 6.9 %collective-permute-start.1 = (bf16[528,128]{1,0:T(8,128)(2,1)S(1)}, bf16[528,128]{1,0:T(8,128)(2,1)S(1)}, u32[]{:S(2)}, u32[]{:S(2)}) collective-permute-start(bf16[528,128]{1,0:T(8,128)(2,1)S(1)} %pair_body.2), channel_id=1, source_target_pairs={{0,8},{1,9},{4,12},{5,13},{8,0},{9,1},{12,4},{13,5},{16,24},{17,25... | collective-permute-start | bytes 405512 | tf_op jit(solution)/shard_map/ppermute | solution.py:55
  13.1 3.5 %collective-permute-start.3 = (bf16[528,128]{1,0:T(8,128)(2,1)S(1)}, bf16[528,128]{1,0:T(8,128)(2,1)S(1)}, u32[]{:S(2)}, u32[]{:S(2)}) collective-permute-start(bf16[528,128]{1,0:T(8,128)(2,1)S(1)} %pair_body.2), channel_id=1, source_target_pairs={{0,1},{1,0},{4,5},{5,4},{8,16},{9,17},{12,20},{13,21},{16,8},{17,9... | collective-permute-start | bytes 405512 | tf_op jit(solution)/shard_map/ppermute | solution.py:55
  17.8 6.3 %collective-permute-start.6 = (bf16[528,128]{1,0:T(8,128)(2,1)S(1)}, bf16[528,128]{1,0:T(8,128)(2,1)S(1)}, u32[]{:S(2)}, u32[]{:S(2)}) collective-permute-start(bf16[528,128]{1,0:T(8,128)(2,1)S(1)} %get-tuple-element.60.own_ref), channel_id=1, source_target_pairs={{0,4},{1,5},{4,0},{5,1},{8,12},{9,13},{12,8},{13,9},{16,20},{17,21... | collective-permute-start | bytes 405512 | tf_op jit(solution)/shard_map/ppermute | solution.py:55
  19.9 16.8 %collective-permute-start.4 = (bf16[128,1024]{1,0:T(8,128)(2,1)S(1)}, bf16[128,1024]{1,0:T(8,128)(2,1)S(1)}, u32[]{:S(2)}, u32[]{:S(2)}) collective-permute-start(bf16[128,1024]{1,0:T(8,128)(2,1)S(1)} %get-tuple-element.56), channel_id=1, source_target_pairs={{0,2},{2,0},{1,3},{3,1},{4,6},{6,4},{5,7},{7,5},{8,10},{10,8},{9,1... | collective-permute-start | bytes 786440 | tf_op jit(solution)/shard_map/ppermute | solution.py:349
  21.4 15.3 %collective-permute-start.5 = (bf16[128,1024]{1,0:T(8,128)(2,1)S(1)}, bf16[128,1024]{1,0:T(8,128)(2,1)S(1)}, u32[]{:S(2)}, u32[]{:S(2)}) collective-permute-start(bf16[128,1024]{1,0:T(8,128)(2,1)S(1)} %get-tuple-element.57), channel_id=1, source_target_pairs={{0,2},{2,0},{1,3},{3,1},{4,6},{6,4},{5,7},{7,5},{8,10},{10,8},{9,1... | collective-permute-start | bytes 786440 | tf_op jit(solution)/shard_map/ppermute | solution.py:349
  21.9 4.7 %collective-permute-start.8 = (bf16[528,128]{1,0:T(8,128)(2,1)S(1)}, bf16[528,128]{1,0:T(8,128)(2,1)S(1)}, u32[]{:S(2)}, u32[]{:S(2)}) collective-permute-start(bf16[528,128]{1,0:T(8,128)(2,1)S(1)} %get-tuple-element.60.own_ref), channel_id=1, source_target_pairs={{0,1},{1,0},{4,16},{5,17},{8,9},{9,8},{12,24},{13,25},{16,4},{17,5... | collective-permute-start | bytes 405512 | tf_op jit(solution)/shard_map/ppermute | solution.py:55
  24.2 8.0 %collective-permute-start.7 = (bf16[528,128]{1,0:T(8,128)(2,1)S(1)}, bf16[528,128]{1,0:T(8,128)(2,1)S(1)}, u32[]{:S(2)}, u32[]{:S(2)}) collective-permute-start(bf16[528,128]{1,0:T(8,128)(2,1)S(1)} %pair_body.3.own_ref), channel_id=1, source_target_pairs={{0,8},{1,9},{4,12},{5,13},{8,0},{9,1},{12,4},{13,5},{16,24},{17,25... | collective-permute-start | bytes 405512 | tf_op jit(solution)/shard_map/ppermute | solution.py:55
  26.3 6.0 %collective-permute-start.10 = (bf16[528,128]{1,0:T(8,128)(2,1)S(1)}, bf16[528,128]{1,0:T(8,128)(2,1)S(1)}, u32[]{:S(2)}, u32[]{:S(2)}) collective-permute-start(bf16[528,128]{1,0:T(8,128)(2,1)S(1)} %pair_body.3.own_ref), channel_id=1, source_target_pairs={{0,1},{1,0},{4,5},{5,4},{8,16},{9,17},{12,20},{13,21},{16,8},{17,9... | collective-permute-start | bytes 405512 | tf_op jit(solution)/shard_map/ppermute | solution.py:55
  32.1 4.5 %collective-permute-start.9 = (f32[4,128]{1,0:T(4,128)S(1)}, f32[4,128]{1,0:T(4,128)S(1)}, u32[]{:S(2)}, u32[]{:S(2)}) collective-permute-start(f32[4,128]{1,0:T(4,128)S(1)} %gain_body.1.one_ref), channel_id=1, source_target_pairs={{0,16},{1,17},{4,20},{5,21},{8,24},{9,25},{12,28},{13,29},{16,0},{... | collective-permute-start | bytes 6152 | tf_op jit(solution)/shard_map/ppermute | solution.py:73
  36.6 1.2 %collective-permute-start.11 = (f32[4,128]{1,0:T(4,128)S(1)}, f32[4,128]{1,0:T(4,128)S(1)}, u32[]{:S(2)}, u32[]{:S(2)}) collective-permute-start(f32[4,128]{1,0:T(4,128)S(1)} %add_body.2.one_ref), channel_id=1, source_target_pairs={{0,1},{1,0},{4,5},{5,4},{8,9},{9,8},{12,13},{13,12},{16,17},{17,16... | collective-permute-start | bytes 6152 | tf_op jit(solution)/shard_map/ppermute | solution.py:73

commit v7 on v6

--- a/solution.py
+++ b/solution.py
@@ -12,8 +12,9 @@
 F32 = jnp.float32
 BF16 = jnp.bfloat16
 TAIL = 16
+TIE = (True, True)
 GAIN = 4
-PARTS = 2
+PARTS = 1
 
 
 def nn(a, b):
@@ -173,7 +174,8 @@
     return sent_gain(own_ref) + sent_gain(other_ref) if gains else None
 
 
-def pair_body(forward, gains, number_ref, sum_ref, own_ref, pair_ref, msg_ref):
+def pair_body(forward, gains, number_ref, sum_ref, own_ref, pair_ref, *refs):
+    *gain_refs, msg_ref = refs
     rows = sum_ref.shape[0]
     number = number_ref[:1, :]
     leads = lax.rem(lax.axis_index("seq"), 2) == (1 if forward else 0)
@@ -182,7 +184,10 @@
     same = theirs == number
     keep_mine, keep_theirs = same | leads, same | jnp.logical_not(leads)
     msg_ref[:rows, :] = (jnp.where(keep_mine, mine, 0.0) + jnp.where(keep_theirs, sums, 0.0)).astype(BF16)
-    put_tail(msg_ref, jnp.where(leads, number, theirs), merge_gain(gains, own_ref, pair_ref))
+    gain = merge_gain(gains, own_ref, pair_ref)
+    if gains:
+        gain = gain + (gain_refs[0][...] + gain_refs[1][...])
+    put_tail(msg_ref, jnp.where(leads, number, theirs), gain)
 
 
 def merge_body(distance, forward, gains, number_ref, sum_ref, own_ref, *refs):
@@ -227,7 +232,7 @@
         outer = tn(query, grad)
         outer_ref[rows, :] = outer
         msg_ref[rows, :] = outer.astype(BF16)
-    put_tail(msg_ref, number, gain_grad_ref[...])
+    gain_grad_ref[...] = put_tail(msg_ref, number, gain_grad_ref[...])
     head = lax.axis_index("head")
     keep_ref[...] = normed_ref[pl.ds(pl.multiple_of(head * half, half), half), :]
     give = normed_ref[pl.ds(pl.multiple_of((1 - head) * half, half), half), :]
@@ -272,16 +277,17 @@
         ).astype(BF16)
 
 
-def layer_body(own_ref, *refs):
-    *got_refs, out_ref = refs
+def layer_body(scale, own_ref, *refs):
+    got_refs, gain_refs = refs[:PARTS], refs[PARTS:-2]
+    out_ref, gain_grad_ref = refs[-2:]
     width = got_refs[0].shape[1]
     for i, got_ref in enumerate(got_refs):
         at = slice(i * width, (i + 1) * width)
         out_ref[:, at] = (own_ref[:, at] + got_ref[...].astype(F32)).astype(BF16)
-
-
-def add_body(scale, one_ref, other_ref, out_ref):
-    out_ref[...] = (one_ref[...] + other_ref[...]) * scale
+    gain = gain_refs[0][...]
+    if len(gain_refs) > 1:
+        gain = gain + gain_refs[1][...]
+    gain_grad_ref[...] = gain * scale
 
 
 def on_device(queries, key_rows, value_rows, stretch_doc, head_gain, w_out, cotangent):
@@ -298,19 +304,21 @@
     while 2 * distances[-1] - 1 < size // 2 - 1:
         distances.append(2 * distances[-1])
     last = distances[-1]
-    gains = size & (size - 1) == 0 and len(distances) > 1
+    gains = size == 8
 
     beside = []
 
-    def spread(outer, msg, forward):
-        carry = gains and not forward
+    def spread(outer, msg, forward, gain_part=None):
+        carry = gain_part is not None
         if last == 2:
             pair = exchange(msg, blocks(size, 1, 0))
-            pair, beside[0] = lax.optimization_barrier((pair, beside[0]))
             far = exchange(msg, [(i, i + 3) for i in range(1, size - 3, 2)])
+            gain = [flipped(gain_part, to, 0) for to in (size // 2, size // 2 + 1)] if carry else []
+            if TIE[0] and forward or TIE[1] and not forward:
+                pair, beside[0] = lax.optimization_barrier((pair, beside[0]))
             (msg,) = call(
-                functools.partial(pair_body, forward, carry), [(message, BF16)], "vvvv", flops=0, moved=1 << 20
-            )(number, outer, msg, pair)
+                functools.partial(pair_body, forward, carry), [(message, BF16)], "vvvv" + "v" * len(gain), flops=0, moved=1 << 20
+            )(number, outer, msg, pair, *gain)
             even, odd = swaps(msg, last)
             even, far = lax.optimization_barrier((even, far))
             return [pair, far, even, odd], msg
@@ -353,26 +361,22 @@
         "vvvvvvvv", flops=0, moved=1 << 16,
     )(query, key, value, weights, grad, state, keep, w)
     beside[0] = key_part
-    sums, msg = spread(outer, msg, False)
+    sums, msg = spread(outer, msg, False, gain_part if gains else None)
     (key_part,) = beside
     scale = 1.0 / math.sqrt(size * lax.axis_size("dp") * tokens)
-    add = lambda scale, *gain: call(
-        functools.partial(add_body, scale), [(small, F32)], "vv", flops=0, moved=1 << 16
-    )(*gain)[0]
     if gains:
         (gain,) = call(gain_body, [(small, F32)], "vv", flops=0, moved=1 << 16)(msg, sums[-2])
-        far = flipped(gain, size // 2, 0)
+        gain = [gain, flipped(gain, 0, 1)]
+    else:
+        gain = [lax.psum(gain_part, ("seq", "dp"))]
     key_grad, value_grad = call(
         functools.partial(last_body, heads, dim, last), [(rows, BF16), (rows, BF16)],
         "vvvvv" + "v" * len(sums), flops=2 * matrix, moved=3 << 20,
     )(number, key, value, key_part, value_part, *sums)
-    if gains:
-        far, key_grad = lax.optimization_barrier((far, key_grad))
-        gain = add(1.0, gain, far)
-        gain_grad = add(scale, gain, flipped(gain, 0, 1))
-    else:
-        gain_grad = lax.psum(gain_part, ("seq", "dp")) * scale
-    (layer_out,) = call(layer_body, [(half, BF16)], "v" + "v" * PARTS, flops=0, moved=2 << 20)(own, *got)
+    layer_out, gain_grad = call(
+        functools.partial(layer_body, scale), [(half, BF16), (small, F32)], "v" + "v" * (PARTS + len(gain)),
+        flops=0, moved=2 << 20,
+    )(own, *got, *gain)
     return layer_out[None], query_grad[None], key_grad[None], value_grad[None], gain_grad
 
 

time: 38.5 us -> 37.1 us (0.964)
  waiting for transfers between devices: 13.7 us -> 12.9 us
  Pallas kernels: 10.4 us -> 9.62 us
    ppermute x2 -> x3, starting transfers between devices: 0.17 us -> 2.92 us  [flipped(): return lax.ppermute(block, ('seq', 'dp'), route)]
    ppermute x8, starting transfers between devices: 10.8 us -> 8.54 us  [exchange(): lax.ppermute(block, ('seq', 'dp'), pairing(lax.axis_size('seq'), pairs))]
    pallas_call x3 -> x1, Pallas kernels: 1.49 us -> 0.91 us  [on_device(): call(functools.partial(layer_body, scale), [(half, BF16), (small, F32)],...]
    ppermute x2 -> x3, waiting for transfers between devices: 3.45 us -> 3 us  [flipped(): return lax.ppermute(block, ('seq', 'dp'), route)]
    ppermute x2 -> x1, starting transfers between devices: 2.03 us -> 1.61 us  [on_device(): got = [lax.ppermute(part, 'head', [(0, 1), (1, 0)]) for part in send]]
  transfers between devices with their start and end apart: 12 -> 12, of which waited for: 5 -> 5; matrix products, arithmetic and copies ran while one was open for 0% -> 0% of each run, Pallas kernels for 19% -> 17%
where the time goes in v7:
time: 37.1 us; the launch traced here: 36.9 us
  starting transfers between devices  13.1 us (35%)
  waiting for transfers between devices  12.9 us (35%)
  Pallas kernels  9.62 us (26%)
  between operations  1.36 us (4%)
    ppermute x8, waiting for transfers between devices, exchange(): lax.ppermute(block, ('seq', 'dp'), pairing(lax.axis_size('seq'), pairs))  9.87 us
    ppermute x8, starting transfers between devices, exchange(): lax.ppermute(block, ('seq', 'dp'), pairing(lax.axis_size('seq'), pairs))  8.54 us
    ppermute x3, waiting for transfers between devices, flipped(): return lax.ppermute(block, ('seq', 'dp'), route)  3 us
    ppermute x3, starting transfers between devices, flipped(): return lax.ppermute(block, ('seq', 'dp'), route)  2.92 us
    pallas_call x1, Pallas kernels, on_device(): call(functools.partial(local_body, heads, dim), [(rows, BF16), ((width, m...  2.79 us
    pallas_call x1, Pallas kernels, on_device(): call(functools.partial(backward_body, heads, dim), [(rows, BF16), (rows,...  2.22 us
    ppermute x1, starting transfers between devices, on_device(): got = [lax.ppermute(part, 'head', [(0, 1), (1, 0)]) for part in send]  1.61 us
    pallas_call x1, Pallas kernels, on_device(): call(functools.partial(opening_body, heads, dim), [(rows, BF16)] * 2 + [(...  1.33 us
  transfers between devices with their start and end apart: 12, of which 5 were waited for; matrix products, arithmetic and copies ran while one was open for 0% of the time, Pallas kernels for 17%

profile of v7, /device:TPU:0, one launch (start us, length us, event | category | flops | bytes accessed | tf_op | source)
XLA Modules:
  0.0 36.9 jit_solution(11717795722808146045)
XLA Ops:
  1.3 1.3 %opening_body.1 = (bf16[256,512]{1,0:T(8,128)(2,1)S(1)}, bf16[256,512]{1,0:T(8,128)(2,1)S(1)}, f32[8,128]{1,0:T(8,128)S(1)}, f32[512,128]{1,0:T(8,128)S(1)}, bf16[528,128]{1,0:T(8,128)(2,1)S(1)}) custom-call(s32[1,1]{1,0:T(1,128)S(6)} %copy.12.doc_any, bf16[256,512]{1,0:T(8,128)(2,1)} %bitcast.9, bf16[256,512]{1,0:T(8,128)(2,1)} %bitcast.10), custom_call_target="tpu_custom_call" | custom-call | flops 33554432 | bytes 1048576 | tf_op jit(solution)/shard_map/opening_body/pallas_call | solution.py:335
  2.6 3.0 %collective-permute-start = (bf16[528,128]{1,0:T(8,128)(2,1)S(1)}, bf16[528,128]{1,0:T(8,128)(2,1)S(1)}, u32[]{:S(2)}, u32[]{:S(2)}) collective-permute-start(bf16[528,128]{1,0:T(8,128)(2,1)S(1)} %get-tuple-element.43.own_ref), channel_id=1, source_target_pairs={{0,4},{1,5},{4,0},{5,1},{8,12},{9,13},{12,8},{13,9},{16,20},{17,21... | collective-permute-start | bytes 405512 | tf_op jit(solution)/shard_map/ppermute | solution.py:56
  5.6 0.0 collective-permute-start.2
  5.6 2.8 %local_body.1 = (bf16[256,512]{1,0:T(8,128)(2,1)S(1)}, bf16[512,2048]{1,0:T(8,128)(2,1)S(1)}, bf16[1024,256]{1,0:T(8,128)(2,1)S(1)}, f32[256,512]{1,0:T(8,128)S(1)}, f32[256,512]{1,0:T(8,128)S(1)}) custom-call(bf16[256,512]{1,0:T(8,128)(2,1)} %bitcast.11, bf16[256,512]{1,0:T(8,128)(2,1)S(1)} %get-tuple-element.38.key_ref, ...), custom_call_target="tpu_custom_call" | custom-call | flops 671088640 | bytes 6291456 | tf_op jit(solution)/shard_map/local_body/pallas_call | solution.py:340
  8.4 1.2 %collective-permute-done.pair_ref.refs_0_ = bf16[528,128]{1,0:T(8,128)(2,1)S(1)} collective-permute-done((bf16[528,128]{1,0:T(8,128)(2,1)S(1)}, bf16[528,128]{1,0:T(8,128)(2,1)S(1)}, u32[]{:S(2)}, u32[]{:S(2)}) %collective-permute-start) | collective-permute-done | bytes 135200 | tf_op jit(solution)/shard_map/ppermute | solution.py:56
  9.6 0.1 pair_body.2
  9.7 3.4 %collective-permute-start.1 = (bf16[528,128]{1,0:T(8,128)(2,1)S(1)}, bf16[528,128]{1,0:T(8,128)(2,1)S(1)}, u32[]{:S(2)}, u32[]{:S(2)}) collective-permute-start(bf16[528,128]{1,0:T(8,128)(2,1)S(1)} %pair_body.2), channel_id=1, source_target_pairs={{0,8},{1,9},{4,12},{5,13},{8,0},{9,1},{12,4},{13,5},{16,24},{17,25... | collective-permute-start | bytes 405512 | tf_op jit(solution)/shard_map/ppermute | solution.py:56
  13.1 3.5 %collective-permute-done.1.refs_2_ = bf16[528,128]{1,0:T(8,128)(2,1)S(1)} collective-permute-done((bf16[528,128]{1,0:T(8,128)(2,1)S(1)}, bf16[528,128]{1,0:T(8,128)(2,1)S(1)}, u32[]{:S(2)}, u32[]{:S(2)}) %collective-permute-start.1) | collective-permute-done | bytes 135200 | tf_op jit(solution)/shard_map/ppermute | solution.py:56
  16.5 0.0 collective-permute-done.3.refs_3_
  16.5 1.2 %forward_body.1 = (bf16[512,128]{1,0:T(8,128)(2,1)S(1)}, bf16[128,512]{1,0:T(8,128)(2,1)S(1)}, bf16[128,2048]{1,0:T(8,128)(2,1)S(1)}, bf16[256,512]{1,0:T(8,128)...) custom-call(f32[8,128]{1,0:T(8,128)S(1)} %get-tuple-element.42.number_ref, ...), custom_call_target="tpu_custom_call" | custom-call | flops 335544320 | bytes 4194304 | tf_op jit(solution)/shard_map/forward_body/pallas_call | solution.py:349
  17.7 1.6 %collective-permute-start.4 = (bf16[128,2048]{1,0:T(8,128)(2,1)S(1)}, bf16[128,2048]{1,0:T(8,128)(2,1)S(1)}, u32[]{:S(2)}, u32[]{:S(2)}) collective-permute-start(bf16[128,2048]{1,0:T(8,128)(2,1)S(1)} %get-tuple-element.56), channel_id=1, source_target_pairs={{0,2},{2,0},{1,3},{3,1},{4,6},{6,4},{5,7},{7,5},{8,10},{10,8},{9,1... | collective-permute-start | bytes 1572872 | tf_op jit(solution)/shard_map/ppermute | solution.py:357
  19.3 2.0 %collective-permute-start.5 = (bf16[528,128]{1,0:T(8,128)(2,1)S(1)}, bf16[528,128]{1,0:T(8,128)(2,1)S(1)}, u32[]{:S(2)}, u32[]{:S(2)}) collective-permute-start(bf16[528,128]{1,0:T(8,128)(2,1)S(1)} %get-tuple-element.58.own_ref), channel_id=1, source_target_pairs={{0,4},{1,5},{4,0},{5,1},{8,12},{9,13},{12,8},{13,9},{16,20},{17,21... | collective-permute-start | bytes 405512 | tf_op jit(solution)/shard_map/ppermute | solution.py:56
  21.3 2.4 %collective-permute-start.7 = (f32[4,128]{1,0:T(4,128)S(1)}, f32[4,128]{1,0:T(4,128)S(1)}, u32[]{:S(2)}, u32[]{:S(2)}) collective-permute-start(f32[4,128]{1,0:T(4,128)S(1)} %get-tuple-element.61), channel_id=1, source_target_pairs={{0,20},{1,21},{4,16},{5,17},{8,28},{9,29},{12,24},{13,25},{16,4},{... | collective-permute-start | bytes 6152 | tf_op jit(solution)/shard_map/ppermute | solution.py:74
  23.6 0.6 %collective-permute-start.6 = (f32[4,128]{1,0:T(4,128)S(1)}, f32[4,128]{1,0:T(4,128)S(1)}, u32[]{:S(2)}, u32[]{:S(2)}) collective-permute-start(f32[4,128]{1,0:T(4,128)S(1)} %get-tuple-element.61), channel_id=1, source_target_pairs={{0,16},{1,17},{4,20},{5,21},{8,24},{9,25},{12,28},{13,29},{16,0},{... | collective-permute-start | bytes 6152 | tf_op jit(solution)/shard_map/ppermute | solution.py:74
  24.2 2.2 %backward_body.1 = (bf16[256,512]{1,0:T(8,128)(2,1)}, f32[256,512]{1,0:T(8,128)S(1)}, f32[256,512]{1,0:T(8,128)S(1)}, f32[128,2048]{1,0:T(8,128)S(1)}) custom-call(bf16[256,512]{1,0:T(8,128)(2,1)S(1)} %get-tuple-element.40.query_ref, bf16[256,512]{1,0:T(8,128)(2,1)S(1)} %get-tuple-element.38.key_ref, bf16[256,512]{1,0:T(8,128)(2,1)S(1)} %get-tuple-element.39.value_ref, ...), custom_call_target="tpu_custom_call" | custom-call | bytes 65536 | tf_op jit(solution)/shard_map/backward_body/pallas_call | solution.py:358
  26.4 0.2 collective-permute-done.7.refs_1_
  26.7 2.7 %collective-permute-done.6.refs_0_ = f32[4,128]{1,0:T(4,128)S(1)} collective-permute-done((f32[4,128]{1,0:T(4,128)S(1)}, f32[4,128]{1,0:T(4,128)S(1)}, u32[]{:S(2)}, u32[]{:S(2)}) %collective-permute-start.6) | collective-permute-done | bytes 2080 | tf_op jit(solution)/shard_map/ppermute | solution.py:74
  29.4 0.1 pair_body.3.own_ref
  29.5 0.1 collective-permute-start.8
  29.5 0.1 collective-permute-start.11
  29.6 5.2 %collective-permute-done.8.other_ref.refs_2_ = bf16[528,128]{1,0:T(8,128)(2,1)S(1)} collective-permute-done((bf16[528,128]{1,0:T(8,128)(2,1)S(1)}, bf16[528,128]{1,0:T(8,128)(2,1)S(1)}, u32[]{:S(2)}, u32[]{:S(2)}) %collective-permute-start.8) | collective-permute-done | bytes 135200 | tf_op jit(solution)/shard_map/ppermute | solution.py:56
  34.9 1.1 %last_body.1 = (bf16[256,512]{1,0:T(8,128)(2,1)}, bf16[256,512]{1,0:T(8,128)(2,1)}) custom-call(f32[8,128]{1,0:T(8,128)S(1)} %get-tuple-element.42.number_ref, bf16[256,512]{1,0:T(8,128)(2,1)S(1)} %get-tuple-element.38.key_ref, bf16[256,512]{1,0:T(8,128)(2,1)S(1)} %get-tuple-element.39.value_ref, f32[256,512]{1,0:T(8,128)S(1)} %get-tuple-element.65.key_part_ref, ...), custom_call_target="tpu_custom_call" | custom-call | flops 67108864 | bytes 3145728 | tf_op jit(solution)/shard_map/last_body/pallas_call | solution.py:372
  36.0 0.0 collective-permute-done.10.refs_2_
  36.0 0.9 %layer_body.1 = (bf16[128,2048]{1,0:T(8,128)(2,1)}, f32[4,128]{1,0:T(4,128)}) custom-call(f32[128,2048]{1,0:T(8,128)S(1)} %get-tuple-element.55.own_ref, bf16[128,2048]{1,0:T(8,128)(2,1)S(1)} %collective-permute-done.4.refs_0_, f32[4,128]{1,0:T(4,128)S(1)} %gain_body.1.refs_1_, f32[4,128]{1,0:T(4,128)S(1)} %collective-permute-done.10.refs_2_), custom_call_target="tpu_custom_call" | custom-call | bytes 2097152 | tf_op jit(solution)/shard_map/layer_body/pallas_call | solution.py:376
  (11 shorter events, 0.0 us)
Async XLA Ops:
  2.6 7.0 %collective-permute-start = (bf16[528,128]{1,0:T(8,128)(2,1)S(1)}, bf16[528,128]{1,0:T(8,128)(2,1)S(1)}, u32[]{:S(2)}, u32[]{:S(2)}) collective-permute-start(bf16[528,128]{1,0:T(8,128)(2,1)S(1)} %get-tuple-element.43.own_ref), channel_id=1, source_target_pairs={{0,4},{1,5},{4,0},{5,1},{8,12},{9,13},{12,8},{13,9},{16,20},{17,21... | collective-permute-start | bytes 405512 | tf_op jit(solution)/shard_map/ppermute | solution.py:56
  5.6 7.4 %collective-permute-start.2 = (bf16[528,128]{1,0:T(8,128)(2,1)S(1)}, bf16[528,128]{1,0:T(8,128)(2,1)S(1)}, u32[]{:S(2)}, u32[]{:S(2)}) collective-permute-start(bf16[528,128]{1,0:T(8,128)(2,1)S(1)} %get-tuple-element.43.own_ref), channel_id=1, source_target_pairs={{0,1},{1,0},{4,16},{5,17},{8,9},{9,8},{12,24},{13,25},{16,4},{17,5... | collective-permute-start | bytes 405512 | tf_op jit(solution)/shard_map/ppermute | solution.py:56
  5.6 10.9 %copy-start = (f32[4,128]{1,0:T(4,128)S(1)}, f32[4,128]{1,0:T(4,128)}, u32[]{:S(2)}) copy-start(f32[4,128]{1,0:T(4,128)} %gain_ref.1) | copy-start | bytes 6148
  9.7 6.9 %collective-permute-start.1 = (bf16[528,128]{1,0:T(8,128)(2,1)S(1)}, bf16[528,128]{1,0:T(8,128)(2,1)S(1)}, u32[]{:S(2)}, u32[]{:S(2)}) collective-permute-start(bf16[528,128]{1,0:T(8,128)(2,1)S(1)} %pair_body.2), channel_id=1, source_target_pairs={{0,8},{1,9},{4,12},{5,13},{8,0},{9,1},{12,4},{13,5},{16,24},{17,25... | collective-permute-start | bytes 405512 | tf_op jit(solution)/shard_map/ppermute | solution.py:56
  13.1 3.5 %collective-permute-start.3 = (bf16[528,128]{1,0:T(8,128)(2,1)S(1)}, bf16[528,128]{1,0:T(8,128)(2,1)S(1)}, u32[]{:S(2)}, u32[]{:S(2)}) collective-permute-start(bf16[528,128]{1,0:T(8,128)(2,1)S(1)} %pair_body.2), channel_id=1, source_target_pairs={{0,1},{1,0},{4,5},{5,4},{8,16},{9,17},{12,20},{13,21},{16,8},{17,9... | collective-permute-start | bytes 405512 | tf_op jit(solution)/shard_map/ppermute | solution.py:56
  17.7 18.3 %collective-permute-start.4 = (bf16[128,2048]{1,0:T(8,128)(2,1)S(1)}, bf16[128,2048]{1,0:T(8,128)(2,1)S(1)}, u32[]{:S(2)}, u32[]{:S(2)}) collective-permute-start(bf16[128,2048]{1,0:T(8,128)(2,1)S(1)} %get-tuple-element.56), channel_id=1, source_target_pairs={{0,2},{2,0},{1,3},{3,1},{4,6},{6,4},{5,7},{7,5},{8,10},{10,8},{9,1... | collective-permute-start | bytes 1572872 | tf_op jit(solution)/shard_map/ppermute | solution.py:357
  19.3 7.1 %collective-permute-start.5 = (bf16[528,128]{1,0:T(8,128)(2,1)S(1)}, bf16[528,128]{1,0:T(8,128)(2,1)S(1)}, u32[]{:S(2)}, u32[]{:S(2)}) collective-permute-start(bf16[528,128]{1,0:T(8,128)(2,1)S(1)} %get-tuple-element.58.own_ref), channel_id=1, source_target_pairs={{0,4},{1,5},{4,0},{5,1},{8,12},{9,13},{12,8},{13,9},{16,20},{17,21... | collective-permute-start | bytes 405512 | tf_op jit(solution)/shard_map/ppermute | solution.py:56
  21.3 5.4 %collective-permute-start.7 = (f32[4,128]{1,0:T(4,128)S(1)}, f32[4,128]{1,0:T(4,128)S(1)}, u32[]{:S(2)}, u32[]{:S(2)}) collective-permute-start(f32[4,128]{1,0:T(4,128)S(1)} %get-tuple-element.61), channel_id=1, source_target_pairs={{0,20},{1,21},{4,16},{5,17},{8,28},{9,29},{12,24},{13,25},{16,4},{... | collective-permute-start | bytes 6152 | tf_op jit(solution)/shard_map/ppermute | solution.py:74
  23.6 5.8 %collective-permute-start.6 = (f32[4,128]{1,0:T(4,128)S(1)}, f32[4,128]{1,0:T(4,128)S(1)}, u32[]{:S(2)}, u32[]{:S(2)}) collective-permute-start(f32[4,128]{1,0:T(4,128)S(1)} %get-tuple-element.61), channel_id=1, source_target_pairs={{0,16},{1,17},{4,20},{5,21},{8,24},{9,25},{12,28},{13,29},{16,0},{... | collective-permute-start | bytes 6152 | tf_op jit(solution)/shard_map/ppermute | solution.py:74
  24.2 5.4 %collective-permute-start.9 = (bf16[528,128]{1,0:T(8,128)(2,1)S(1)}, bf16[528,128]{1,0:T(8,128)(2,1)S(1)}, u32[]{:S(2)}, u32[]{:S(2)}) collective-permute-start(bf16[528,128]{1,0:T(8,128)(2,1)S(1)} %get-tuple-element.58.own_ref), channel_id=1, source_target_pairs={{0,1},{1,0},{4,16},{5,17},{8,9},{9,8},{12,24},{13,25},{16,4},{17,5... | collective-permute-start | bytes 405512 | tf_op jit(solution)/shard_map/ppermute | solution.py:56
  29.5 5.4 %collective-permute-start.8 = (bf16[528,128]{1,0:T(8,128)(2,1)S(1)}, bf16[528,128]{1,0:T(8,128)(2,1)S(1)}, u32[]{:S(2)}, u32[]{:S(2)}) collective-permute-start(bf16[528,128]{1,0:T(8,128)(2,1)S(1)} %pair_body.3.own_ref), channel_id=1, source_target_pairs={{0,8},{1,9},{4,12},{5,13},{8,0},{9,1},{12,4},{13,5},{16,24},{17,25... | collective-permute-start | bytes 405512 | tf_op jit(solution)/shard_map/ppermute | solution.py:56
  29.5 5.3 %collective-permute-start.11 = (bf16[528,128]{1,0:T(8,128)(2,1)S(1)}, bf16[528,128]{1,0:T(8,128)(2,1)S(1)}, u32[]{:S(2)}, u32[]{:S(2)}) collective-permute-start(bf16[528,128]{1,0:T(8,128)(2,1)S(1)} %pair_body.3.own_ref), channel_id=1, source_target_pairs={{0,1},{1,0},{4,5},{5,4},{8,16},{9,17},{12,20},{13,21},{16,8},{17,9... | collective-permute-start | bytes 405512 | tf_op jit(solution)/shard_map/ppermute | solution.py:56
  34.9 1.2 %collective-permute-start.10 = (f32[4,128]{1,0:T(4,128)S(1)}, f32[4,128]{1,0:T(4,128)S(1)}, u32[]{:S(2)}, u32[]{:S(2)}) collective-permute-start(f32[4,128]{1,0:T(4,128)S(1)} %gain_body.1.refs_1_), channel_id=1, source_target_pairs={{0,1},{1,0},{4,5},{5,4},{8,9},{9,8},{12,13},{13,12},{16,17},{17,16... | collective-permute-start | bytes 6152 | tf_op jit(solution)/shard_map/ppermute | solution.py:74

commit v8 on v7

--- a/solution.py
+++ b/solution.py
@@ -65,6 +65,11 @@
     return [exchange(block, blocks(size, distance, odd)) for odd in (0, 1)]
 
 
+def turned(block, distance):
+    size = lax.axis_size("seq")
+    return lax.ppermute(block, "seq", [(i, (i + distance) % size) for i in range(size)])
+
+
 def flipped(block, distance, cores):
     route = [
         (2 * i + core, 2 * (i ^ distance) + (core ^ cores))
@@ -175,7 +180,7 @@
 
 
 def pair_body(forward, gains, number_ref, sum_ref, own_ref, pair_ref, *refs):
-    *gain_refs, msg_ref = refs
+    msg_ref, *gain_ref = refs
     rows = sum_ref.shape[0]
     number = number_ref[:1, :]
     leads = lax.rem(lax.axis_index("seq"), 2) == (1 if forward else 0)
@@ -184,10 +189,9 @@
     same = theirs == number
     keep_mine, keep_theirs = same | leads, same | jnp.logical_not(leads)
     msg_ref[:rows, :] = (jnp.where(keep_mine, mine, 0.0) + jnp.where(keep_theirs, sums, 0.0)).astype(BF16)
-    gain = merge_gain(gains, own_ref, pair_ref)
+    gain = put_tail(msg_ref, jnp.where(leads, number, theirs), merge_gain(gains, own_ref, pair_ref))
     if gains:
-        gain = gain + (gain_refs[0][...] + gain_refs[1][...])
-    put_tail(msg_ref, jnp.where(leads, number, theirs), gain)
+        gain_ref[0][...] = gain
 
 
 def merge_body(distance, forward, gains, number_ref, sum_ref, own_ref, *refs):
@@ -202,8 +206,8 @@
     put_tail(msg_ref, number, merge_gain(gains, own_ref, even_ref))
 
 
-def gain_body(own_ref, other_ref, out_ref):
-    out_ref[...] = merge_gain(True, own_ref, other_ref)
+def gain_body(own_ref, far_ref, farther_ref, near_ref, out_ref):
+    out_ref[...] = (own_ref[...] + far_ref[...]) + (sent_gain(near_ref) + farther_ref[...])
 
 
 def forward_body(
@@ -308,20 +312,22 @@
 
     beside = []
 
-    def spread(outer, msg, forward, gain_part=None):
-        carry = gain_part is not None
+    def spread(outer, msg, forward):
+        carry = gains and not forward
         if last == 2:
             pair = exchange(msg, blocks(size, 1, 0))
             far = exchange(msg, [(i, i + 3) for i in range(1, size - 3, 2)])
-            gain = [flipped(gain_part, to, 0) for to in (size // 2, size // 2 + 1)] if carry else []
             if TIE[0] and forward or TIE[1] and not forward:
                 pair, beside[0] = lax.optimization_barrier((pair, beside[0]))
-            (msg,) = call(
-                functools.partial(pair_body, forward, carry), [(message, BF16)], "vvvv" + "v" * len(gain), flops=0, moved=1 << 20
-            )(number, outer, msg, pair, *gain)
-            even, odd = swaps(msg, last)
+            msg, *gain = call(
+                functools.partial(pair_body, forward, carry), [(message, BF16)] + [(small, F32)] * carry, "vvvv",
+                flops=0, moved=1 << 20,
+            )(number, outer, msg, pair)
+            even = odd = turned(msg, last if forward else -last)
+            gain = [*gain, *(turned(block, -to) for block in gain for to in (size // 2, size // 2 + last))]
             even, far = lax.optimization_barrier((even, far))
-            return [pair, far, even, odd], msg
+            odd = even
+            return [pair, far, even, odd], msg, gain
         terms = []
         for distance in distances[:-1]:
             even, odd = swaps(msg, distance)
@@ -329,7 +335,7 @@
                 functools.partial(merge_body, distance, forward, carry), [(summed, F32), (message, BF16)],
                 "vvvvv" + "v" * len(terms), flops=0, moved=1 << 20,
             )(number, outer, msg, *terms, even, odd)
-        return [*terms, *swaps(msg, last)], msg
+        return [*terms, *swaps(msg, last)], msg, []
 
     in_hbm = lambda block: pltpu.with_memory_space_constraint(block, pltpu.HBM)
     key, value, number, outer, msg = call(
@@ -344,7 +350,7 @@
         scratch=[pltpu.VMEM((tokens, model), BF16), pltpu.SemaphoreType.DMA((3,))],
     )(in_hbm(queries[0]), key, value, in_hbm(cotangent[0]), in_hbm(w_out))
     beside.append(within)
-    sums, _ = spread(outer, msg, True)
+    sums, _, _ = spread(outer, msg, True)
     (within,) = beside
     state, keep, *send, grad, outer, msg, gain_part = call(
         functools.partial(forward_body, heads, dim, last),
@@ -361,11 +367,11 @@
         "vvvvvvvv", flops=0, moved=1 << 16,
     )(query, key, value, weights, grad, state, keep, w)
     beside[0] = key_part
-    sums, msg = spread(outer, msg, False, gain_part if gains else None)
+    sums, msg, gain = spread(outer, msg, False)
     (key_part,) = beside
     scale = 1.0 / math.sqrt(size * lax.axis_size("dp") * tokens)
     if gains:
-        (gain,) = call(gain_body, [(small, F32)], "vv", flops=0, moved=1 << 16)(msg, sums[-2])
+        (gain,) = call(gain_body, [(small, F32)], "vvvv", flops=0, moved=1 << 16)(*gain, sums[-2])
         gain = [gain, flipped(gain, 0, 1)]
     else:
         gain = [lax.psum(gain_part, ("seq", "dp"))]

time: 37.1 us -> 36 us (0.970)
  waiting for transfers between devices: 12.9 us -> 8.79 us
  starting transfers between devices: 13.1 us -> 15.6 us
    ppermute x0 -> x4, starting transfers between devices: none -> 8.17 us  [turned(): lax.ppermute(block, 'seq', [(i, (i + distance) % size) for i in range(siz...]
    ppermute x8 -> x4, waiting for transfers between devices: 9.87 us -> 1.94 us  [exchange(): lax.ppermute(block, ('seq', 'dp'), pairing(lax.axis_size('seq'), pairs))]
    ppermute x0 -> x4, waiting for transfers between devices: none -> 6.82 us  [turned(): lax.ppermute(block, 'seq', [(i, (i + distance) % size) for i in range(siz...]
    ppermute x3 -> x1, waiting for transfers between devices: 3 us -> 0.04 us  [flipped(): return lax.ppermute(block, ('seq', 'dp'), route)]
    ppermute x3 -> x1, starting transfers between devices: 2.92 us -> 0.01 us  [flipped(): return lax.ppermute(block, ('seq', 'dp'), route)]
    ppermute x8 -> x4, starting transfers between devices: 8.54 us -> 5.92 us  [exchange(): lax.ppermute(block, ('seq', 'dp'), pairing(lax.axis_size('seq'), pairs))]
  transfers between devices with their start and end apart: 12 -> 10, of which waited for: 5 -> 6; matrix products, arithmetic and copies ran while one was open for 0% -> 0% of each run, Pallas kernels for 17% -> 18%
where the time goes in v8:
time: 36 us; the launch traced here: 35.5 us
  starting transfers between devices  15.6 us (43%)
  Pallas kernels  9.8 us (27%)
  waiting for transfers between devices  8.79 us (24%)
  between operations  1.32 us (4%)
    ppermute x4, starting transfers between devices, turned(): lax.ppermute(block, 'seq', [(i, (i + distance) % size) for i in range(siz...  8.17 us
    ppermute x4, waiting for transfers between devices, turned(): lax.ppermute(block, 'seq', [(i, (i + distance) % size) for i in range(siz...  6.82 us
    ppermute x4, starting transfers between devices, exchange(): lax.ppermute(block, ('seq', 'dp'), pairing(lax.axis_size('seq'), pairs))  5.92 us
    pallas_call x1, Pallas kernels, on_device(): call(functools.partial(local_body, heads, dim), [(rows, BF16), ((width, m...  2.79 us
    pallas_call x1, Pallas kernels, on_device(): call(functools.partial(backward_body, heads, dim), [(rows, BF16), (rows,...  2.24 us
    ppermute x4, waiting for transfers between devices, exchange(): lax.ppermute(block, ('seq', 'dp'), pairing(lax.axis_size('seq'), pairs))  1.94 us
    ppermute x1, starting transfers between devices, on_device(): got = [lax.ppermute(part, 'head', [(0, 1), (1, 0)]) for part in send]  1.49 us
    pallas_call x1, Pallas kernels, on_device(): call(functools.partial(forward_body, heads, dim, last), [(summed, BF16),...  1.33 us
  transfers between devices with their start and end apart: 10, of which 6 were waited for; matrix products, arithmetic and copies ran while one was open for 0% of the time, Pallas kernels for 18%

profile of v8, /device:TPU:0, one launch (start us, length us, event | category | flops | bytes accessed | tf_op | source)
XLA Modules:
  0.0 35.5 jit_solution(11603836902412470801)
XLA Ops:
  1.3 1.3 %opening_body.1 = (bf16[256,512]{1,0:T(8,128)(2,1)S(1)}, bf16[256,512]{1,0:T(8,128)(2,1)S(1)}, f32[8,128]{1,0:T(8,128)S(1)}, f32[512,128]{1,0:T(8,128)S(1)}, bf16[528,128]{1,0:T(8,128)(2,1)S(1)}) custom-call(s32[1,1]{1,0:T(1,128)S(6)} %copy.12.doc_any, bf16[256,512]{1,0:T(8,128)(2,1)} %bitcast.9, bf16[256,512]{1,0:T(8,128)(2,1)} %bitcast.10), custom_call_target="tpu_custom_call" | custom-call | flops 33554432 | bytes 1048576 | tf_op jit(solution)/shard_map/opening_body/pallas_call | solution.py:341
  2.6 3.0 %collective-permute-start = (bf16[528,128]{1,0:T(8,128)(2,1)S(1)}, bf16[528,128]{1,0:T(8,128)(2,1)S(1)}, u32[]{:S(2)}, u32[]{:S(2)}) collective-permute-start(bf16[528,128]{1,0:T(8,128)(2,1)S(1)} %get-tuple-element.44.own_ref), channel_id=1, source_target_pairs={{0,4},{1,5},{4,0},{5,1},{8,12},{9,13},{12,8},{13,9},{16,20},{17,21... | collective-permute-start | bytes 405512 | tf_op jit(solution)/shard_map/ppermute | solution.py:56
  5.6 0.0 collective-permute-start.2
  5.6 2.8 %local_body.1 = (bf16[256,512]{1,0:T(8,128)(2,1)S(1)}, bf16[512,2048]{1,0:T(8,128)(2,1)S(1)}, bf16[1024,256]{1,0:T(8,128)(2,1)S(1)}, f32[256,512]{1,0:T(8,128)S(1)}, f32[256,512]{1,0:T(8,128)S(1)}) custom-call(bf16[256,512]{1,0:T(8,128)(2,1)} %bitcast.11, bf16[256,512]{1,0:T(8,128)(2,1)S(1)} %get-tuple-element.39.key_ref, ...), custom_call_target="tpu_custom_call" | custom-call | flops 671088640 | bytes 6291456 | tf_op jit(solution)/shard_map/local_body/pallas_call | solution.py:346
  8.4 1.2 %collective-permute-done.pair_ref.refs_0_ = bf16[528,128]{1,0:T(8,128)(2,1)S(1)} collective-permute-done((bf16[528,128]{1,0:T(8,128)(2,1)S(1)}, bf16[528,128]{1,0:T(8,128)(2,1)S(1)}, u32[]{:S(2)}, u32[]{:S(2)}) %collective-permute-start) | collective-permute-done | bytes 135200 | tf_op jit(solution)/shard_map/ppermute | solution.py:56
  9.6 0.1 pair_body.2
  9.7 3.4 %collective-permute-start.1 = (bf16[528,128]{1,0:T(8,128)(2,1)S(1)}, bf16[528,128]{1,0:T(8,128)(2,1)S(1)}, u32[]{:S(2)}, u32[]{:S(2)}) collective-permute-start(bf16[528,128]{1,0:T(8,128)(2,1)S(1)} %pair_body.2), channel_id=1, source_target_pairs={{0,8},{4,12},{8,16},{12,20},{16,24},{20,28},{24,0},{28,4},{1,9},{5... | collective-permute-start | bytes 405512 | tf_op jit(solution)/shard_map/ppermute | solution.py:70
  13.0 3.5 %collective-permute-done.1.refs_2_.refs_3_ = bf16[528,128]{1,0:T(8,128)(2,1)S(1)} collective-permute-done((bf16[528,128]{1,0:T(8,128)(2,1)S(1)}, bf16[528,128]{1,0:T(8,128)(2,1)S(1)}, u32[]{:S(2)}, u32[]{:S(2)}) %collective-permute-start.1) | collective-permute-done | bytes 135200 | tf_op jit(solution)/shard_map/ppermute | solution.py:70
  16.5 1.3 %forward_body.1 = (bf16[512,128]{1,0:T(8,128)(2,1)S(1)}, bf16[128,512]{1,0:T(8,128)(2,1)S(1)}, bf16[128,2048]{1,0:T(8,128)(2,1)S(1)}, bf16[256,512]{1,0:T(8,128)...) custom-call(f32[8,128]{1,0:T(8,128)S(1)} %get-tuple-element.43.number_ref, ...), custom_call_target="tpu_custom_call" | custom-call | flops 335544320 | bytes 4194304 | tf_op jit(solution)/shard_map/forward_body/pallas_call | solution.py:355
  17.9 1.5 %collective-permute-start.3 = (bf16[128,2048]{1,0:T(8,128)(2,1)S(1)}, bf16[128,2048]{1,0:T(8,128)(2,1)S(1)}, u32[]{:S(2)}, u32[]{:S(2)}) collective-permute-start(bf16[128,2048]{1,0:T(8,128)(2,1)S(1)} %get-tuple-element.57), channel_id=1, source_target_pairs={{0,2},{2,0},{1,3},{3,1},{4,6},{6,4},{5,7},{7,5},{8,10},{10,8},{9,1... | collective-permute-start | bytes 1572872 | tf_op jit(solution)/shard_map/ppermute | solution.py:363
  19.4 2.9 %collective-permute-start.4 = (bf16[528,128]{1,0:T(8,128)(2,1)S(1)}, bf16[528,128]{1,0:T(8,128)(2,1)S(1)}, u32[]{:S(2)}, u32[]{:S(2)}) collective-permute-start(bf16[528,128]{1,0:T(8,128)(2,1)S(1)} %get-tuple-element.59.own_ref), channel_id=1, source_target_pairs={{0,4},{1,5},{4,0},{5,1},{8,12},{9,13},{12,8},{13,9},{16,20},{17,21... | collective-permute-start | bytes 405512 | tf_op jit(solution)/shard_map/ppermute | solution.py:56
  22.3 2.2 %backward_body.1 = (bf16[256,512]{1,0:T(8,128)(2,1)}, f32[256,512]{1,0:T(8,128)S(1)}, f32[256,512]{1,0:T(8,128)S(1)}, f32[128,2048]{1,0:T(8,128)S(1)}) custom-call(bf16[256,512]{1,0:T(8,128)(2,1)S(1)} %get-tuple-element.41.query_ref, bf16[256,512]{1,0:T(8,128)(2,1)S(1)} %get-tuple-element.39.key_ref, bf16[256,512]{1,0:T(8,128)(2,1)S(1)} %get-tuple-element.40.value_ref, ...), custom_call_target="tpu_custom_call" | custom-call | bytes 65536 | tf_op jit(solution)/shard_map/backward_body/pallas_call | solution.py:364
  24.5 0.7 %collective-permute-done.4.pair_ref.refs_0_ = bf16[528,128]{1,0:T(8,128)(2,1)S(1)} collective-permute-done((bf16[528,128]{1,0:T(8,128)(2,1)S(1)}, bf16[528,128]{1,0:T(8,128)(2,1)S(1)}, u32[]{:S(2)}, u32[]{:S(2)}) %collective-permute-start.4) | collective-permute-done | bytes 135200 | tf_op jit(solution)/shard_map/ppermute | solution.py:56
  25.3 0.1 pair_body.3
  25.3 2.6 %collective-permute-start.7 = (bf16[528,128]{1,0:T(8,128)(2,1)S(1)}, bf16[528,128]{1,0:T(8,128)(2,1)S(1)}, u32[]{:S(2)}, u32[]{:S(2)}) collective-permute-start(bf16[528,128]{1,0:T(8,128)(2,1)S(1)} %get-tuple-element.63), channel_id=1, source_target_pairs={{0,24},{4,28},{8,0},{12,4},{16,8},{20,12},{24,16},{28,20},{1,25},{... | collective-permute-start | bytes 405512 | tf_op jit(solution)/shard_map/ppermute | solution.py:70
  27.9 0.8 %collective-permute-start.6 = (f32[4,128]{1,0:T(4,128)S(1)}, f32[4,128]{1,0:T(4,128)S(1)}, u32[]{:S(2)}, u32[]{:S(2)}) collective-permute-start(f32[4,128]{1,0:T(4,128)S(1)} %get-tuple-element.62.own_ref), channel_id=1, source_target_pairs={{0,8},{4,12},{8,16},{12,20},{16,24},{20,28},{24,0},{28,4},{1,9},{5... | collective-permute-start | bytes 6152 | tf_op jit(solution)/shard_map/ppermute | solution.py:70
  28.7 1.4 %collective-permute-start.5 = (f32[4,128]{1,0:T(4,128)S(1)}, f32[4,128]{1,0:T(4,128)S(1)}, u32[]{:S(2)}, u32[]{:S(2)}) collective-permute-start(f32[4,128]{1,0:T(4,128)S(1)} %get-tuple-element.62.own_ref), channel_id=1, source_target_pairs={{0,16},{4,20},{8,24},{12,28},{16,0},{20,4},{24,8},{28,12},{1,17},{... | collective-permute-start | bytes 6152 | tf_op jit(solution)/shard_map/ppermute | solution.py:70
  30.1 2.7 %collective-permute-done.7.near_ref.refs_2_.refs_3_ = bf16[528,128]{1,0:T(8,128)(2,1)S(1)} collective-permute-done((bf16[528,128]{1,0:T(8,128)(2,1)S(1)}, bf16[528,128]{1,0:T(8,128)(2,1)S(1)}, u32[]{:S(2)}, u32[]{:S(2)}) %collective-permute-start.7) | collective-permute-done | bytes 135200 | tf_op jit(solution)/shard_map/ppermute | solution.py:70
  32.8 0.6 %collective-permute-done.6.farther_ref = f32[4,128]{1,0:T(4,128)S(1)} collective-permute-done((f32[4,128]{1,0:T(4,128)S(1)}, f32[4,128]{1,0:T(4,128)S(1)}, u32[]{:S(2)}, u32[]{:S(2)}) %collective-permute-start.6) | collective-permute-done | bytes 2080 | tf_op jit(solution)/shard_map/ppermute | solution.py:70
  33.4 0.1 collective-permute-done.5.far_ref
  33.5 0.0 collective-permute-start.9
  33.5 1.1 %last_body.1 = (bf16[256,512]{1,0:T(8,128)(2,1)}, bf16[256,512]{1,0:T(8,128)(2,1)}) custom-call(f32[8,128]{1,0:T(8,128)S(1)} %get-tuple-element.43.number_ref, bf16[256,512]{1,0:T(8,128)(2,1)S(1)} %get-tuple-element.39.key_ref, bf16[256,512]{1,0:T(8,128)(2,1)S(1)} %get-tuple-element.40.value_ref, f32[256,512]{1,0:T(8,128)S(1)} %get-tuple-element.67.key_part_ref, ...), custom_call_target="tpu_custom_call" | custom-call | flops 67108864 | bytes 3145728 | tf_op jit(solution)/shard_map/last_body/pallas_call | solution.py:378
  34.6 0.0 collective-permute-done.9.refs_2_
  34.6 0.9 %layer_body.1 = (bf16[128,2048]{1,0:T(8,128)(2,1)}, f32[4,128]{1,0:T(4,128)}) custom-call(f32[128,2048]{1,0:T(8,128)S(1)} %get-tuple-element.56.own_ref, bf16[128,2048]{1,0:T(8,128)(2,1)S(1)} %collective-permute-done.3.refs_0_, f32[4,128]{1,0:T(4,128)S(1)} %gain_body.1.refs_1_, f32[4,128]{1,0:T(4,128)S(1)} %collective-permute-done.9.refs_2_), custom_call_target="tpu_custom_call" | custom-call | bytes 2097152 | tf_op jit(solution)/shard_map/layer_body/pallas_call | solution.py:382
  (7 shorter events, 0.0 us)
Async XLA Ops:
  2.6 7.0 %collective-permute-start = (bf16[528,128]{1,0:T(8,128)(2,1)S(1)}, bf16[528,128]{1,0:T(8,128)(2,1)S(1)}, u32[]{:S(2)}, u32[]{:S(2)}) collective-permute-start(bf16[528,128]{1,0:T(8,128)(2,1)S(1)} %get-tuple-element.44.own_ref), channel_id=1, source_target_pairs={{0,4},{1,5},{4,0},{5,1},{8,12},{9,13},{12,8},{13,9},{16,20},{17,21... | collective-permute-start | bytes 405512 | tf_op jit(solution)/shard_map/ppermute | solution.py:56
  5.6 7.4 %collective-permute-start.2 = (bf16[528,128]{1,0:T(8,128)(2,1)S(1)}, bf16[528,128]{1,0:T(8,128)(2,1)S(1)}, u32[]{:S(2)}, u32[]{:S(2)}) collective-permute-start(bf16[528,128]{1,0:T(8,128)(2,1)S(1)} %get-tuple-element.44.own_ref), channel_id=1, source_target_pairs={{0,1},{1,0},{4,16},{5,17},{8,9},{9,8},{12,24},{13,25},{16,4},{17,5... | collective-permute-start | bytes 405512 | tf_op jit(solution)/shard_map/ppermute | solution.py:56
  5.6 10.9 %copy-start = (f32[4,128]{1,0:T(4,128)S(1)}, f32[4,128]{1,0:T(4,128)}, u32[]{:S(2)}) copy-start(f32[4,128]{1,0:T(4,128)} %gain_ref.1) | copy-start | bytes 6148
  9.7 6.9 %collective-permute-start.1 = (bf16[528,128]{1,0:T(8,128)(2,1)S(1)}, bf16[528,128]{1,0:T(8,128)(2,1)S(1)}, u32[]{:S(2)}, u32[]{:S(2)}) collective-permute-start(bf16[528,128]{1,0:T(8,128)(2,1)S(1)} %pair_body.2), channel_id=1, source_target_pairs={{0,8},{4,12},{8,16},{12,20},{16,24},{20,28},{24,0},{28,4},{1,9},{5... | collective-permute-start | bytes 405512 | tf_op jit(solution)/shard_map/ppermute | solution.py:70
  17.9 16.8 %collective-permute-start.3 = (bf16[128,2048]{1,0:T(8,128)(2,1)S(1)}, bf16[128,2048]{1,0:T(8,128)(2,1)S(1)}, u32[]{:S(2)}, u32[]{:S(2)}) collective-permute-start(bf16[128,2048]{1,0:T(8,128)(2,1)S(1)} %get-tuple-element.57), channel_id=1, source_target_pairs={{0,2},{2,0},{1,3},{3,1},{4,6},{6,4},{5,7},{7,5},{8,10},{10,8},{9,1... | collective-permute-start | bytes 1572872 | tf_op jit(solution)/shard_map/ppermute | solution.py:363
  19.4 5.9 %collective-permute-start.4 = (bf16[528,128]{1,0:T(8,128)(2,1)S(1)}, bf16[528,128]{1,0:T(8,128)(2,1)S(1)}, u32[]{:S(2)}, u32[]{:S(2)}) collective-permute-start(bf16[528,128]{1,0:T(8,128)(2,1)S(1)} %get-tuple-element.59.own_ref), channel_id=1, source_target_pairs={{0,4},{1,5},{4,0},{5,1},{8,12},{9,13},{12,8},{13,9},{16,20},{17,21... | collective-permute-start | bytes 405512 | tf_op jit(solution)/shard_map/ppermute | solution.py:56
  22.3 7.8 %collective-permute-start.8 = (bf16[528,128]{1,0:T(8,128)(2,1)S(1)}, bf16[528,128]{1,0:T(8,128)(2,1)S(1)}, u32[]{:S(2)}, u32[]{:S(2)}) collective-permute-start(bf16[528,128]{1,0:T(8,128)(2,1)S(1)} %get-tuple-element.59.own_ref), channel_id=1, source_target_pairs={{0,1},{1,0},{4,16},{5,17},{8,9},{9,8},{12,24},{13,25},{16,4},{17,5... | collective-permute-start | bytes 405512 | tf_op jit(solution)/shard_map/ppermute | solution.py:56
  25.3 7.5 %collective-permute-start.7 = (bf16[528,128]{1,0:T(8,128)(2,1)S(1)}, bf16[528,128]{1,0:T(8,128)(2,1)S(1)}, u32[]{:S(2)}, u32[]{:S(2)}) collective-permute-start(bf16[528,128]{1,0:T(8,128)(2,1)S(1)} %get-tuple-element.63), channel_id=1, source_target_pairs={{0,24},{4,28},{8,0},{12,4},{16,8},{20,12},{24,16},{28,20},{1,25},{... | collective-permute-start | bytes 405512 | tf_op jit(solution)/shard_map/ppermute | solution.py:70
  27.9 5.5 %collective-permute-start.6 = (f32[4,128]{1,0:T(4,128)S(1)}, f32[4,128]{1,0:T(4,128)S(1)}, u32[]{:S(2)}, u32[]{:S(2)}) collective-permute-start(f32[4,128]{1,0:T(4,128)S(1)} %get-tuple-element.62.own_ref), channel_id=1, source_target_pairs={{0,8},{4,12},{8,16},{12,20},{16,24},{20,28},{24,0},{28,4},{1,9},{5... | collective-permute-start | bytes 6152 | tf_op jit(solution)/shard_map/ppermute | solution.py:70
  28.7 4.7 %collective-permute-start.5 = (f32[4,128]{1,0:T(4,128)S(1)}, f32[4,128]{1,0:T(4,128)S(1)}, u32[]{:S(2)}, u32[]{:S(2)}) collective-permute-start(f32[4,128]{1,0:T(4,128)S(1)} %get-tuple-element.62.own_ref), channel_id=1, source_target_pairs={{0,16},{4,20},{8,24},{12,28},{16,0},{20,4},{24,8},{28,12},{1,17},{... | collective-permute-start | bytes 6152 | tf_op jit(solution)/shard_map/ppermute | solution.py:70
  33.5 1.2 %collective-permute-start.9 = (f32[4,128]{1,0:T(4,128)S(1)}, f32[4,128]{1,0:T(4,128)S(1)}, u32[]{:S(2)}, u32[]{:S(2)}) collective-permute-start(f32[4,128]{1,0:T(4,128)S(1)} %gain_body.1.refs_1_), channel_id=1, source_target_pairs={{0,1},{1,0},{4,5},{5,4},{8,9},{9,8},{12,13},{13,12},{16,17},{17,16... | collective-permute-start | bytes 6152 | tf_op jit(solution)/shard_map/ppermute | solution.py:79

commit v9 on v8

--- a/solution.py
+++ b/solution.py
@@ -12,7 +12,6 @@
 F32 = jnp.float32
 BF16 = jnp.bfloat16
 TAIL = 16
-TIE = (True, True)
 GAIN = 4
 PARTS = 1
 
@@ -30,7 +29,7 @@
 
 
 def call(body, outs, places, flops, moved, scratch=()):
-    space = {"a": pl.ANY, "v": pltpu.VMEM, "h": pltpu.HBM}
+    space = {"s": pltpu.SMEM, "v": pltpu.VMEM, "h": pltpu.HBM}
     return pl.pallas_call(
         body,
         out_shape=[jax.ShapeDtypeStruct(s, t) for s, t in outs],
@@ -56,6 +55,13 @@
     return lax.ppermute(block, ("seq", "dp"), pairing(lax.axis_size("seq"), pairs))
 
 
+def turning(size, loops):
+    to = {a: b for loop in loops for a, b in zip(loop, loop[1:] + loop[:1])}
+    return [
+        (2 * i + core, 2 * to.get(i, i) + (core ^ (i not in to))) for i in range(size) for core in (0, 1)
+    ]
+
+
 def blocks(size, distance, odd):
     return [(i, i + distance) for i in range(size - distance) if (i // distance) % 2 == odd]
 
@@ -127,16 +133,15 @@
 
 
 def opening_body(
-    heads, dim, doc_any, key_hbm, value_hbm,
-    key_ref, value_ref, number_ref, sum_ref, msg_ref, doc_ref, sems,
+    heads, dim, doc_ref, key_hbm, value_hbm,
+    key_ref, value_ref, number_ref, sum_ref, msg_ref, sems,
 ):
     copies = [
         pltpu.make_async_copy(src, dst, sems.at[i])
-        for i, (src, dst) in enumerate(((key_hbm, key_ref), (value_hbm, value_ref), (doc_any, doc_ref)))
+        for i, (src, dst) in enumerate(((key_hbm, key_ref), (value_hbm, value_ref)))
     ]
     for copy in copies:
         copy.start()
-    copies[2].wait()
     number = jnp.full(number_ref.shape, doc_ref[0, 0] + 1, jnp.int32).astype(F32)
     number_ref[...] = number
     put_tail(msg_ref, number[:1, :])
@@ -316,8 +321,9 @@
         carry = gains and not forward
         if last == 2:
             pair = exchange(msg, blocks(size, 1, 0))
-            far = exchange(msg, [(i, i + 3) for i in range(1, size - 3, 2)])
-            if TIE[0] and forward or TIE[1] and not forward:
+            loops = [[i, i + 3, i + 4] if forward else [i + 3, i, i - 1] for i in range(1, size - 3, 2)]
+            far = lax.ppermute(msg, ("seq", "dp"), turning(size, loops))
+            if not forward:
                 pair, beside[0] = lax.optimization_barrier((pair, beside[0]))
             msg, *gain = call(
                 functools.partial(pair_body, forward, carry), [(message, BF16)] + [(small, F32)] * carry, "vvvv",
@@ -341,7 +347,7 @@
     key, value, number, outer, msg = call(
         functools.partial(opening_body, heads, dim),
         [(rows, BF16)] * 2 + [((8, dim), F32), (summed, F32), (message, BF16)],
-        "ahh", flops=matrix, moved=1 << 20, scratch=[pltpu.SMEM((1, 1), jnp.int32), pltpu.SemaphoreType.DMA((3,))],
+        "shh", flops=matrix, moved=1 << 20, scratch=[pltpu.SemaphoreType.DMA((2,))],
     )(stretch_doc, in_hbm(key_rows[0]), in_hbm(value_rows[0]))
     query, w, weights, within, normed_grad = call(
         functools.partial(local_body, heads, dim),

time: 36 us -> 35.6 us (0.989)
  starting transfers between devices: 15.6 us -> 14.9 us
  waiting for transfers between devices: 8.79 us -> 9.4 us
    ppermute x4, starting transfers between devices: 8.17 us -> 5.2 us  [turned(): lax.ppermute(block, 'seq', [(i, (i + distance) % size) for i in range(siz...]
    ppermute x0 -> x2, starting transfers between devices: none -> 2.65 us  [spread(): far = lax.ppermute(msg, ('seq', 'dp'), turning(size, loops))]
    ppermute x4 -> x2, waiting for transfers between devices: 1.94 us -> 3.58 us  [exchange(): lax.ppermute(block, ('seq', 'dp'), pairing(lax.axis_size('seq'), pairs))]
    ppermute x4, waiting for transfers between devices: 6.82 us -> 5.77 us  [turned(): lax.ppermute(block, 'seq', [(i, (i + distance) % size) for i in range(siz...]
    ppermute x4 -> x2, starting transfers between devices: 5.92 us -> 5.43 us  [exchange(): lax.ppermute(block, ('seq', 'dp'), pairing(lax.axis_size('seq'), pairs))]
  transfers between devices with their start and end apart: 10 -> 10, of which waited for: 6 -> 4; matrix products, arithmetic and copies ran while one was open for 0% -> 0% of each run, Pallas kernels for 18% -> 18%
where the time goes in v9:
time: 35.6 us; the launch traced here: 35.4 us
  starting transfers between devices  14.9 us (42%)
  Pallas kernels  9.78 us (27%)
  waiting for transfers between devices  9.4 us (26%)
  between operations  1.34 us (4%)
    ppermute x4, waiting for transfers between devices, turned(): lax.ppermute(block, 'seq', [(i, (i + distance) % size) for i in range(siz...  5.77 us
    ppermute x2, starting transfers between devices, exchange(): lax.ppermute(block, ('seq', 'dp'), pairing(lax.axis_size('seq'), pairs))  5.43 us
    ppermute x4, starting transfers between devices, turned(): lax.ppermute(block, 'seq', [(i, (i + distance) % size) for i in range(siz...  5.2 us
    ppermute x2, waiting for transfers between devices, exchange(): lax.ppermute(block, ('seq', 'dp'), pairing(lax.axis_size('seq'), pairs))  3.58 us
    pallas_call x1, Pallas kernels, on_device(): call(functools.partial(local_body, heads, dim), [(rows, BF16), ((width, m...  2.78 us
    ppermute x2, starting transfers between devices, spread(): far = lax.ppermute(msg, ('seq', 'dp'), turning(size, loops))  2.65 us
    pallas_call x1, Pallas kernels, on_device(): call(functools.partial(backward_body, heads, dim), [(rows, BF16), (rows,...  2.24 us
    ppermute x1, starting transfers between devices, on_device(): got = [lax.ppermute(part, 'head', [(0, 1), (1, 0)]) for part in send]  1.59 us
  transfers between devices with their start and end apart: 10, of which 4 were waited for; matrix products, arithmetic and copies ran while one was open for 0% of the time, Pallas kernels for 18%

profile of v9, /device:TPU:0, one launch (start us, length us, event | category | flops | bytes accessed | tf_op | source)
XLA Modules:
  0.0 35.4 jit_solution(9896626106325820568)
XLA Ops:
  1.3 1.3 %opening_body.1 = (bf16[256,512]{1,0:T(8,128)(2,1)S(1)}, bf16[256,512]{1,0:T(8,128)(2,1)S(1)}, f32[8,128]{1,0:T(8,128)S(1)}, f32[512,128]{1,0:T(8,128)S(1)}, bf16[528,128]{1,0:T(8,128)(2,1)S(1)}) custom-call(s32[1,1]{1,0:T(1,128)S(6)} %copy.12.doc_ref, bf16[256,512]{1,0:T(8,128)(2,1)} %bitcast.9, bf16[256,512]{1,0:T(8,128)(2,1)} %bitcast.10), custom_call_target="tpu_custom_call" | custom-call | flops 33554432 | bytes 1048576 | tf_op jit(solution)/shard_map/opening_body/pallas_call | solution.py:347
  2.6 3.0 %collective-permute-start = (bf16[528,128]{1,0:T(8,128)(2,1)S(1)}, bf16[528,128]{1,0:T(8,128)(2,1)S(1)}, u32[]{:S(2)}, u32[]{:S(2)}) collective-permute-start(bf16[528,128]{1,0:T(8,128)(2,1)S(1)} %get-tuple-element.45.own_ref), channel_id=1, source_target_pairs={{0,4},{1,5},{4,0},{5,1},{8,12},{9,13},{12,8},{13,9},{16,20},{17,21... | collective-permute-start | bytes 405512 | tf_op jit(solution)/shard_map/ppermute | solution.py:55
  5.6 3.6 %collective-permute-done.pair_ref.refs_0_ = bf16[528,128]{1,0:T(8,128)(2,1)S(1)} collective-permute-done((bf16[528,128]{1,0:T(8,128)(2,1)S(1)}, bf16[528,128]{1,0:T(8,128)(2,1)S(1)}, u32[]{:S(2)}, u32[]{:S(2)}) %collective-permute-start) | collective-permute-done | bytes 135200 | tf_op jit(solution)/shard_map/ppermute | solution.py:55
  9.2 0.1 pair_body.2
  9.3 0.0 copy-start
  9.3 1.9 %collective-permute-start.1 = (bf16[528,128]{1,0:T(8,128)(2,1)S(1)}, bf16[528,128]{1,0:T(8,128)(2,1)S(1)}, u32[]{:S(2)}, u32[]{:S(2)}) collective-permute-start(bf16[528,128]{1,0:T(8,128)(2,1)S(1)} %pair_body.2), channel_id=1, source_target_pairs={{0,8},{4,12},{8,16},{12,20},{16,24},{20,28},{24,0},{28,4},{1,9},{5... | collective-permute-start | bytes 405512 | tf_op jit(solution)/shard_map/ppermute | solution.py:76
  11.1 2.8 %local_body.1 = (bf16[256,512]{1,0:T(8,128)(2,1)S(1)}, bf16[512,2048]{1,0:T(8,128)(2,1)S(1)}, bf16[1024,256]{1,0:T(8,128)(2,1)S(1)}, f32[256,512]{1,0:T(8,128)S(1)}, f32[256,512]{1,0:T(8,128)S(1)}) custom-call(bf16[256,512]{1,0:T(8,128)(2,1)} %bitcast.11, bf16[256,512]{1,0:T(8,128)(2,1)S(1)} %get-tuple-element.37.key_ref, ...), custom_call_target="tpu_custom_call" | custom-call | flops 671088640 | bytes 6291456 | tf_op jit(solution)/shard_map/local_body/pallas_call | solution.py:352
  13.9 2.4 %collective-permute-done.1.refs_2_.refs_3_ = bf16[528,128]{1,0:T(8,128)(2,1)S(1)} collective-permute-done((bf16[528,128]{1,0:T(8,128)(2,1)S(1)}, bf16[528,128]{1,0:T(8,128)(2,1)S(1)}, u32[]{:S(2)}, u32[]{:S(2)}) %collective-permute-start.1) | collective-permute-done | bytes 135200 | tf_op jit(solution)/shard_map/ppermute | solution.py:76
  16.3 1.3 %forward_body.1 = (bf16[512,128]{1,0:T(8,128)(2,1)S(1)}, bf16[128,512]{1,0:T(8,128)(2,1)S(1)}, bf16[128,2048]{1,0:T(8,128)(2,1)S(1)}, bf16[256,512]{1,0:T(8,128)...) custom-call(f32[8,128]{1,0:T(8,128)S(1)} %get-tuple-element.41.number_ref, ...), custom_call_target="tpu_custom_call" | custom-call | flops 335544320 | bytes 4194304 | tf_op jit(solution)/shard_map/forward_body/pallas_call | solution.py:361
  17.7 1.6 %collective-permute-start.3 = (bf16[128,2048]{1,0:T(8,128)(2,1)S(1)}, bf16[128,2048]{1,0:T(8,128)(2,1)S(1)}, u32[]{:S(2)}, u32[]{:S(2)}) collective-permute-start(bf16[128,2048]{1,0:T(8,128)(2,1)S(1)} %get-tuple-element.53), channel_id=1, source_target_pairs={{0,2},{2,0},{1,3},{3,1},{4,6},{6,4},{5,7},{7,5},{8,10},{10,8},{9,1... | collective-permute-start | bytes 1572872 | tf_op jit(solution)/shard_map/ppermute | solution.py:369
  19.2 2.4 %collective-permute-start.4 = (bf16[528,128]{1,0:T(8,128)(2,1)S(1)}, bf16[528,128]{1,0:T(8,128)(2,1)S(1)}, u32[]{:S(2)}, u32[]{:S(2)}) collective-permute-start(bf16[528,128]{1,0:T(8,128)(2,1)S(1)} %get-tuple-element.55.own_ref), channel_id=1, source_target_pairs={{0,4},{1,5},{4,0},{5,1},{8,12},{9,13},{12,8},{13,9},{16,20},{17,21... | collective-permute-start | bytes 405512 | tf_op jit(solution)/shard_map/ppermute | solution.py:55
  21.7 2.6 %collective-permute-start.8 = (bf16[528,128]{1,0:T(8,128)(2,1)S(1)}, bf16[528,128]{1,0:T(8,128)(2,1)S(1)}, u32[]{:S(2)}, u32[]{:S(2)}) collective-permute-start(bf16[528,128]{1,0:T(8,128)(2,1)S(1)} %get-tuple-element.55.own_ref), channel_id=1, source_target_pairs={{0,16},{1,17},{4,0},{5,1},{8,24},{9,25},{12,8},{13,9},{16,4},{17,5... | collective-permute-start | bytes 405512 | tf_op jit(solution)/shard_map/ppermute | solution.py:325
  24.3 2.2 %backward_body.1 = (bf16[256,512]{1,0:T(8,128)(2,1)}, f32[256,512]{1,0:T(8,128)S(1)}, f32[256,512]{1,0:T(8,128)S(1)}, f32[128,2048]{1,0:T(8,128)S(1)}) custom-call(bf16[256,512]{1,0:T(8,128)(2,1)S(1)} %get-tuple-element.39.query_ref, bf16[256,512]{1,0:T(8,128)(2,1)S(1)} %get-tuple-element.37.key_ref, bf16[256,512]{1,0:T(8,128)(2,1)S(1)} %get-tuple-element.38.value_ref, ...), custom_call_target="tpu_custom_call" | custom-call | bytes 65536 | tf_op jit(solution)/shard_map/backward_body/pallas_call | solution.py:370
  26.6 0.1 pair_body.3
  26.6 1.2 %collective-permute-start.7 = (bf16[528,128]{1,0:T(8,128)(2,1)S(1)}, bf16[528,128]{1,0:T(8,128)(2,1)S(1)}, u32[]{:S(2)}, u32[]{:S(2)}) collective-permute-start(bf16[528,128]{1,0:T(8,128)(2,1)S(1)} %get-tuple-element.59), channel_id=1, source_target_pairs={{0,24},{4,28},{8,0},{12,4},{16,8},{20,12},{24,16},{28,20},{1,25},{... | collective-permute-start | bytes 405512 | tf_op jit(solution)/shard_map/ppermute | solution.py:76
  27.8 0.9 %collective-permute-start.6 = (f32[4,128]{1,0:T(4,128)S(1)}, f32[4,128]{1,0:T(4,128)S(1)}, u32[]{:S(2)}, u32[]{:S(2)}) collective-permute-start(f32[4,128]{1,0:T(4,128)S(1)} %get-tuple-element.58.own_ref), channel_id=1, source_target_pairs={{0,8},{4,12},{8,16},{12,20},{16,24},{20,28},{24,0},{28,4},{1,9},{5... | collective-permute-start | bytes 6152 | tf_op jit(solution)/shard_map/ppermute | solution.py:76
  28.7 1.2 %collective-permute-start.5 = (f32[4,128]{1,0:T(4,128)S(1)}, f32[4,128]{1,0:T(4,128)S(1)}, u32[]{:S(2)}, u32[]{:S(2)}) collective-permute-start(f32[4,128]{1,0:T(4,128)S(1)} %get-tuple-element.58.own_ref), channel_id=1, source_target_pairs={{0,16},{4,20},{8,24},{12,28},{16,0},{20,4},{24,8},{28,12},{1,17},{... | collective-permute-start | bytes 6152 | tf_op jit(solution)/shard_map/ppermute | solution.py:76
  29.9 3.3 %collective-permute-done.7.near_ref.refs_2_.refs_3_ = bf16[528,128]{1,0:T(8,128)(2,1)S(1)} collective-permute-done((bf16[528,128]{1,0:T(8,128)(2,1)S(1)}, bf16[528,128]{1,0:T(8,128)(2,1)S(1)}, u32[]{:S(2)}, u32[]{:S(2)}) %collective-permute-start.7) | collective-permute-done | bytes 135200 | tf_op jit(solution)/shard_map/ppermute | solution.py:76
  33.3 0.1 collective-permute-done.6.farther_ref
  33.3 0.0 collective-permute-done.5.far_ref
  33.3 0.0 collective-permute-start.9
  33.4 1.1 %last_body.1 = (bf16[256,512]{1,0:T(8,128)(2,1)}, bf16[256,512]{1,0:T(8,128)(2,1)}) custom-call(f32[8,128]{1,0:T(8,128)S(1)} %get-tuple-element.41.number_ref, bf16[256,512]{1,0:T(8,128)(2,1)S(1)} %get-tuple-element.37.key_ref, bf16[256,512]{1,0:T(8,128)(2,1)S(1)} %get-tuple-element.38.value_ref, f32[256,512]{1,0:T(8,128)S(1)} %get-tuple-element.63.key_part_ref, ...), custom_call_target="tpu_custom_call" | custom-call | flops 67108864 | bytes 3145728 | tf_op jit(solution)/shard_map/last_body/pallas_call | solution.py:384
  34.5 0.0 collective-permute-done.9.refs_2_
  34.5 0.9 %layer_body.1 = (bf16[128,2048]{1,0:T(8,128)(2,1)}, f32[4,128]{1,0:T(4,128)}) custom-call(f32[128,2048]{1,0:T(8,128)S(1)} %get-tuple-element.52.own_ref, bf16[128,2048]{1,0:T(8,128)(2,1)S(1)} %collective-permute-done.3.refs_0_, f32[4,128]{1,0:T(4,128)S(1)} %gain_body.1.refs_1_, f32[4,128]{1,0:T(4,128)S(1)} %collective-permute-done.9.refs_2_), custom_call_target="tpu_custom_call" | custom-call | bytes 2097152 | tf_op jit(solution)/shard_map/layer_body/pallas_call | solution.py:388
  (7 shorter events, 0.0 us)
Async XLA Ops:
  2.6 6.6 %collective-permute-start = (bf16[528,128]{1,0:T(8,128)(2,1)S(1)}, bf16[528,128]{1,0:T(8,128)(2,1)S(1)}, u32[]{:S(2)}, u32[]{:S(2)}) collective-permute-start(bf16[528,128]{1,0:T(8,128)(2,1)S(1)} %get-tuple-element.45.own_ref), channel_id=1, source_target_pairs={{0,4},{1,5},{4,0},{5,1},{8,12},{9,13},{12,8},{13,9},{16,20},{17,21... | collective-permute-start | bytes 405512 | tf_op jit(solution)/shard_map/ppermute | solution.py:55
  5.6 8.3 %collective-permute-start.2 = (bf16[528,128]{1,0:T(8,128)(2,1)S(1)}, bf16[528,128]{1,0:T(8,128)(2,1)S(1)}, u32[]{:S(2)}, u32[]{:S(2)}) collective-permute-start(bf16[528,128]{1,0:T(8,128)(2,1)S(1)} %get-tuple-element.45.own_ref), channel_id=1, source_target_pairs={{0,1},{1,0},{4,16},{5,17},{8,9},{9,8},{12,24},{13,25},{16,20},{17,... | collective-permute-start | bytes 405512 | tf_op jit(solution)/shard_map/ppermute | solution.py:325
  9.3 7.1 %copy-start = (f32[4,128]{1,0:T(4,128)S(1)}, f32[4,128]{1,0:T(4,128)}, u32[]{:S(2)}) copy-start(f32[4,128]{1,0:T(4,128)} %gain_ref.1) | copy-start | bytes 6148
  9.3 7.0 %collective-permute-start.1 = (bf16[528,128]{1,0:T(8,128)(2,1)S(1)}, bf16[528,128]{1,0:T(8,128)(2,1)S(1)}, u32[]{:S(2)}, u32[]{:S(2)}) collective-permute-start(bf16[528,128]{1,0:T(8,128)(2,1)S(1)} %pair_body.2), channel_id=1, source_target_pairs={{0,8},{4,12},{8,16},{12,20},{16,24},{20,28},{24,0},{28,4},{1,9},{5... | collective-permute-start | bytes 405512 | tf_op jit(solution)/shard_map/ppermute | solution.py:76
  17.7 16.9 %collective-permute-start.3 = (bf16[128,2048]{1,0:T(8,128)(2,1)S(1)}, bf16[128,2048]{1,0:T(8,128)(2,1)S(1)}, u32[]{:S(2)}, u32[]{:S(2)}) collective-permute-start(bf16[128,2048]{1,0:T(8,128)(2,1)S(1)} %get-tuple-element.53), channel_id=1, source_target_pairs={{0,2},{2,0},{1,3},{3,1},{4,6},{6,4},{5,7},{7,5},{8,10},{10,8},{9,1... | collective-permute-start | bytes 1572872 | tf_op jit(solution)/shard_map/ppermute | solution.py:369
  19.2 7.3 %collective-permute-start.4 = (bf16[528,128]{1,0:T(8,128)(2,1)S(1)}, bf16[528,128]{1,0:T(8,128)(2,1)S(1)}, u32[]{:S(2)}, u32[]{:S(2)}) collective-permute-start(bf16[528,128]{1,0:T(8,128)(2,1)S(1)} %get-tuple-element.55.own_ref), channel_id=1, source_target_pairs={{0,4},{1,5},{4,0},{5,1},{8,12},{9,13},{12,8},{13,9},{16,20},{17,21... | collective-permute-start | bytes 405512 | tf_op jit(solution)/shard_map/ppermute | solution.py:55
  21.7 8.3 %collective-permute-start.8 = (bf16[528,128]{1,0:T(8,128)(2,1)S(1)}, bf16[528,128]{1,0:T(8,128)(2,1)S(1)}, u32[]{:S(2)}, u32[]{:S(2)}) collective-permute-start(bf16[528,128]{1,0:T(8,128)(2,1)S(1)} %get-tuple-element.55.own_ref), channel_id=1, source_target_pairs={{0,16},{1,17},{4,0},{5,1},{8,24},{9,25},{12,8},{13,9},{16,4},{17,5... | collective-permute-start | bytes 405512 | tf_op jit(solution)/shard_map/ppermute | solution.py:325
  26.6 6.6 %collective-permute-start.7 = (bf16[528,128]{1,0:T(8,128)(2,1)S(1)}, bf16[528,128]{1,0:T(8,128)(2,1)S(1)}, u32[]{:S(2)}, u32[]{:S(2)}) collective-permute-start(bf16[528,128]{1,0:T(8,128)(2,1)S(1)} %get-tuple-element.59), channel_id=1, source_target_pairs={{0,24},{4,28},{8,0},{12,4},{16,8},{20,12},{24,16},{28,20},{1,25},{... | collective-permute-start | bytes 405512 | tf_op jit(solution)/shard_map/ppermute | solution.py:76
  27.8 5.5 %collective-permute-start.6 = (f32[4,128]{1,0:T(4,128)S(1)}, f32[4,128]{1,0:T(4,128)S(1)}, u32[]{:S(2)}, u32[]{:S(2)}) collective-permute-start(f32[4,128]{1,0:T(4,128)S(1)} %get-tuple-element.58.own_ref), channel_id=1, source_target_pairs={{0,8},{4,12},{8,16},{12,20},{16,24},{20,28},{24,0},{28,4},{1,9},{5... | collective-permute-start | bytes 6152 | tf_op jit(solution)/shard_map/ppermute | solution.py:76
  28.7 4.6 %collective-permute-start.5 = (f32[4,128]{1,0:T(4,128)S(1)}, f32[4,128]{1,0:T(4,128)S(1)}, u32[]{:S(2)}, u32[]{:S(2)}) collective-permute-start(f32[4,128]{1,0:T(4,128)S(1)} %get-tuple-element.58.own_ref), channel_id=1, source_target_pairs={{0,16},{4,20},{8,24},{12,28},{16,0},{20,4},{24,8},{28,12},{1,17},{... | collective-permute-start | bytes 6152 | tf_op jit(solution)/shard_map/ppermute | solution.py:76
  33.3 1.2 %collective-permute-start.9 = (f32[4,128]{1,0:T(4,128)S(1)}, f32[4,128]{1,0:T(4,128)S(1)}, u32[]{:S(2)}, u32[]{:S(2)}) collective-permute-start(f32[4,128]{1,0:T(4,128)S(1)} %gain_body.1.refs_1_), channel_id=1, source_target_pairs={{0,1},{1,0},{4,5},{5,4},{8,9},{9,8},{12,13},{13,12},{16,17},{17,16... | collective-permute-start | bytes 6152 | tf_op jit(solution)/shard_map/ppermute | solution.py:85
